TPU v7x, 128 devices: a whole 4x4x4 slice. The times are simulated.
128 devices in a mesh: lat: 8 (over x, core), lon: 16 (over z, y).
Axes of the slice: x: 4, y: 4, z: 4, core: 2. Of those that a mesh axis runs over, the one named last changes fastest.
Arguments:
- prognostic_samples: float32 [40, 25, 64, 2048], P(None, None, 'lat', 'lon'), may hold values from -6 to 6
- wind: float32 [2, 64, 2048], P(None, 'lat', 'lon'), may hold values from -0.4 to 0.4
- obs_lat: int32 [2, 512], replicated, may hold values from 0 to 63
- obs_lon: int32 [2, 512], replicated, may hold values from 0 to 2047
- obs_var: int32 [2, 512], replicated, may hold values from 0 to 24
- obs_value: float32 [2, 512], replicated, may hold values from -6 to 6
- obs_error: float32 [2, 512], replicated, may hold values from 0.5 to 4
Outputs:
- analysis: float32 [40, 25, 64, 2048], P(None, None, 'lat', 'lon')
All inputs are finite; a program needn't handle non-finite values.
Results may differ from a plain program's by a relative error of at most 0.0001.
Values sent between devices are 32-bit elements; how exact they have to be, the bound alone decides.
A program may use at most 128 MiB of HBM per device.

v0:
```python
import jax
import jax.numpy as jnp
from jax import lax
from jax.sharding import PartitionSpec as P

STEPS = 2
BLOCK = 128


HIGHEST = lax.Precision.HIGHEST
DIFFUSE = 0.1


def with_halo(block, sides, width):
    for axis, dim in sides:
        count = lax.axis_size(axis)
        forward = [(i, i + 1) for i in range(count - 1)]
        forward.append((count - 1, 0))
        backward = [(target, source) for source, target in forward]
        low = lax.ppermute(
            lax.slice_in_dim(block, block.shape[dim] - width, None, axis=dim), axis, forward
        )
        high = lax.ppermute(lax.slice_in_dim(block, 0, width, axis=dim), axis, backward)
        block = jnp.concatenate([low, block, high], axis=dim)
    return block


def taper(scaled):
    inner_part = (
        ((-0.25 * scaled + 0.5) * scaled + 0.625) * scaled - 5.0 / 3.0
    ) * scaled * scaled + 1.0
    scaled_safe = jnp.maximum(scaled, 1.0)
    outer_part = (
        ((((scaled / 12.0 - 0.5) * scaled + 0.625) * scaled + 5.0 / 3.0) * scaled - 5.0) * scaled
        + 4.0
        - 2.0 / (3.0 * scaled_safe)
    )
    return jnp.where(scaled <= 1.0, inner_part, jnp.where(scaled < 2.0, outer_part, 0.0))


def taper_to(lat_a, lon_a, lat_b, lon_b, cycle_length, reach):
    meridional_spacing = (lat_a - lat_b).astype(jnp.float32)
    lon_gap = jnp.abs(lon_a - lon_b)
    lon_gap = jnp.minimum(lon_gap, cycle_length - lon_gap).astype(jnp.float32)
    return taper(jnp.sqrt(meridional_spacing * meridional_spacing + lon_gap * lon_gap) / reach)


def advance(padded, east_wind, north_wind):
    centre = padded[..., 1:-1, 1:-1]
    above_v = padded[..., 2:, 1:-1]
    below_v = padded[..., :-2, 1:-1]
    right_v = padded[..., 1:-1, 2:]
    left_v = padded[..., 1:-1, :-2]
    return (
        centre
        - 0.5 * east_wind * (right_v - left_v)
        - 0.5 * north_wind * (above_v - below_v)
        + DIFFUSE * (right_v + left_v + above_v + below_v - 4.0 * centre)
    )


def zero_outside_block(padded, margin):
    overall_line_count = padded.shape[-2]
    band_rows = overall_line_count - 2 * margin
    global_row = (
        lax.axis_index("lat") * band_rows - margin + lax.iota(jnp.int32, overall_line_count)
    )
    inside = (global_row >= 0) & (global_row < band_rows * lax.axis_size("lat"))
    return jnp.where(inside[:, None], padded, 0.0)


def gains(prior, values, errors):
    members = prior.shape[0]
    average = jnp.mean(prior, axis=0)
    anomaly = prior - average
    ensemble_spread = jnp.sum(anomaly * anomaly, axis=0) / (members - 1)
    total = ensemble_spread + errors
    weights = anomaly / ((members - 1) * total)
    shifts = values - average - anomaly / (1.0 + jnp.sqrt(errors / total))
    return (weights, shifts)


def read_priors(sample_realizations, sel_lat, sel_lon, sel_var, band_rows, band_cols):
    members, variables, cells = sample_realizations.shape
    local_lat = sel_lat - lax.axis_index("lat") * band_rows
    local_lon = sel_lon - lax.axis_index("lon") * band_cols
    owned = (local_lat >= 0) & (local_lat < band_rows) & (local_lon >= 0) & (local_lon < band_cols)
    position = (
        sel_var * cells
        + jnp.clip(local_lat, 0, band_rows - 1) * band_cols
        + jnp.clip(local_lon, 0, band_cols - 1)
    )
    picked = jnp.take(sample_realizations.reshape(members, variables * cells), position, axis=1)
    return jnp.where(owned[None, :], picked, 0.0)


def apply_block(sample_realizations, weights, shifts, damping_factors):
    projected = jnp.einsum("mvc,mk->vck", sample_realizations, weights, precision=HIGHEST)
    return sample_realizations + jnp.einsum(
        "vck,mk->mvc", projected * damping_factors, shifts, precision=HIGHEST
    )


def body(prognostic_samples, wind, obs_lat, obs_lon, obs_var, obs_value, obs_error):
    members, variables, band_rows, band_cols = prognostic_samples.shape
    state_now = prognostic_samples
    for section in range(STEPS):
        padded = with_halo(state_now, (("lat", 2), ("lon", 3)), 1)
        state_now = advance(zero_outside_block(padded, 1), wind[0], wind[1])
    sample_realizations = state_now.reshape(members, variables, band_rows * band_cols)
    cycle_length = band_cols * lax.axis_size("lon")
    reach = float(band_rows * lax.axis_size("lat") // 2)
    cell_ids = lax.iota(jnp.int32, band_rows * band_cols)
    cell_lat = (lax.axis_index("lat") * band_rows + cell_ids // band_cols)[:, None]
    cell_lon = (lax.axis_index("lon") * band_cols + cell_ids % band_cols)[:, None]
    block_count = obs_lat.shape[1] // BLOCK
    for batch_no in range(obs_lat.shape[0]):
        sel_lat = obs_lat[batch_no]
        sel_lon = obs_lon[batch_no]
        sel_var = obs_var[batch_no]
        values = obs_value[batch_no]
        errors = obs_error[batch_no]

        def block_slice(array, first_obs):
            return lax.dynamic_slice_in_dim(array, first_obs, BLOCK)

        def single_block(block_no, members_now):
            first_obs = block_no * BLOCK
            blk_lat = block_slice(sel_lat, first_obs)
            block_longitude = block_slice(sel_lon, first_obs)
            own_part = read_priors(
                members_now,
                blk_lat,
                block_longitude,
                block_slice(sel_var, first_obs),
                band_rows,
                band_cols,
            )
            prior = lax.psum(own_part, ("lat", "lon"))
            weights, shifts = gains(
                prior, block_slice(values, first_obs), block_slice(errors, first_obs)
            )
            damping_factors = taper_to(
                cell_lat, cell_lon, blk_lat[None, :], block_longitude[None, :], cycle_length, reach
            )
            return apply_block(members_now, weights, shifts, damping_factors)

        sample_realizations = lax.fori_loop(0, block_count, single_block, sample_realizations)
    return sample_realizations.reshape(members, variables, band_rows, band_cols)


def solution(mesh):
    in_specs = (P(None, None, "lat", "lon"), P(None, "lat", "lon"), P(), P(), P(), P(), P())
    out_specs = P(None, None, "lat", "lon")
    return jax.shard_map(body, mesh=mesh, in_specs=in_specs, out_specs=out_specs, check_vma=False)
```

profile of v0, /device:TPU:1, one launch (start us, length us, event | category | flops | bytes accessed | tf_op | source)
XLA Modules:
  0.0 1001.3 jit_solution(13554984503513488470)
XLA Ops:
  7.6 9.6 copy.111
  21.9 8.5 pad_maximum_fusion
  30.4 7.0 copy-done
  44.0 15.4 %copy.114 = f32[40,25,10,128]{3,0,2,1:T(8,128)} copy(f32[40,25,10,128]{0,1,3,2:T(8,128)} %copy-done) | data formatting | bytes 10240000 | tf_op jit(solution)/shard_map/concatenate | solution.py:24
  66.1 13.4 %maximum_select_fusion = f32[40,25,10,130]{3,0,2,1:T(8,128)} fusion(f32[40,25,10,1]{3,0,2,1:T(8,128)} %copy.115, f32[40,25,10,128]{3,0,2,1:T(8,128)} %copy.114, f32[40,25,10,1]{3,0,2,1:T(8,128)} %copy.113, pred[10]{0:T(512)(128)(4,1)S(1)} %compare_and_fusion.4), kind=kLoop, calls=%fused_computation.101 | loop fusion | flops 3900000 | bytes 10400010 | tf_op jit(solution)/shard_map/jit(_where)/select_n | solution.py:69
  79.4 14.2 %multiply_add_fusion.2 = f32[40,25,8,128]{3,0,2,1:T(8,128)S(1)} fusion(f32[40,25,10,130]{3,0,2,1:T(8,128)} %maximum_select_fusion, f32[8,128]{1,0:T(8,128)S(1)} %get-tuple-element.578, f32[8,128]{1,0:T(8,128)S(1)} %get-tuple-element.577), kind=kLoop, calls=%fused_computation.106 | loop fusion | flops 13312000 | bytes 24584192 | tf_op jit(solution)/shard_map/add | solution.py:55
  96.0 5.8 collective-permute-done.4
  105.0 5.5 fusion.59
  118.7 17.7 %collective-permute-start.7 = (f32[40,25,10,1]{0,1,3,2:T(8,128)S(1)}, f32[40,25,10,1]{0,1,3,2:T(8,128)S(1)}, u32[]{:S(2)}, u32[]{:S(2)}) collective-permute-start(f32[40,25,10,1]{0,1,3,2:T(8,128)S(1)} %copy.127), channel_id=1, source_target_pairs={{1,0},{2,1},{3,2},{4,3},{5,4},{6,5},{7,6},{8,7},{9,8},{10,9},{11,1... | collective-permute-start | bytes 120008 | tf_op jit(solution)/shard_map/ppermute | solution.py:23
  143.1 9.6 maximum_select_fusion.1
  152.7 5.7 copy_bitcast_fusion
  158.4 419.8 %while.32 = (s32[]{:T(128)}, f32[40,25,1024]{2,0,1:T(8,128)}, f32[512]{0:T(512)S(1)}, s32[512]{0:T(512)S(1)}, s32[512]{0:T(512)S(1)}, /*index=5*/s32[512]{0:T(51...) while((s32[]{:T(128)}, f32[40,25,1024]{2,0,1:T(8,128)}, ...), condition=%wide.region_4.6_spmd.clone, body=%wide.region_0.5_spmd.clone.sunk | while | flops 3155089920 | bytes 48024392 | solution.py:148
  158.6 9.1 copy.135
  167.7 5.4 gather_fusion
  173.2 67.1 %psum.32 = f32[40,128]{1,0:T(8,128)S(1)} all-reduce(f32[40,128]{1,0:T(8,128)S(1)} %bitcast_select_fusion.4), channel_id=1, replica_groups=mesh['lat'=8,'lon'=16] {'lat','lon'}, use_global_device_ids=true, to_apply=%region_1.2 | all-reduce | flops 5120 | bytes 40960 | tf_op jit(solution)/shard_map/while/body/eval_jaxpr/psum | solution.py:139
  240.5 14.2 %fusion.86 = f32[128,25,1024]{2,0,1:T(8,128)S(1)} fusion(f32[40,25,1024]{2,0,1:T(8,128)} %get-tuple-element.762, f32[40,128]{1,0:T(8,128)S(1)} %psum.32, f32[128]{0:T(128)S(1)} %get-tuple-element.718, f32[128]{0:T(128)S(1)} %get-tuple-element.717), kind=kOutput, calls=%fused_computation.22.clone.1 | convolution fusion | flops 1572874240 | bytes 17224704 | tf_op jit(solution)/shard_map/while/body/eval_jaxpr/mvc,mk->vck/dot_general | solution.py:98
  255.7 10.6 %fusion.89 = f32[40,25,1024]{2,0,1:T(8,128)} fusion(f32[40,25,1024]{2,0,1:T(8,128)} %get-tuple-element.762, f32[128,25,1024]{2,0,1:T(8,128)S(1)} %fusion.86, f32[1024,128]{0,1:T(8,128)S(1)} %fusion.88, f32[40,128]{1,0:T(8,128)S(1)} %psum.32, f32[128]{0:T(128)S(1)} %get-tuple-element.721, f32[128]{0:T(128)S(1)} %get-tuple-element.717, ...), kind=kOutput, calls=%fused_computation.9.clone.1 | convolution fusion | flops 1577180160 | bytes 21845504 | tf_op jit(solution)/shard_map/while/body/eval_jaxpr/vck,mk->mvc/dot_general | solution.py:99
  266.5 9.1 copy.135
  281.1 63.1 %psum.32 = f32[40,128]{1,0:T(8,128)S(1)} all-reduce(f32[40,128]{1,0:T(8,128)S(1)} %bitcast_select_fusion.4), channel_id=1, replica_groups=mesh['lat'=8,'lon'=16] {'lat','lon'}, use_global_device_ids=true, to_apply=%region_1.2 | all-reduce | flops 5120 | bytes 40960 | tf_op jit(solution)/shard_map/while/body/eval_jaxpr/psum | solution.py:139
  344.4 14.2 %fusion.86 = f32[128,25,1024]{2,0,1:T(8,128)S(1)} fusion(f32[40,25,1024]{2,0,1:T(8,128)} %get-tuple-element.762, f32[40,128]{1,0:T(8,128)S(1)} %psum.32, f32[128]{0:T(128)S(1)} %get-tuple-element.718, f32[128]{0:T(128)S(1)} %get-tuple-element.717), kind=kOutput, calls=%fused_computation.22.clone.1 | convolution fusion | flops 1572874240 | bytes 17224704 | tf_op jit(solution)/shard_map/while/body/eval_jaxpr/mvc,mk->vck/dot_general | solution.py:98
  359.5 10.6 %fusion.89 = f32[40,25,1024]{2,0,1:T(8,128)} fusion(f32[40,25,1024]{2,0,1:T(8,128)} %get-tuple-element.762, f32[128,25,1024]{2,0,1:T(8,128)S(1)} %fusion.86, f32[1024,128]{0,1:T(8,128)S(1)} %fusion.88, f32[40,128]{1,0:T(8,128)S(1)} %psum.32, f32[128]{0:T(128)S(1)} %get-tuple-element.721, f32[128]{0:T(128)S(1)} %get-tuple-element.717, ...), kind=kOutput, calls=%fused_computation.9.clone.1 | convolution fusion | flops 1577180160 | bytes 21845504 | tf_op jit(solution)/shard_map/while/body/eval_jaxpr/vck,mk->mvc/dot_general | solution.py:99
  370.3 9.1 copy.135
  379.4 5.4 gather_fusion
  384.9 63.9 %psum.32 = f32[40,128]{1,0:T(8,128)S(1)} all-reduce(f32[40,128]{1,0:T(8,128)S(1)} %bitcast_select_fusion.4), channel_id=1, replica_groups=mesh['lat'=8,'lon'=16] {'lat','lon'}, use_global_device_ids=true, to_apply=%region_1.2 | all-reduce | flops 5120 | bytes 40960 | tf_op jit(solution)/shard_map/while/body/eval_jaxpr/psum | solution.py:139
  449.0 14.2 %fusion.86 = f32[128,25,1024]{2,0,1:T(8,128)S(1)} fusion(f32[40,25,1024]{2,0,1:T(8,128)} %get-tuple-element.762, f32[40,128]{1,0:T(8,128)S(1)} %psum.32, f32[128]{0:T(128)S(1)} %get-tuple-element.718, f32[128]{0:T(128)S(1)} %get-tuple-element.717), kind=kOutput, calls=%fused_computation.22.clone.1 | convolution fusion | flops 1572874240 | bytes 17224704 | tf_op jit(solution)/shard_map/while/body/eval_jaxpr/mvc,mk->vck/dot_general | solution.py:98
  464.1 10.6 %fusion.89 = f32[40,25,1024]{2,0,1:T(8,128)} fusion(f32[40,25,1024]{2,0,1:T(8,128)} %get-tuple-element.762, f32[128,25,1024]{2,0,1:T(8,128)S(1)} %fusion.86, f32[1024,128]{0,1:T(8,128)S(1)} %fusion.88, f32[40,128]{1,0:T(8,128)S(1)} %psum.32, f32[128]{0:T(128)S(1)} %get-tuple-element.721, f32[128]{0:T(128)S(1)} %get-tuple-element.717, ...), kind=kOutput, calls=%fused_computation.9.clone.1 | convolution fusion | flops 1577180160 | bytes 21845504 | tf_op jit(solution)/shard_map/while/body/eval_jaxpr/vck,mk->mvc/dot_general | solution.py:99
  474.9 9.1 copy.135
  489.5 62.8 %psum.32 = f32[40,128]{1,0:T(8,128)S(1)} all-reduce(f32[40,128]{1,0:T(8,128)S(1)} %bitcast_select_fusion.4), channel_id=1, replica_groups=mesh['lat'=8,'lon'=16] {'lat','lon'}, use_global_device_ids=true, to_apply=%region_1.2 | all-reduce | flops 5120 | bytes 40960 | tf_op jit(solution)/shard_map/while/body/eval_jaxpr/psum | solution.py:139
  552.5 14.2 %fusion.86 = f32[128,25,1024]{2,0,1:T(8,128)S(1)} fusion(f32[40,25,1024]{2,0,1:T(8,128)} %get-tuple-element.762, f32[40,128]{1,0:T(8,128)S(1)} %psum.32, f32[128]{0:T(128)S(1)} %get-tuple-element.718, f32[128]{0:T(128)S(1)} %get-tuple-element.717), kind=kOutput, calls=%fused_computation.22.clone.1 | convolution fusion | flops 1572874240 | bytes 17224704 | tf_op jit(solution)/shard_map/while/body/eval_jaxpr/mvc,mk->vck/dot_general | solution.py:98
  567.6 10.6 %fusion.89 = f32[40,25,1024]{2,0,1:T(8,128)} fusion(f32[40,25,1024]{2,0,1:T(8,128)} %get-tuple-element.762, f32[128,25,1024]{2,0,1:T(8,128)S(1)} %fusion.86, f32[1024,128]{0,1:T(8,128)S(1)} %fusion.88, f32[40,128]{1,0:T(8,128)S(1)} %psum.32, f32[128]{0:T(128)S(1)} %get-tuple-element.721, f32[128]{0:T(128)S(1)} %get-tuple-element.717, ...), kind=kOutput, calls=%fused_computation.9.clone.1 | convolution fusion | flops 1577180160 | bytes 21845504 | tf_op jit(solution)/shard_map/while/body/eval_jaxpr/vck,mk->mvc/dot_general | solution.py:99
  578.3 417.2 %while.33 = (s32[]{:T(128)}, f32[40,25,1024]{2,0,1:T(8,128)}, f32[512]{0:T(512)S(1)}, s32[512]{0:T(512)S(1)}, s32[512]{0:T(512)S(1)}, /*index=5*/s32[512]{0:T(51...) while((s32[]{:T(128)}, f32[40,25,1024]{2,0,1:T(8,128)}, ...), condition=%wide.region_9.11_spmd.clone, body=%wide.region_5.10_spmd.clone.sunk | while | flops 3155089920 | bytes 48024392 | solution.py:148
  578.6 9.1 copy.137
  593.2 64.2 %psum.33 = f32[40,128]{1,0:T(8,128)S(1)} all-reduce(f32[40,128]{1,0:T(8,128)S(1)} %bitcast_select_fusion.5), channel_id=1, replica_groups=mesh['lat'=8,'lon'=16] {'lat','lon'}, use_global_device_ids=true, to_apply=%region_6.7 | all-reduce | flops 5120 | bytes 40960 | tf_op jit(solution)/shard_map/while/body/eval_jaxpr/psum | solution.py:139
  657.6 14.2 %fusion.93 = f32[128,25,1024]{2,0,1:T(8,128)S(1)} fusion(f32[40,25,1024]{2,0,1:T(8,128)} %get-tuple-element.816, f32[40,128]{1,0:T(8,128)S(1)} %psum.33, f32[128]{0:T(128)S(1)} %get-tuple-element.738, f32[128]{0:T(128)S(1)} %get-tuple-element.737), kind=kOutput, calls=%fused_computation.69.clone.1 | convolution fusion | flops 1572874240 | bytes 17224704 | tf_op jit(solution)/shard_map/while/body/eval_jaxpr/mvc,mk->vck/dot_general | solution.py:98
  672.8 10.6 %fusion.96 = f32[40,25,1024]{2,0,1:T(8,128)} fusion(f32[40,25,1024]{2,0,1:T(8,128)} %get-tuple-element.816, f32[128,25,1024]{2,0,1:T(8,128)S(1)} %fusion.93, f32[1024,128]{0,1:T(8,128)S(1)} %fusion.95, f32[40,128]{1,0:T(8,128)S(1)} %psum.33, f32[128]{0:T(128)S(1)} %get-tuple-element.741, f32[128]{0:T(128)S(1)} %get-tuple-element.737, ...), kind=kOutput, calls=%fused_computation.56.clone.1 | convolution fusion | flops 1577180160 | bytes 21845504 | tf_op jit(solution)/shard_map/while/body/eval_jaxpr/vck,mk->mvc/dot_general | solution.py:99
  683.5 9.1 copy.137
  698.1 62.7 %psum.33 = f32[40,128]{1,0:T(8,128)S(1)} all-reduce(f32[40,128]{1,0:T(8,128)S(1)} %bitcast_select_fusion.5), channel_id=1, replica_groups=mesh['lat'=8,'lon'=16] {'lat','lon'}, use_global_device_ids=true, to_apply=%region_6.7 | all-reduce | flops 5120 | bytes 40960 | tf_op jit(solution)/shard_map/while/body/eval_jaxpr/psum | solution.py:139
  761.0 14.2 %fusion.93 = f32[128,25,1024]{2,0,1:T(8,128)S(1)} fusion(f32[40,25,1024]{2,0,1:T(8,128)} %get-tuple-element.816, f32[40,128]{1,0:T(8,128)S(1)} %psum.33, f32[128]{0:T(128)S(1)} %get-tuple-element.738, f32[128]{0:T(128)S(1)} %get-tuple-element.737), kind=kOutput, calls=%fused_computation.69.clone.1 | convolution fusion | flops 1572874240 | bytes 17224704 | tf_op jit(solution)/shard_map/while/body/eval_jaxpr/mvc,mk->vck/dot_general | solution.py:98
  776.2 10.6 %fusion.96 = f32[40,25,1024]{2,0,1:T(8,128)} fusion(f32[40,25,1024]{2,0,1:T(8,128)} %get-tuple-element.816, f32[128,25,1024]{2,0,1:T(8,128)S(1)} %fusion.93, f32[1024,128]{0,1:T(8,128)S(1)} %fusion.95, f32[40,128]{1,0:T(8,128)S(1)} %psum.33, f32[128]{0:T(128)S(1)} %get-tuple-element.741, f32[128]{0:T(128)S(1)} %get-tuple-element.737, ...), kind=kOutput, calls=%fused_computation.56.clone.1 | convolution fusion | flops 1577180160 | bytes 21845504 | tf_op jit(solution)/shard_map/while/body/eval_jaxpr/vck,mk->mvc/dot_general | solution.py:99
  787.0 9.1 copy.137
  796.1 5.4 gather_fusion.1
  801.6 64.4 %psum.33 = f32[40,128]{1,0:T(8,128)S(1)} all-reduce(f32[40,128]{1,0:T(8,128)S(1)} %bitcast_select_fusion.5), channel_id=1, replica_groups=mesh['lat'=8,'lon'=16] {'lat','lon'}, use_global_device_ids=true, to_apply=%region_6.7 | all-reduce | flops 5120 | bytes 40960 | tf_op jit(solution)/shard_map/while/body/eval_jaxpr/psum | solution.py:139
  866.1 14.2 %fusion.93 = f32[128,25,1024]{2,0,1:T(8,128)S(1)} fusion(f32[40,25,1024]{2,0,1:T(8,128)} %get-tuple-element.816, f32[40,128]{1,0:T(8,128)S(1)} %psum.33, f32[128]{0:T(128)S(1)} %get-tuple-element.738, f32[128]{0:T(128)S(1)} %get-tuple-element.737), kind=kOutput, calls=%fused_computation.69.clone.1 | convolution fusion | flops 1572874240 | bytes 17224704 | tf_op jit(solution)/shard_map/while/body/eval_jaxpr/mvc,mk->vck/dot_general | solution.py:98
  881.3 10.6 %fusion.96 = f32[40,25,1024]{2,0,1:T(8,128)} fusion(f32[40,25,1024]{2,0,1:T(8,128)} %get-tuple-element.816, f32[128,25,1024]{2,0,1:T(8,128)S(1)} %fusion.93, f32[1024,128]{0,1:T(8,128)S(1)} %fusion.95, f32[40,128]{1,0:T(8,128)S(1)} %psum.33, f32[128]{0:T(128)S(1)} %get-tuple-element.741, f32[128]{0:T(128)S(1)} %get-tuple-element.737, ...), kind=kOutput, calls=%fused_computation.56.clone.1 | convolution fusion | flops 1577180160 | bytes 21845504 | tf_op jit(solution)/shard_map/while/body/eval_jaxpr/vck,mk->mvc/dot_general | solution.py:99
  892.1 9.1 copy.137
  906.7 62.8 %psum.33 = f32[40,128]{1,0:T(8,128)S(1)} all-reduce(f32[40,128]{1,0:T(8,128)S(1)} %bitcast_select_fusion.5), channel_id=1, replica_groups=mesh['lat'=8,'lon'=16] {'lat','lon'}, use_global_device_ids=true, to_apply=%region_6.7 | all-reduce | flops 5120 | bytes 40960 | tf_op jit(solution)/shard_map/while/body/eval_jaxpr/psum | solution.py:139
  969.7 14.2 %fusion.93 = f32[128,25,1024]{2,0,1:T(8,128)S(1)} fusion(f32[40,25,1024]{2,0,1:T(8,128)} %get-tuple-element.816, f32[40,128]{1,0:T(8,128)S(1)} %psum.33, f32[128]{0:T(128)S(1)} %get-tuple-element.738, f32[128]{0:T(128)S(1)} %get-tuple-element.737), kind=kOutput, calls=%fused_computation.69.clone.1 | convolution fusion | flops 1572874240 | bytes 17224704 | tf_op jit(solution)/shard_map/while/body/eval_jaxpr/mvc,mk->vck/dot_general | solution.py:98
  984.9 10.6 %fusion.96 = f32[40,25,1024]{2,0,1:T(8,128)} fusion(f32[40,25,1024]{2,0,1:T(8,128)} %get-tuple-element.816, f32[128,25,1024]{2,0,1:T(8,128)S(1)} %fusion.93, f32[1024,128]{0,1:T(8,128)S(1)} %fusion.95, f32[40,128]{1,0:T(8,128)S(1)} %psum.33, f32[128]{0:T(128)S(1)} %get-tuple-element.741, f32[128]{0:T(128)S(1)} %get-tuple-element.737, ...), kind=kOutput, calls=%fused_computation.56.clone.1 | convolution fusion | flops 1577180160 | bytes 21845504 | tf_op jit(solution)/shard_map/while/body/eval_jaxpr/vck,mk->mvc/dot_general | solution.py:99
  (145 shorter events, 89.1 us)
Async XLA Ops:
  4.2 13.1 %collective-permute-start = (f32[40,25,1,128]{3,0,2,1:T(8,128)S(1)}, f32[40,25,1,128]{3,0,2,1:T(8,128)S(1)}, u32[]{:S(2)}, u32[]{:S(2)}) collective-permute-start(f32[40,25,1,128]{3,0,2,1:T(8,128)S(1)} %copy.124), channel_id=1, source_target_pairs={{0,16},{16,32},{32,48},{48,64},{64,80},{80,96},{96,112},{112,0},{1... | collective-permute-start | bytes 1536008 | tf_op jit(solution)/shard_map/ppermute | solution.py:20
  7.6 9.6 copy-start.3
  7.6 9.6 copy-start.2
  7.6 11.5 %collective-permute-start.1 = (f32[40,25,1,128]{3,0,2,1:T(8,128)}, f32[40,25,1,128]{3,0,2,1:T(8,128)S(1)}, u32[]{:S(2)}, u32[]{:S(2)}) collective-permute-start(f32[40,25,1,128]{3,0,2,1:T(8,128)} %copy.125), channel_id=1, source_target_pairs={{16,0},{32,16},{48,32},{64,48},{80,64},{96,80},{112,96},{0,112},{1... | collective-permute-start | bytes 1536008 | tf_op jit(solution)/shard_map/ppermute | solution.py:23
  30.4 7.0 copy-start
  37.4 22.0 %collective-permute-start.2 = (f32[40,25,10,1]{0,1,3,2:T(8,128)S(1)}, f32[40,25,10,1]{0,1,3,2:T(8,128)S(1)}, u32[]{:S(2)}, u32[]{:S(2)}) collective-permute-start(f32[40,25,10,1]{0,1,3,2:T(8,128)S(1)} %get-tuple-element.569), channel_id=1, source_target_pairs={{0,1},{1,2},{2,3},{3,4},{4,5},{5,6},{6,7},{7,8},{8,9},{9,10},{10,1... | collective-permute-start | bytes 120008 | tf_op jit(solution)/shard_map/ppermute | solution.py:20
  38.7 24.0 %collective-permute-start.3 = (f32[40,25,10,1]{0,1,3,2:T(8,128)S(1)}, f32[40,25,10,1]{0,1,3,2:T(8,128)S(1)}, u32[]{:S(2)}, u32[]{:S(2)}) collective-permute-start(f32[40,25,10,1]{0,1,3,2:T(8,128)S(1)} %get-tuple-element.570), channel_id=1, source_target_pairs={{1,0},{2,1},{3,2},{4,3},{5,4},{6,5},{7,6},{8,7},{9,8},{10,9},{11,1... | collective-permute-start | bytes 120008 | tf_op jit(solution)/shard_map/ppermute | solution.py:23
  79.4 16.5 %copy-start.4 = (s32[2,512]{1,0:T(2,128)S(1)}, s32[2,512]{1,0:T(2,128)}, u32[]{:S(2)}) copy-start(s32[2,512]{1,0:T(2,128)} %param.15) | copy-start | bytes 12292
  79.4 16.5 %copy-start.5 = (s32[2,512]{1,0:T(2,128)S(1)}, s32[2,512]{1,0:T(2,128)}, u32[]{:S(2)}) copy-start(s32[2,512]{1,0:T(2,128)} %param.16) | copy-start | bytes 12292
  79.4 16.5 %copy-start.6 = (s32[2,512]{1,0:T(2,128)S(1)}, s32[2,512]{1,0:T(2,128)}, u32[]{:S(2)}) copy-start(s32[2,512]{1,0:T(2,128)} %param.17) | copy-start | bytes 12292
  93.7 11.3 %copy-start.1 = (f32[40,25,8,128]{3,0,2,1:T(8,128)}, f32[40,25,8,128]{3,0,2,1:T(8,128)S(1)}, u32[]{:S(2)}) copy-start(f32[40,25,8,128]{3,0,2,1:T(8,128)S(1)} %multiply_add_fusion.2) | copy-start | bytes 12288004
  93.8 8.0 collective-permute-start.4
  95.8 8.8 collective-permute-start.5
  110.5 25.9 %copy-start.7 = (f32[2,512]{1,0:T(2,128)S(1)}, f32[2,512]{1,0:T(2,128)}, u32[]{:S(2)}) copy-start(f32[2,512]{1,0:T(2,128)} %param.19) | copy-start | bytes 12292
  114.6 21.8 %collective-permute-start.6 = (f32[40,25,10,1]{0,1,3,2:T(8,128)S(1)}, f32[40,25,10,1]{0,1,3,2:T(8,128)S(1)}, u32[]{:S(2)}, u32[]{:S(2)}) collective-permute-start(f32[40,25,10,1]{0,1,3,2:T(8,128)S(1)} %copy.126), channel_id=1, source_target_pairs={{0,1},{1,2},{2,3},{3,4},{4,5},{5,6},{6,7},{7,8},{8,9},{9,10},{10,1... | collective-permute-start | bytes 120008 | tf_op jit(solution)/shard_map/ppermute | solution.py:20
  118.7 21.0 %collective-permute-start.7 = (f32[40,25,10,1]{0,1,3,2:T(8,128)S(1)}, f32[40,25,10,1]{0,1,3,2:T(8,128)S(1)}, u32[]{:S(2)}, u32[]{:S(2)}) collective-permute-start(f32[40,25,10,1]{0,1,3,2:T(8,128)S(1)} %copy.127), channel_id=1, source_target_pairs={{1,0},{2,1},{3,2},{4,3},{5,4},{6,5},{7,6},{8,7},{9,8},{10,9},{11,1... | collective-permute-start | bytes 120008 | tf_op jit(solution)/shard_map/ppermute | solution.py:23
where the time goes:
time: 1010 us; the launch traced here: 1000 us
  blocking collectives  511 us (51%)
  matrix products  199 us (20%)
  local copies, waits for them, and re-layouts  190 us (19%)
  other arithmetic  62.4 us (6%)
  starting transfers between devices  29.1 us (3%)
    psum x8, blocking collectives, single_block(): prior = lax.psum(own_part, ('lat', 'lon'))  511 us
    dot_general x8, matrix products, apply_block(): jnp.einsum('mvc,mk->vck', sample_realizations, weights, precision=HIGHEST)  114 us
    dot_general x8, matrix products, apply_block(): jnp.einsum('vck,mk->mvc', projected * damping_factors, shifts, precision=...  84.8 us
    while x8, local copies, waits for them, and re-layouts  73 us
    gather x16, local copies, waits for them, and re-layouts, read_priors(): jnp.take(sample_realizations.reshape(members, variables * cells), positio...  43.4 us
    unnamed x22, local copies, waits for them, and re-layouts  28.7 us
    ppermute x4, starting transfers between devices, with_halo(): lax.ppermute(lax.slice_in_dim(block, 0, width, axis=dim), axis, backward)  23.1 us
    select_n x2, other arithmetic, zero_outside_block(): return jnp.where(inside[:, None], padded, 0.0)  23 us
  transfers between devices with their start and end apart: 8, of which 2 were waited for; matrix products, arithmetic and copies ran while one was open for 4% of the time, Pallas kernels for 0%

commit v1 on v0

v1 whole, which is shorter than its diff:
```python
import jax
import jax.numpy as jnp
from jax import lax
from jax.experimental import pallas as pl
from jax.experimental.pallas import tpu as pltpu
from jax.sharding import PartitionSpec as P

MEMBERS, NVAR, ROWS, COLS = 40, 25, 8, 128
NLON = 2048
NB, BLOCK = 8, 128
LOC = 32.0
KC = 32
NCH = BLOCK // KC
VG = 5
F32, BF = jnp.float32, jnp.bfloat16
STEPS = 2
DIFFUSE = 0.1


def taper_sq(d2):
    z = jnp.sqrt(d2) * (1.0 / LOC)
    inner = (((-0.25 * z + 0.5) * z + 0.625) * z - 5.0 / 3.0) * z * z + 1.0
    outer = (
        ((((z * (1.0 / 12.0) - 0.5) * z + 0.625) * z + 5.0 / 3.0) * z - 5.0) * z
        + 4.0
        - (2.0 / 3.0) / jnp.maximum(z, 1.0)
    )
    return jnp.where(z <= 1.0, inner, jnp.where(z < 2.0, outer, 0.0))


def hi(x):
    return x.astype(BF).astype(F32)


def dot(a, b, dims=((1,), (0,))):
    return lax.dot_general(a, b, (dims, ((), ())), preferred_element_type=F32)


def analysis_kernel(
    orig_ref, x_ref, y_ref, lat_ref, lon_ref, val_ref, err_ref,
    out_ref,
    ys, a_all, s_all, a_pk, b_pk, t_pk, xv, rhs, q3, nch,
):
    lat0 = orig_ref[0]
    lon0 = orig_ref[1]
    lat = lat_ref[...].astype(F32)
    lon = lon_ref[...].astype(F32)
    lat_t = lat.T
    lon_t = lon.T
    lat0f = lat0.astype(F32)
    lon0f = lon0.astype(F32)
    dy = jnp.maximum(jnp.maximum(lat0f - lat, lat - (lat0f + (ROWS - 1))), 0.0)
    off = lon - lon0f
    off = jnp.where(off < 0, off + NLON, off)
    dx = jnp.maximum(jnp.minimum(off - (COLS - 1), NLON - off), 0.0)
    reach = dx * dx + dy * dy < 4.0 * LOC * LOC
    reach_b = reach.astype(F32)
    before = (
        lax.broadcasted_iota(jnp.int32, (BLOCK, BLOCK), 0)
        < lax.broadcasted_iota(jnp.int32, (BLOCK, BLOCK), 1)
    ).astype(F32)
    rank = dot(reach_b.astype(BF), before.astype(BF))
    rank = jnp.where(reach, rank, -1.0)
    for b in range(NB):
        n = jnp.sum(reach_b[b : b + 1, :])
        nch[b] = ((n + (KC - 1)) * (1.0 / KC)).astype(jnp.int32)

    for b in range(NB):
        ys[:, b * BLOCK : (b + 1) * BLOCK] = y_ref[b]
    zero8 = jnp.zeros((8, BLOCK), F32)
    for b in range(NB):
        prior = ys[:, b * BLOCK : (b + 1) * BLOCK]
        average = jnp.sum(prior, axis=0, keepdims=True) * (1.0 / MEMBERS)
        anomaly = prior - average
        spread = jnp.sum(anomaly * anomaly, axis=0, keepdims=True) / (MEMBERS - 1)
        errors = err_ref[b : b + 1, :]
        total = spread + errors
        weights = anomaly * (1.0 / ((MEMBERS - 1) * total))
        shifts = (val_ref[b : b + 1, :] - average) - anomaly * (
            1.0 / (1.0 + jnp.sqrt(errors / total))
        )
        wh = hi(weights)
        a = jnp.concatenate([wh, weights - wh, wh, zero8], axis=0).T.astype(BF)
        sh = shifts.astype(BF)
        sl = (shifts - sh.astype(F32)).astype(BF)
        s2 = jnp.concatenate([sh, sl], axis=1)
        a_all[b] = a
        s_all[b] = s2
        if b + 1 < NB:
            first = (b + 1) * BLOCK
            s3 = jnp.concatenate([sh, sl, sh], axis=1)
            latk = lat_t[:, b : b + 1]
            lonk = lon_t[:, b : b + 1]
            for j in range(b + 1, NB):
                yl = ys[:, j * BLOCK : (j + 1) * BLOCK]
                yh = hi(yl)
                y3 = jnp.concatenate([yh, yh, yl - yh, zero8], axis=0).astype(BF)
                p = dot(a, y3)
                dlat = latk - lat[j : j + 1, :]
                dlon = jnp.abs(lonk - lon[j : j + 1, :])
                dlon = jnp.minimum(dlon, NLON - dlon)
                q = p * taper_sq(dlat * dlat + dlon * dlon)
                qh = q.astype(BF)
                ql = (q - qh.astype(F32)).astype(BF)
                ys[:, j * BLOCK : (j + 1) * BLOCK] = yl + dot(
                    s3, jnp.concatenate([qh, qh, ql], axis=0)
                )

    row_id = lax.broadcasted_iota(jnp.int32, (KC, BLOCK), 0)
    col_f = lax.broadcasted_iota(jnp.int32, (KC, COLS), 1).astype(F32) + lon0f
    for b in range(NB):

        @pl.loop(0, nch[b])
        def _(c):
            slot = b * NCH + c
            pick = ((row_id + c * KC).astype(F32) == rank[b : b + 1, :]).astype(F32)
            pick_b = pick.astype(BF)
            a_pk[slot] = dot(pick_b, a_all[b]).astype(BF)
            zero = jnp.zeros_like(pick_b)
            pick3 = jnp.concatenate(
                [
                    jnp.concatenate([pick_b, zero], axis=1),
                    jnp.concatenate([zero, pick_b], axis=1),
                    jnp.concatenate([pick_b, zero], axis=1),
                ],
                axis=0,
            )
            b_pk[slot] = dot(s_all[b], pick3, ((1,), (1,))).astype(BF)
            latc = jnp.sum(pick * lat[b : b + 1, :], axis=1, keepdims=True)
            lonc = jnp.sum(pick * lon[b : b + 1, :], axis=1, keepdims=True)
            dlon = jnp.abs(lonc - col_f)
            dlon = jnp.minimum(dlon, NLON - dlon)
            dlon = dlon * dlon
            for r in range(ROWS):
                dlat = latc - (lat0f + float(r))
                t_pk[slot, :, r * COLS : (r + 1) * COLS] = taper_sq(dlon + dlat * dlat)

    zero256 = jnp.zeros((8, 256), F32)

    @pl.loop(0, NVAR // VG)
    def _(g):
        for i in range(VG):
            for r in range(ROWS):
                xv[i, :, r * COLS : (r + 1) * COLS] = x_ref[
                    pl.ds((g * VG + i) * ROWS + r, MEMBERS, stride=NVAR * ROWS), :
                ]

        @pl.loop(0, NB)
        def _(b):
            for i in range(VG):
                for h in range(4):
                    x = xv[i, :, h * 256 : (h + 1) * 256]
                    xh = hi(x)
                    rhs[i, :, h * 256 : (h + 1) * 256] = jnp.concatenate(
                        [xh, xh, x - xh, zero256], axis=0
                    ).astype(BF)

            @pl.loop(0, nch[b])
            def _(c):
                slot = b * NCH + c
                a = a_pk[slot]
                s3 = b_pk[slot]
                for i in range(VG):
                    q = dot(a, rhs[i]) * t_pk[slot]
                    qh = q.astype(BF)
                    q3[i] = jnp.concatenate([qh, qh, (q - qh.astype(F32)).astype(BF)], axis=0)
                for i in range(VG):
                    xv[i] += dot(s3, q3[i])

        for i in range(VG):
            for r in range(ROWS):
                out_ref[
                    pl.ds((g * VG + i) * ROWS + r, MEMBERS, stride=NVAR * ROWS), :
                ] = xv[i, :, r * COLS : (r + 1) * COLS]


def analysis(origin, x, y, lat, lon, val, err):
    vm = pl.BlockSpec(memory_space=pltpu.VMEM)
    return pl.pallas_call(
        analysis_kernel,
        out_shape=jax.ShapeDtypeStruct((MEMBERS * NVAR * ROWS, COLS), F32),
        in_specs=[pl.BlockSpec(memory_space=pltpu.SMEM)] + [vm] * 6,
        out_specs=vm,
        scratch_shapes=[
            pltpu.VMEM((MEMBERS, NB * BLOCK), F32),
            pltpu.VMEM((NB, BLOCK, 128), BF),
            pltpu.VMEM((NB, MEMBERS, 256), BF),
            pltpu.VMEM((NB * NCH, KC, 128), BF),
            pltpu.VMEM((NB * NCH, MEMBERS, 3 * KC), BF),
            pltpu.VMEM((NB * NCH, KC, ROWS * COLS), F32),
            pltpu.VMEM((VG, MEMBERS, ROWS * COLS), F32),
            pltpu.VMEM((VG, 128, ROWS * COLS), BF),
            pltpu.VMEM((VG, 3 * KC, ROWS * COLS), BF),
            pltpu.SMEM((NB,), jnp.int32),
        ],
        compiler_params=pltpu.CompilerParams(vmem_limit_bytes=40 << 20),
        name="analysis",
    )(origin, x, y, lat, lon, val, err)


def with_halo(block, sides, width):
    for axis, dim in sides:
        count = lax.axis_size(axis)
        forward = [(i, i + 1) for i in range(count - 1)]
        forward.append((count - 1, 0))
        backward = [(target, source) for source, target in forward]
        low = lax.ppermute(
            lax.slice_in_dim(block, block.shape[dim] - width, None, axis=dim), axis, forward
        )
        high = lax.ppermute(lax.slice_in_dim(block, 0, width, axis=dim), axis, backward)
        block = jnp.concatenate([low, block, high], axis=dim)
    return block


def advance(padded, east_wind, north_wind):
    centre = padded[..., 1:-1, 1:-1]
    above_v = padded[..., 2:, 1:-1]
    below_v = padded[..., :-2, 1:-1]
    right_v = padded[..., 1:-1, 2:]
    left_v = padded[..., 1:-1, :-2]
    return (
        centre
        - 0.5 * east_wind * (right_v - left_v)
        - 0.5 * north_wind * (above_v - below_v)
        + DIFFUSE * (right_v + left_v + above_v + below_v - 4.0 * centre)
    )


def zero_outside_block(padded, margin):
    overall_line_count = padded.shape[-2]
    band_rows = overall_line_count - 2 * margin
    global_row = (
        lax.axis_index("lat") * band_rows - margin + lax.iota(jnp.int32, overall_line_count)
    )
    inside = (global_row >= 0) & (global_row < band_rows * lax.axis_size("lat"))
    return jnp.where(inside[:, None], padded, 0.0)


def read_priors(sample_realizations, sel_lat, sel_lon, sel_var, band_rows, band_cols):
    members, variables, cells = sample_realizations.shape
    local_lat = sel_lat - lax.axis_index("lat") * band_rows
    local_lon = sel_lon - lax.axis_index("lon") * band_cols
    owned = (local_lat >= 0) & (local_lat < band_rows) & (local_lon >= 0) & (local_lon < band_cols)
    position = (
        sel_var * cells
        + jnp.clip(local_lat, 0, band_rows - 1) * band_cols
        + jnp.clip(local_lon, 0, band_cols - 1)
    )
    picked = jnp.take(sample_realizations.reshape(members, variables * cells), position, axis=1)
    return jnp.where(owned[None, :], picked, 0.0)


def body(prognostic_samples, wind, obs_lat, obs_lon, obs_var, obs_value, obs_error):
    members, variables, band_rows, band_cols = prognostic_samples.shape
    state_now = prognostic_samples
    for section in range(STEPS):
        padded = with_halo(state_now, (("lat", 2), ("lon", 3)), 1)
        state_now = advance(zero_outside_block(padded, 1), wind[0], wind[1])
    sample_realizations = state_now.reshape(members, variables, band_rows * band_cols)
    own_part = read_priors(
        sample_realizations,
        obs_lat.reshape(-1),
        obs_lon.reshape(-1),
        obs_var.reshape(-1),
        band_rows,
        band_cols,
    )
    prior = lax.psum(own_part, ("lat", "lon"))
    y = jnp.moveaxis(prior.reshape(members, NB, BLOCK), 1, 0)
    origin = jnp.stack([lax.axis_index("lat") * band_rows, lax.axis_index("lon") * band_cols])
    out = analysis(
        origin.astype(jnp.int32),
        state_now.reshape(members * variables * band_rows, band_cols),
        y,
        obs_lat.reshape(NB, BLOCK),
        obs_lon.reshape(NB, BLOCK),
        obs_value.reshape(NB, BLOCK),
        obs_error.reshape(NB, BLOCK),
    )
    return out.reshape(members, variables, band_rows, band_cols)


def solution(mesh):
    in_specs = (P(None, None, "lat", "lon"), P(None, "lat", "lon"), P(), P(), P(), P(), P())
    out_specs = P(None, None, "lat", "lon")
    return jax.shard_map(body, mesh=mesh, in_specs=in_specs, out_specs=out_specs, check_vma=False)
```

time: 1010 us -> 359 us (0.36)
  blocking collectives: 511 us -> 0 us
  matrix products: 199 us -> 0 us
  waiting for transfers between devices: 8.6 us -> 147 us
  local copies, waits for them, and re-layouts: 190 us -> 94.4 us
  Pallas kernels: 0 us -> 35.1 us
  between operations: 0.58 us -> 13.6 us
  starting transfers between devices: 29.1 us -> 16.5 us
    psum x8 -> x0, blocking collectives: 511 us -> none  [single_block(): prior = lax.psum(own_part, ('lat', 'lon'))]
    dot_general x16 -> x0, matrix products: 199 us -> none  [the longest x8 114 us: apply_block(): jnp.einsum('mvc,mk->vck', sample_realizations, weights, precision=HIGHEST)]
    psum x0 -> x1, waiting for transfers between devices: none -> 138 us  [body(): prior = lax.psum(own_part, ('lat', 'lon'))]
    while x8 -> x0, local copies, waits for them, and re-layouts: 73 us -> none
    gather x16 -> x1, local copies, waits for them, and re-layouts: 43.4 us -> 7.79 us  [read_priors(): jnp.take(sample_realizations.reshape(members, variables * cells), positio...]
    pallas_call x0 -> x1, Pallas kernels: none -> 35.1 us  [analysis(): pl.pallas_call(analysis_kernel, out_shape=jax.ShapeDtypeStruct((MEMBERS *...]
    add x0 -> x2, local copies, waits for them, and re-layouts: none -> 13.9 us  [advance(): centre - 0.5 * east_wind * (right_v - left_v)]
    ppermute x4, starting transfers between devices: 23.1 us -> 10.4 us  [with_halo(): lax.ppermute(lax.slice_in_dim(block, 0, width, axis=dim), axis, backward)]
  transfers between devices with their start and end apart: 8 -> 9, of which waited for: 2 -> 3; matrix products, arithmetic and copies ran while one was open for 4% -> 12% of each run, Pallas kernels for 0% -> 0%
where the time goes in v1:
time: 359 us
  waiting for transfers between devices  147 us (41%)
  local copies, waits for them, and re-layouts  94.4 us (26%)
  other arithmetic  52.4 us (15%)
  Pallas kernels  35.1 us (10%)
  starting transfers between devices  16.5 us (5%)
  between operations  13.6 us (4%)
    psum x1, waiting for transfers between devices, body(): prior = lax.psum(own_part, ('lat', 'lon'))  138 us
    pallas_call x1, Pallas kernels, analysis(): pl.pallas_call(analysis_kernel, out_shape=jax.ShapeDtypeStruct((MEMBERS *...  35.1 us
    unnamed x27, local copies, waits for them, and re-layouts  28.7 us
    select_n x2, other arithmetic, zero_outside_block(): return jnp.where(inside[:, None], padded, 0.0)  23 us
    add x2, other arithmetic, advance(): centre - 0.5 * east_wind * (right_v - left_v)  20.1 us
    concatenate x1, local copies, waits for them, and re-layouts, with_halo(): block = jnp.concatenate([low, block, high], axis=dim)  15.4 us
    add x2, local copies, waits for them, and re-layouts, advance(): centre - 0.5 * east_wind * (right_v - left_v)  13.9 us
    ppermute x4, starting transfers between devices, with_halo(): lax.ppermute(lax.slice_in_dim(block, 0, width, axis=dim), axis, backward)  10.4 us
  transfers between devices with their start and end apart: 9, of which 3 were waited for; matrix products, arithmetic and copies ran while one was open for 12% of the time, Pallas kernels for 0%

profile of v1, /device:TPU:1, one launch (start us, length us, event | category | flops | bytes accessed | tf_op | source)
XLA Modules:
  0.0 358.7 jit_solution(15789583099227045076)
XLA Ops:
  6.5 4.1 %fusion.3 = (f32[40,25,1,128]{3,2,1,0:T(1,128)S(1)}, f32[40,25,1,128]{3,2,1,0:T(1,128)S(1)}) fusion(f32[40,25,8,128]{3,2,1,0:T(8,128)} %param.7), kind=kLoop, calls=%fused_computation.21 | loop fusion | bytes 2048000 | tf_op jit(solution)/shard_map/slice | solution.py:208
  10.7 2.6 collective-permute-start
  13.3 0.8 copy.59
  14.1 0.0 collective-permute-start.1
  14.1 0.0 copy-start.7
  14.2 9.6 %copy.43 = f32[40,25,8,128]{0,1,3,2:T(8,128)} copy(f32[40,25,8,128]{3,2,1,0:T(8,128)} %param.7) | data formatting | bytes 8192000 | tf_op args[0]
  23.8 1.8 copy.42
  25.6 0.0 collective-permute-done.1
  25.7 2.8 copy.44
  28.5 8.5 %pad_maximum_fusion = f32[40,25,10,128]{0,1,3,2:T(8,128)S(1)} fusion(f32[40,25,1,128]{0,1,3,2:T(8,128)} %copy.44, f32[40,25,8,128]{0,1,3,2:T(8,128)} %copy.43, f32[40,25,1,128]{0,1,3,2:T(8,128)S(1)} %copy.42), kind=kLoop, calls=%fused_computation.1 | loop fusion | flops 2560000 | bytes 10240000 | tf_op jit(solution)/shard_map/concatenate | solution.py:211
  36.9 7.0 %copy-done.2 = f32[40,25,10,128]{0,1,3,2:T(8,128)} copy-done((f32[40,25,10,128]{0,1,3,2:T(8,128)}, f32[40,25,10,128]{0,1,3,2:T(8,128)S(1)}, u32[]{:S(2)}) %copy-start.2) | copy-done | bytes 5120024
  44.0 1.4 collective-permute-start.2
  45.3 5.2 %collective-permute-start.3 = (f32[40,25,10,1]{0,1,3,2:T(8,128)S(1)}, f32[40,25,10,1]{0,1,3,2:T(8,128)S(1)}, u32[]{:S(2)}, u32[]{:S(2)}) collective-permute-start(f32[40,25,10,1]{0,1,3,2:T(8,128)S(1)} %get-tuple-element.6), channel_id=1, source_target_pairs={{1,0},{2,1},{3,2},{4,3},{5,4},{6,5},{7,6},{8,7},{9,8},{10,9},{11,1... | collective-permute-start | bytes 120008 | tf_op jit(solution)/shard_map/ppermute | solution.py:210
  50.5 15.4 %copy.46 = f32[40,25,10,128]{3,0,2,1:T(8,128)} copy(f32[40,25,10,128]{0,1,3,2:T(8,128)} %copy-done.2) | data formatting | bytes 10240000 | tf_op jit(solution)/shard_map/concatenate | solution.py:211
  65.9 0.0 collective-permute-done.2
  65.9 3.3 copy.45
  69.3 0.0 collective-permute-done.3
  69.3 3.3 copy.47
  72.6 13.4 %maximum_select_fusion = f32[40,25,10,130]{3,0,2,1:T(8,128)} fusion(f32[40,25,10,1]{3,0,2,1:T(8,128)} %copy.47, f32[40,25,10,128]{3,0,2,1:T(8,128)} %copy.46, f32[40,25,10,1]{3,0,2,1:T(8,128)} %copy.45, pred[10]{0:T(512)(128)(4,1)S(1)} %compare_and_fusion.2), kind=kLoop, calls=%fused_computation.2 | loop fusion | flops 3900000 | bytes 10400010 | tf_op jit(solution)/shard_map/jit(_where)/select_n | solution.py:236
  86.0 14.3 %multiply_add_fusion.1 = f32[40,25,8,128]{3,0,2,1:T(8,128)S(1)} fusion(f32[40,25,10,130]{3,0,2,1:T(8,128)} %maximum_select_fusion, f32[8,128]{1,0:T(8,128)S(1)} %get-tuple-element.14, f32[8,128]{1,0:T(8,128)S(1)} %get-tuple-element.13), kind=kLoop, calls=%fused_computation.6 | loop fusion | flops 13312000 | bytes 24584192 | tf_op jit(solution)/shard_map/add | solution.py:222
  100.3 0.0 copy-start.3
  100.3 0.1 fusion.2
  100.4 2.0 collective-permute-start.4
  102.4 0.1 collective-permute-start.5
  102.6 5.8 %collective-permute-done.4 = f32[40,25,1,128]{3,0,2,1:T(8,128)S(1)} collective-permute-done((f32[40,25,1,128]{3,0,2,1:T(8,128)S(1)}, f32[40,25,1,128]{3,0,2,1:T(8,128)S(1)}, u32[]{:S(2)}, u32[]{:S(2)}) %collective-permute-start.4) | collective-permute-done | bytes 512032 | tf_op jit(solution)/shard_map/ppermute | solution.py:207
  108.4 2.8 collective-permute-done.5
  111.2 0.4 pad_maximum_fusion.1
  111.6 5.5 %fusion.1 = (f32[40,25,10,1]{3,0,2,1:T(8,128)}, f32[40,25,10,1]{3,0,2,1:T(8,128)}) fusion(f32[40,25,10,128]{3,0,2,1:T(8,128)S(1)} %pad_maximum_fusion.1), kind=kLoop, calls=%fused_computation.19 | loop fusion | bytes 160000 | tf_op jit(solution)/shard_map/slice | solution.py:208
  117.2 4.1 %copy.60 = f32[40,25,10,1]{0,1,3,2:T(8,128)S(1)} copy(f32[40,25,10,1]{3,0,2,1:T(8,128)} %get-tuple-element.7) | data formatting | bytes 80000
  121.3 0.1 collective-permute-start.6
  121.3 4.1 %copy.61 = f32[40,25,10,1]{0,1,3,2:T(8,128)S(1)} copy(f32[40,25,10,1]{3,0,2,1:T(8,128)} %get-tuple-element.8) | data formatting | bytes 80000
  125.4 5.1 %collective-permute-start.7 = (f32[40,25,10,1]{0,1,3,2:T(8,128)S(1)}, f32[40,25,10,1]{0,1,3,2:T(8,128)S(1)}, u32[]{:S(2)}, u32[]{:S(2)}) collective-permute-start(f32[40,25,10,1]{0,1,3,2:T(8,128)S(1)} %copy.61), channel_id=1, source_target_pairs={{1,0},{2,1},{3,2},{4,3},{5,4},{6,5},{7,6},{8,7},{9,8},{10,9},{11,1... | collective-permute-start | bytes 120008 | tf_op jit(solution)/shard_map/ppermute | solution.py:210
  130.5 0.0 collective-permute-done.6
  130.6 3.3 copy.50
  133.9 3.3 copy.51
  137.2 9.6 %maximum_select_fusion.1 = f32[40,25,10,130]{3,0,2,1:T(8,128)S(1)} fusion(f32[40,25,10,1]{3,0,2,1:T(8,128)} %copy.51, f32[40,25,1,128]{3,0,2,1:T(8,128)S(1)} %collective-permute-done.5, f32[40,25,8,128]{3,0,2,1:T(8,128)} %copy-done.3, f32[40,25,1,128]{3,0,2,1:T(8,128)S(1)} %collective-permute-done.4, f32[40,25,10,1]{3,0,2,1:T(8,128)} %copy.50, ...), kind=kLoop, calls=%fused_computation.3 | loop fusion | flops 6500000 | bytes 10400010 | tf_op jit(solution)/shard_map/jit(_where)/select_n | solution.py:236
  146.9 5.7 %multiply_add_fusion = f32[40,25,8,128]{3,0,2,1:T(8,128)} fusion(f32[40,25,10,130]{3,0,2,1:T(8,128)S(1)} %maximum_select_fusion.1, f32[8,128]{1,0:T(8,128)S(1)} %get-tuple-element.14, f32[8,128]{1,0:T(8,128)S(1)} %get-tuple-element.13), kind=kLoop, calls=%fused_computation.5 | loop fusion | flops 13312000 | bytes 24584192 | tf_op jit(solution)/shard_map/add | solution.py:222
  152.6 9.0 %copy.53 = f32[40,25,8,128]{0,3,2,1:T(8,128)} copy(f32[40,25,8,128]{3,0,2,1:T(8,128)} %multiply_add_fusion) | data formatting | bytes 8192000 | tf_op jit(solution)/shard_map/add | solution.py:222
  161.6 7.8 %gather_fusion = f32[1024,40]{1,0:T(8,128)S(1)} fusion(f32[40,25600]{0,1:T(8,128)} %bitcast.21, s32[1024]{0:T(1024)S(1)} %broadcast_clamp_fusion), kind=kCustom, calls=%fused_computation | custom fusion | bytes 331776 | tf_op jit(solution)/shard_map/jit(_take)/gather | solution.py:249
  169.4 0.3 select_select_fusion
  169.7 0.9 copy.55
  170.6 0.0 all-reduce.2.cloned.1.call-update
  170.6 0.1 pad_add_fusion.orig_ref
  170.7 4.9 %copy.52 = f32[40,25,8,128]{3,2,1,0:T(8,128)} copy(f32[40,25,8,128]{3,0,2,1:T(8,128)} %multiply_add_fusion) | data formatting | bytes 8192000 | tf_op jit(solution)/shard_map/add | solution.py:222
  175.6 138.1 %all-reduce.2.cloned.1.call-done.y_ref = f32[8,40,128]{2,1,0:T(8,128)} async-done(((f32[8,40,128]{2,1,0:T(8,128)}), f32[8,40,128]{2,1,0:T(8,128)}) %all-reduce.2.cloned.1.call-update) | async-done | bytes 163856 | tf_op jit(solution)/shard_map/psum | solution.py:268
  313.7 2.2 copy-done
  315.9 0.9 copy-done.1
  316.8 35.1 %analysis.1 = f32[8000,128]{1,0:T(8,128)} custom-call(s32[2]{0:T(128)S(1)} %pad_add_fusion.orig_ref, f32[8000,128]{1,0:T(8,128)S(1)} %bitcast.20, f32[8,40,128]{2,1,0:T(8,128)S(1)} %copy-done.1, s32[8,128]{1,0:T(8,128)S(1)} %reshape.161.lat_ref, s32[8,128]{1,0:T(8,128)S(1)} %reshape.162.lon_ref, f32[8,128]{1,0:T(8,128)S(1)} %reshape.163.val_ref, ...), custom_call_target="tpu_custom_call" | custom-call | tf_op jit(solution)/shard_map/analysis/pallas_call | solution.py:179
  (34 shorter events, 0.2 us)
Async XLA Ops:
  6.5 307.2 %all-reduce.2.cloned.1.call-start = ((), (), s32[]{:S(2)}) async-start(), calls=%async_computation | async-start | bytes 327680 | tf_op jit(solution)/shard_map/psum | solution.py:268
  10.7 13.1 %collective-permute-start = (f32[40,25,1,128]{3,0,2,1:T(8,128)S(1)}, f32[40,25,1,128]{3,0,2,1:T(8,128)S(1)}, u32[]{:S(2)}, u32[]{:S(2)}) collective-permute-start(f32[40,25,1,128]{3,0,2,1:T(8,128)S(1)} %copy.58), channel_id=1, source_target_pairs={{0,16},{16,32},{32,48},{48,64},{64,80},{80,96},{96,112},{112,0},{1... | collective-permute-start | bytes 1536008 | tf_op jit(solution)/shard_map/ppermute | solution.py:207
  14.1 11.5 %collective-permute-start.1 = (f32[40,25,1,128]{3,0,2,1:T(8,128)}, f32[40,25,1,128]{3,0,2,1:T(8,128)S(1)}, u32[]{:S(2)}, u32[]{:S(2)}) collective-permute-start(f32[40,25,1,128]{3,0,2,1:T(8,128)} %copy.59), channel_id=1, source_target_pairs={{16,0},{32,16},{48,32},{64,48},{80,64},{96,80},{112,96},{0,112},{1... | collective-permute-start | bytes 1536008 | tf_op jit(solution)/shard_map/ppermute | solution.py:210
  14.1 9.6 %copy-start.6 = (f32[2,8,128]{2,1,0:T(8,128)S(1)}, f32[2,8,128]{2,1,0:T(8,128)}, u32[]{:S(2)}) copy-start(f32[2,8,128]{2,1,0:T(8,128)} %param.8) | copy-start | bytes 24580
  14.1 9.6 %copy-start.4 = (s32[2,512]{1,0:T(2,128)S(1)}, s32[2,512]{1,0:T(2,128)}, u32[]{:S(2)}) copy-start(s32[2,512]{1,0:T(2,128)} %param.9) | copy-start | bytes 12292
  14.1 9.6 %copy-start.5 = (s32[2,512]{1,0:T(2,128)S(1)}, s32[2,512]{1,0:T(2,128)}, u32[]{:S(2)}) copy-start(s32[2,512]{1,0:T(2,128)} %param.10) | copy-start | bytes 12292
  14.1 9.6 %copy-start.7 = (s32[2,512]{1,0:T(2,128)S(1)}, s32[2,512]{1,0:T(2,128)}, u32[]{:S(2)}) copy-start(s32[2,512]{1,0:T(2,128)} %param.11) | copy-start | bytes 12292
  36.9 7.0 %copy-start.2 = (f32[40,25,10,128]{0,1,3,2:T(8,128)}, f32[40,25,10,128]{0,1,3,2:T(8,128)S(1)}, u32[]{:S(2)}) copy-start(f32[40,25,10,128]{0,1,3,2:T(8,128)S(1)} %pad_maximum_fusion) | copy-start | bytes 15360004
  44.0 22.0 %collective-permute-start.2 = (f32[40,25,10,1]{0,1,3,2:T(8,128)S(1)}, f32[40,25,10,1]{0,1,3,2:T(8,128)S(1)}, u32[]{:S(2)}, u32[]{:S(2)}) collective-permute-start(f32[40,25,10,1]{0,1,3,2:T(8,128)S(1)} %get-tuple-element.5), channel_id=1, source_target_pairs={{0,1},{1,2},{2,3},{3,4},{4,5},{5,6},{6,7},{7,8},{8,9},{9,10},{10,1... | collective-permute-start | bytes 120008 | tf_op jit(solution)/shard_map/ppermute | solution.py:207
  45.3 23.9 %collective-permute-start.3 = (f32[40,25,10,1]{0,1,3,2:T(8,128)S(1)}, f32[40,25,10,1]{0,1,3,2:T(8,128)S(1)}, u32[]{:S(2)}, u32[]{:S(2)}) collective-permute-start(f32[40,25,10,1]{0,1,3,2:T(8,128)S(1)} %get-tuple-element.6), channel_id=1, source_target_pairs={{1,0},{2,1},{3,2},{4,3},{5,4},{6,5},{7,6},{8,7},{9,8},{10,9},{11,1... | collective-permute-start | bytes 120008 | tf_op jit(solution)/shard_map/ppermute | solution.py:210
  100.3 11.3 %copy-start.3 = (f32[40,25,8,128]{3,0,2,1:T(8,128)}, f32[40,25,8,128]{3,0,2,1:T(8,128)S(1)}, u32[]{:S(2)}) copy-start(f32[40,25,8,128]{3,0,2,1:T(8,128)S(1)} %multiply_add_fusion.1) | copy-start | bytes 12288004
  100.4 8.0 %collective-permute-start.4 = (f32[40,25,1,128]{3,0,2,1:T(8,128)S(1)}, f32[40,25,1,128]{3,0,2,1:T(8,128)S(1)}, u32[]{:S(2)}, u32[]{:S(2)}) collective-permute-start(f32[40,25,1,128]{3,0,2,1:T(8,128)S(1)} %get-tuple-element.9), channel_id=1, source_target_pairs={{0,16},{16,32},{32,48},{48,64},{64,80},{80,96},{96,112},{112,0},{1... | collective-permute-start | bytes 1536008 | tf_op jit(solution)/shard_map/ppermute | solution.py:207
  102.4 8.8 %collective-permute-start.5 = (f32[40,25,1,128]{3,0,2,1:T(8,128)S(1)}, f32[40,25,1,128]{3,0,2,1:T(8,128)S(1)}, u32[]{:S(2)}, u32[]{:S(2)}) collective-permute-start(f32[40,25,1,128]{3,0,2,1:T(8,128)S(1)} %get-tuple-element.10), channel_id=1, source_target_pairs={{16,0},{32,16},{48,32},{64,48},{80,64},{96,80},{112,96},{0,112},{1... | collective-permute-start | bytes 1536008 | tf_op jit(solution)/shard_map/ppermute | solution.py:210
  117.2 13.3 %copy-start.8 = (f32[2,512]{1,0:T(2,128)S(1)}, f32[2,512]{1,0:T(2,128)}, u32[]{:S(2)}) copy-start(f32[2,512]{1,0:T(2,128)} %param.12) | copy-start | bytes 12292
  117.2 13.3 %copy-start.9 = (f32[2,512]{1,0:T(2,128)S(1)}, f32[2,512]{1,0:T(2,128)}, u32[]{:S(2)}) copy-start(f32[2,512]{1,0:T(2,128)} %param.13) | copy-start | bytes 12292
  121.3 9.3 %collective-permute-start.6 = (f32[40,25,10,1]{0,1,3,2:T(8,128)S(1)}, f32[40,25,10,1]{0,1,3,2:T(8,128)S(1)}, u32[]{:S(2)}, u32[]{:S(2)}) collective-permute-start(f32[40,25,10,1]{0,1,3,2:T(8,128)S(1)} %copy.60), channel_id=1, source_target_pairs={{0,1},{1,2},{2,3},{3,4},{4,5},{5,6},{6,7},{7,8},{8,9},{9,10},{10,1... | collective-permute-start | bytes 120008 | tf_op jit(solution)/shard_map/ppermute | solution.py:207
  125.4 8.5 %collective-permute-start.7 = (f32[40,25,10,1]{0,1,3,2:T(8,128)S(1)}, f32[40,25,10,1]{0,1,3,2:T(8,128)S(1)}, u32[]{:S(2)}, u32[]{:S(2)}) collective-permute-start(f32[40,25,10,1]{0,1,3,2:T(8,128)S(1)} %copy.61), channel_id=1, source_target_pairs={{1,0},{2,1},{3,2},{4,3},{5,4},{6,5},{7,6},{8,7},{9,8},{10,9},{11,1... | collective-permute-start | bytes 120008 | tf_op jit(solution)/shard_map/ppermute | solution.py:210
  313.7 2.2 copy-start
  315.9 0.9 copy-start.1
Sparse Core Ops, SparseCore 0:
  170.7 142.9 all-reduce.1

commit v2 on v1

--- a/solution.py
+++ b/solution.py
@@ -13,8 +13,290 @@
 NCH = BLOCK // KC
 VG = 5
 F32, BF = jnp.float32, jnp.bfloat16
-STEPS = 2
+VS = 5
+MG = MEMBERS // 8
+MESH = pl.DeviceIdType.MESH
 DIFFUSE = 0.1
+
+
+def front_kernel(
+    nlat, nlon,
+    x_ref, wind_ref, lat_ref, lon_ref, var_ref,
+    xf, out,
+    xt, from_lo, from_hi, edge, edge_w, edge_e, corner, wind_n, halo, halo1, coef,
+    part, line, block_sum, got_a, got_b,
+    s_row, r_row, s_edge, r_edge, s_corner, r_corner, s_wind, r_wind,
+    send, recv_a, recv_b, recv_c,
+):
+    me_lat = lax.axis_index("lat")
+    me_lon = lax.axis_index("lon")
+
+    def lat_peer(o):
+        return lax.rem(me_lat + (o + nlat), nlat)
+
+    def lon_peer(o):
+        return lax.rem(me_lon + (o + nlon), nlon)
+
+    def remote(src, dst, ssem, rsem, dlat, dlon):
+        return pltpu.make_async_remote_copy(
+            src_ref=src,
+            dst_ref=dst,
+            send_sem=ssem,
+            recv_sem=rsem,
+            device_id=(lat_peer(dlat) if dlat else me_lat, lon_peer(dlon) if dlon else me_lon),
+            device_id_type=MESH,
+        )
+
+    barrier = pltpu.get_barrier_semaphore()
+    greet = [(o, 0) for o in range(1, nlat)] + [(0, o) for o in range(1, nlon)]
+    greet += [(-1, -1), (-1, 1), (1, -1), (1, 1)]
+    for dlat, dlon in greet:
+        pl.semaphore_signal(
+            barrier,
+            inc=1,
+            device_id=(lat_peer(dlat) if dlat else me_lat, lon_peer(dlon) if dlon else me_lon),
+            device_id_type=MESH,
+        )
+
+    lane = lax.broadcasted_iota(jnp.int32, (8, COLS), 1)
+    lane4 = lax.rem(lane, 4)
+    edge[...] = jnp.zeros_like(edge)
+
+    def pack(vg):
+        @pl.loop(0, VS)
+        def _(vi):
+            v = vg * VS + vi
+            for r in range(ROWS):
+                e = edge[r, vg]
+                for mg in range(MG):
+                    t = x_ref[pl.ds(mg * (8 * NVAR * ROWS) + v * ROWS + r, 8, stride=NVAR * ROWS), :]
+                    xt[v, r, mg * 8 : (mg + 1) * 8, :] = t
+                    g4 = 4 * (vi * MG + mg)
+                    e = jnp.where(((lane - g4 + 2) & (COLS - 1)) < 4, pltpu.roll(t, g4, 1), e)
+                edge[r, vg] = e
+
+    def rows(vg, up):
+        vs = pl.ds(vg * VS, VS)
+        if up:
+            return remote(xt.at[vs, 0:2], from_hi.at[vs], s_row.at[vg, 0], r_row.at[vg, 0], -1, 0)
+        return remote(
+            xt.at[vs, ROWS - 2 : ROWS], from_lo.at[vs], s_row.at[vg, 1], r_row.at[vg, 1], 1, 0
+        )
+
+    winds = [
+        remote(wind_ref, wind_n.at[i], s_wind.at[i], r_wind.at[i], dlat, dlon)
+        for i, (dlat, dlon) in enumerate([(1, 0), (-1, 0), (0, 1), (0, -1)])
+    ]
+    edges = [
+        remote(edge, edge_w, s_edge.at[0], r_edge.at[0], 0, 1),
+        remote(edge, edge_e, s_edge.at[1], r_edge.at[1], 0, -1),
+    ]
+    corners = [
+        remote(edge.at[ROWS - 1], corner.at[0], s_corner.at[0], r_corner.at[0], 1, 1),
+        remote(edge.at[ROWS - 1], corner.at[1], s_corner.at[1], r_corner.at[1], 1, -1),
+        remote(edge.at[0], corner.at[2], s_corner.at[2], r_corner.at[2], -1, 1),
+        remote(edge.at[0], corner.at[3], s_corner.at[3], r_corner.at[3], -1, -1),
+    ]
+
+    pack(0)
+    pl.semaphore_wait(barrier, len(greet))
+    for w in winds:
+        w.start()
+    rows(0, True).start()
+    rows(0, False).start()
+    for vg in range(1, NVAR // VS):
+        pack(vg)
+        rows(vg, True).start()
+        rows(vg, False).start()
+    for e in edges + corners:
+        e.start()
+
+    for w in winds:
+        w.wait_recv()
+    has_lo = (me_lat > 0).astype(F32)
+    has_hi = (me_lat < nlat - 1).astype(F32)
+
+    def row_wind(r):
+        if r < 0:
+            return wind_n[0, 0, ROWS - 1 : ROWS, :], wind_n[0, 1, ROWS - 1 : ROWS, :]
+        if r == ROWS:
+            return wind_n[1, 0, 0:1, :], wind_n[1, 1, 0:1, :]
+        return wind_ref[0, r : r + 1, :], wind_ref[1, r : r + 1, :]
+
+    def four(u, v, r):
+        nxt, prv = DIFFUSE - 0.5 * v, DIFFUSE + 0.5 * v
+        if r == 0:
+            prv = prv * has_lo
+        if r == ROWS - 1:
+            nxt = nxt * has_hi
+        return DIFFUSE - 0.5 * u, DIFFUSE + 0.5 * u, nxt, prv
+
+    for r in range(-1, ROWS + 1):
+        u, v = row_wind(r)
+        for i, c in enumerate(four(u, v, r)):
+            coef[r + 1, i] = jnp.broadcast_to(c, (8, COLS))
+
+    for e in edges + corners:
+        e.wait_recv()
+    nvg = NVAR // VS
+    for vg in range(nvg):
+        halo[0, vg] = jnp.where(lane4 >= 2, corner[0, vg], corner[1, vg])
+        halo[ROWS + 1, vg] = jnp.where(lane4 >= 2, corner[2, vg], corner[3, vg])
+        for r in range(ROWS):
+            halo[r + 1, vg] = jnp.where(lane4 >= 2, edge_w[r, vg], edge_e[r, vg])
+    for r in range(ROWS):
+        u, v = [
+            jnp.where(
+                lane4 >= 2,
+                jnp.broadcast_to(wind_n[2, i, r : r + 1, COLS - 1 : COLS], (8, COLS)),
+                jnp.broadcast_to(wind_n[3, i, r : r + 1, 0:1], (8, COLS)),
+            )
+            for i in range(2)
+        ]
+        ce, cw, cn, cs = four(u, v, r)
+        for vg in range(nvg):
+            own, got = edge[r, vg], halo[r + 1, vg]
+            east = pltpu.roll(jnp.where(lane4 == 0, own, got), COLS - 1, 1)
+            west = pltpu.roll(jnp.where(lane4 == 3, own, got), 1, 1)
+            halo1[r, vg] = (
+                (1.0 - 4.0 * DIFFUSE) * got
+                + ce * east
+                + cw * west
+                + cn * halo[r + 2, vg]
+                + cs * halo[r, vg]
+            )
+
+    def step(q, nxt, prv, side, r):
+        east = pltpu.roll(jnp.where(lane == 0, side, q), COLS - 1, 1)
+        west = pltpu.roll(jnp.where(lane == COLS - 1, side, q), 1, 1)
+        return (
+            (1.0 - 4.0 * DIFFUSE) * q
+            + coef[r + 1, 0] * east
+            + coef[r + 1, 1] * west
+            + coef[r + 1, 2] * nxt
+            + coef[r + 1, 3] * prv
+        )
+
+    @pl.loop(0, nvg)
+    def _(vg):
+        rows(vg, True).wait_recv()
+        rows(vg, False).wait_recv()
+
+        @pl.loop(0, VS)
+        def _(vi):
+            v = vg * VS + vi
+            for mg in range(MG):
+                ms = slice(mg * 8, (mg + 1) * 8)
+                back = lax.rem(COLS - 4 * (vi * MG + mg), COLS)
+                q = [from_lo[v, 0, ms, :], from_lo[v, 1, ms, :]]
+                q += [xt[v, r, ms, :] for r in range(ROWS)]
+                q += [from_hi[v, 0, ms, :], from_hi[v, 1, ms, :]]
+                q1 = [
+                    step(q[i], q[i + 1], q[i - 1], pltpu.roll(halo[i - 1, vg], back, 1), i - 2)
+                    for i in range(1, ROWS + 3)
+                ]
+                for r in range(ROWS):
+                    xf[v, r, ms, :] = step(
+                        q1[r + 1], q1[r + 2], q1[r], pltpu.roll(halo1[r, vg], back, 1), r
+                    )
+
+    lane_m = lax.broadcasted_iota(jnp.int32, (MEMBERS, COLS), 1)
+    lat0 = me_lat * ROWS
+    lon0 = me_lon * COLS
+    for b in range(NB):
+
+        def pick(k, acc):
+            row = lat_ref[b * BLOCK + k] - lat0
+            col = lon_ref[b * BLOCK + k] - lon0
+            owned = (row >= 0) & (row < ROWS) & (col >= 0) & (col < COLS)
+            row = jnp.clip(row, 0, ROWS - 1)
+            t = xf[var_ref[b * BLOCK + k], row]
+            return jnp.where(
+                lane_m == jnp.where(owned, k, -1), pltpu.roll(t, (k - col) & (COLS - 1), 1), acc
+            )
+
+        part[b] = lax.fori_loop(
+            0, BLOCK, pick, jnp.zeros((MEMBERS, COLS), F32), unroll=8
+        )
+
+    first = [
+        remote(part.at[lat_peer(o)], got_a.at[o - 1], send.at[o - 1], recv_a.at[o - 1], o, 0)
+        for o in range(1, nlat)
+    ]
+    for c in first:
+        c.start()
+    total = part[me_lat]
+    for i, c in enumerate(first):
+        c.wait_recv()
+        total = total + got_a[i]
+    line[...] = total
+    second = [
+        remote(line, got_b.at[o - 1], send.at[nlat + o - 2], recv_b.at[o - 1], 0, o)
+        for o in range(1, nlon)
+    ]
+    for c in second:
+        c.start()
+    for i, c in enumerate(second):
+        c.wait_recv()
+        total = total + got_b[i]
+    block_sum[...] = total
+    third = [
+        remote(block_sum, out.at[me_lat], send.at[nlat + nlon + o - 3], recv_c.at[o - 1], o, 0)
+        for o in range(1, nlat)
+    ]
+    for c in third:
+        c.start()
+    out[me_lat] = total
+    for c in third:
+        c.wait_recv()
+    for c in winds + edges + corners + first + second + third:
+        c.wait_send()
+
+    @pl.loop(0, nvg)
+    def _(vg):
+        rows(vg, True).wait_send()
+        rows(vg, False).wait_send()
+
+
+def front(x, wind, lat, lon, var, nlat, nlon):
+    vm = pl.BlockSpec(memory_space=pltpu.VMEM)
+    sm = pl.BlockSpec(memory_space=pltpu.SMEM)
+    nvg = NVAR // VS
+    dma = pltpu.SemaphoreType.DMA
+    return pl.pallas_call(
+        lambda *refs: front_kernel(nlat, nlon, *refs),
+        out_shape=(
+            jax.ShapeDtypeStruct((NVAR, ROWS, MEMBERS, COLS), F32),
+            jax.ShapeDtypeStruct((NB, MEMBERS, BLOCK), F32),
+        ),
+        in_specs=[vm, vm, sm, sm, sm],
+        out_specs=(vm, vm),
+        scratch_shapes=[
+            pltpu.VMEM((NVAR, ROWS, MEMBERS, COLS), F32),
+            pltpu.VMEM((NVAR, 2, MEMBERS, COLS), F32),
+            pltpu.VMEM((NVAR, 2, MEMBERS, COLS), F32),
+            pltpu.VMEM((ROWS, nvg, 8, COLS), F32),
+            pltpu.VMEM((ROWS, nvg, 8, COLS), F32),
+            pltpu.VMEM((ROWS, nvg, 8, COLS), F32),
+            pltpu.VMEM((4, nvg, 8, COLS), F32),
+            pltpu.VMEM((4, 2, ROWS, COLS), F32),
+            pltpu.VMEM((ROWS + 2, nvg, 8, COLS), F32),
+            pltpu.VMEM((ROWS, nvg, 8, COLS), F32),
+            pltpu.VMEM((ROWS + 2, 4, 8, COLS), F32),
+            pltpu.VMEM((NB, MEMBERS, BLOCK), F32),
+            pltpu.VMEM((MEMBERS, BLOCK), F32),
+            pltpu.VMEM((MEMBERS, BLOCK), F32),
+            pltpu.VMEM((nlat - 1, MEMBERS, BLOCK), F32),
+            pltpu.VMEM((nlon - 1, MEMBERS, BLOCK), F32),
+            dma((nvg, 2)), dma((nvg, 2)), dma((2,)), dma((2,)), dma((4,)), dma((4,)),
+            dma((4,)), dma((4,)),
+            dma((2 * nlat + nlon - 3,)), dma((nlat - 1,)), dma((nlon - 1,)), dma((nlat - 1,)),
+        ],
+        compiler_params=pltpu.CompilerParams(
+            collective_id=0, has_side_effects=True, vmem_limit_bytes=40 << 20
+        ),
+        name="front",
+    )(x, wind, lat, lon, var)
 
 
 def taper_sq(d2):
@@ -141,9 +423,7 @@
     def _(g):
         for i in range(VG):
             for r in range(ROWS):
-                xv[i, :, r * COLS : (r + 1) * COLS] = x_ref[
-                    pl.ds((g * VG + i) * ROWS + r, MEMBERS, stride=NVAR * ROWS), :
-                ]
+                xv[i, :, r * COLS : (r + 1) * COLS] = x_ref[g * VG + i, r]
 
         @pl.loop(0, NB)
         def _(b):
@@ -198,89 +478,31 @@
     )(origin, x, y, lat, lon, val, err)
 
 
-def with_halo(block, sides, width):
-    for axis, dim in sides:
-        count = lax.axis_size(axis)
-        forward = [(i, i + 1) for i in range(count - 1)]
-        forward.append((count - 1, 0))
-        backward = [(target, source) for source, target in forward]
-        low = lax.ppermute(
-            lax.slice_in_dim(block, block.shape[dim] - width, None, axis=dim), axis, forward
-        )
-        high = lax.ppermute(lax.slice_in_dim(block, 0, width, axis=dim), axis, backward)
-        block = jnp.concatenate([low, block, high], axis=dim)
-    return block
-
-
-def advance(padded, east_wind, north_wind):
-    centre = padded[..., 1:-1, 1:-1]
-    above_v = padded[..., 2:, 1:-1]
-    below_v = padded[..., :-2, 1:-1]
-    right_v = padded[..., 1:-1, 2:]
-    left_v = padded[..., 1:-1, :-2]
-    return (
-        centre
-        - 0.5 * east_wind * (right_v - left_v)
-        - 0.5 * north_wind * (above_v - below_v)
-        + DIFFUSE * (right_v + left_v + above_v + below_v - 4.0 * centre)
-    )
-
-
-def zero_outside_block(padded, margin):
-    overall_line_count = padded.shape[-2]
-    band_rows = overall_line_count - 2 * margin
-    global_row = (
-        lax.axis_index("lat") * band_rows - margin + lax.iota(jnp.int32, overall_line_count)
-    )
-    inside = (global_row >= 0) & (global_row < band_rows * lax.axis_size("lat"))
-    return jnp.where(inside[:, None], padded, 0.0)
-
-
-def read_priors(sample_realizations, sel_lat, sel_lon, sel_var, band_rows, band_cols):
-    members, variables, cells = sample_realizations.shape
-    local_lat = sel_lat - lax.axis_index("lat") * band_rows
-    local_lon = sel_lon - lax.axis_index("lon") * band_cols
-    owned = (local_lat >= 0) & (local_lat < band_rows) & (local_lon >= 0) & (local_lon < band_cols)
-    position = (
-        sel_var * cells
-        + jnp.clip(local_lat, 0, band_rows - 1) * band_cols
-        + jnp.clip(local_lon, 0, band_cols - 1)
-    )
-    picked = jnp.take(sample_realizations.reshape(members, variables * cells), position, axis=1)
-    return jnp.where(owned[None, :], picked, 0.0)
-
-
-def body(prognostic_samples, wind, obs_lat, obs_lon, obs_var, obs_value, obs_error):
-    members, variables, band_rows, band_cols = prognostic_samples.shape
-    state_now = prognostic_samples
-    for section in range(STEPS):
-        padded = with_halo(state_now, (("lat", 2), ("lon", 3)), 1)
-        state_now = advance(zero_outside_block(padded, 1), wind[0], wind[1])
-    sample_realizations = state_now.reshape(members, variables, band_rows * band_cols)
-    own_part = read_priors(
-        sample_realizations,
-        obs_lat.reshape(-1),
-        obs_lon.reshape(-1),
-        obs_var.reshape(-1),
-        band_rows,
-        band_cols,
-    )
-    prior = lax.psum(own_part, ("lat", "lon"))
-    y = jnp.moveaxis(prior.reshape(members, NB, BLOCK), 1, 0)
-    origin = jnp.stack([lax.axis_index("lat") * band_rows, lax.axis_index("lon") * band_cols])
-    out = analysis(
-        origin.astype(jnp.int32),
-        state_now.reshape(members * variables * band_rows, band_cols),
-        y,
-        obs_lat.reshape(NB, BLOCK),
-        obs_lon.reshape(NB, BLOCK),
-        obs_value.reshape(NB, BLOCK),
-        obs_error.reshape(NB, BLOCK),
-    )
-    return out.reshape(members, variables, band_rows, band_cols)
-
-
 def solution(mesh):
+    nlat, nlon = mesh.shape["lat"], mesh.shape["lon"]
+
+    def body(prognostic_samples, wind, obs_lat, obs_lon, obs_var, obs_value, obs_error):
+        xf, y = front(
+            prognostic_samples.reshape(MEMBERS * NVAR * ROWS, COLS),
+            wind,
+            obs_lat.reshape(-1),
+            obs_lon.reshape(-1),
+            obs_var.reshape(-1),
+            nlat,
+            nlon,
+        )
+        origin = jnp.stack([lax.axis_index("lat") * ROWS, lax.axis_index("lon") * COLS])
+        out = analysis(
+            origin.astype(jnp.int32),
+            xf,
+            y,
+            obs_lat.reshape(NB, BLOCK),
+            obs_lon.reshape(NB, BLOCK),
+            obs_value.reshape(NB, BLOCK),
+            obs_error.reshape(NB, BLOCK),
+        )
+        return out.reshape(prognostic_samples.shape)
+
     in_specs = (P(None, None, "lat", "lon"), P(None, "lat", "lon"), P(), P(), P(), P(), P())
     out_specs = P(None, None, "lat", "lon")
     return jax.shard_map(body, mesh=mesh, in_specs=in_specs, out_specs=out_specs, check_vma=False)

time: 359 us -> 138 us (0.38)
  waiting for transfers between devices: 147 us -> 0 us
  Pallas kernels: 35.1 us -> 130 us
  local copies, waits for them, and re-layouts: 94.4 us -> 7.7 us
  other arithmetic: 52.4 us -> 0.07 us
  starting transfers between devices: 16.5 us -> 0 us
  between operations: 13.6 us -> 0.02 us
    psum x1 -> x0, waiting for transfers between devices: 138 us -> none  [body(): prior = lax.psum(own_part, ('lat', 'lon'))]
    pallas_call x0 -> x1, Pallas kernels: none -> 94.9 us  [front(): pl.pallas_call(lambda *refs: front_kernel(nlat, nlon, *refs), out_shape=(...]
    unnamed x27 -> x7, local copies, waits for them, and re-layouts: 28.7 us -> 4.92 us
    select_n x4 -> x0, other arithmetic: 23.4 us -> none  [the longest x2 23 us: zero_outside_block(): return jnp.where(inside[:, None], padded, 0.0)]
    add x3 -> x0, other arithmetic: 20.1 us -> none  [the longest x2 20.1 us: advance(): centre - 0.5 * east_wind * (right_v - left_v)]
    ppermute x6 -> x0, local copies, waits for them, and re-layouts: 18 us -> none  [the longest x3 9.46 us: with_halo(): lax.ppermute(lax.slice_in_dim(block, 0, width, axis=dim), axis, backward)]
    ppermute x8 -> x0, starting transfers between devices: 16.5 us -> none  [the longest x4 10.4 us: with_halo(): lax.ppermute(lax.slice_in_dim(block, 0, width, axis=dim), axis, backward)]
    concatenate x1 -> x0, local copies, waits for them, and re-layouts: 15.4 us -> none  [with_halo(): block = jnp.concatenate([low, block, high], axis=dim)]
  transfers between devices with their start and end apart: 9 -> 0, of which waited for: 3 -> 0; matrix products, arithmetic and copies ran while one was open for 12% -> 0% of each run, Pallas kernels for 0% -> 0%
where the time goes in v2:
time: 138 us; the launch traced here: 137 us
  Pallas kernels  130 us (94%)
  local copies, waits for them, and re-layouts  7.7 us (6%)
    pallas_call x1, Pallas kernels, front(): pl.pallas_call(lambda *refs: front_kernel(nlat, nlon, *refs), out_shape=(...  94.9 us
    pallas_call x1, Pallas kernels, analysis(): pl.pallas_call(analysis_kernel, out_shape=jax.ShapeDtypeStruct((MEMBERS *...  34.6 us
    unnamed x7, local copies, waits for them, and re-layouts  4.92 us

profile of v2, /device:TPU:1, one launch (start us, length us, event | category | flops | bytes accessed | tf_op | source)
XLA Modules:
  0.0 137.3 jit_solution(5055079476665497510)
XLA Ops:
  0.0 0.1 pad_add_fusion.orig_ref
  0.1 0.7 copy.10
  0.8 0.7 reshape.33.val_ref
  1.5 0.7 reshape.34.err_ref
  2.2 0.7 copy.9
  2.8 0.7 copy.8
  3.5 0.7 reshape.31.lat_ref
  4.2 0.7 reshape.32.lon_ref
  4.9 0.0 copy-start
  4.9 2.2 %copy-done = f32[40,25,8,128]{3,2,1,0:T(8,128)S(1)} copy-done((f32[40,25,8,128]{3,2,1,0:T(8,128)S(1)}, f32[40,25,8,128]{3,2,1,0:T(8,128)}, u32[]{:S(2)}) %copy-start) | copy-done | bytes 4096024
  7.1 0.0 copy-start.1
  7.1 0.7 copy-done.1
  7.8 94.9 %front.1 = (f32[25,8,40,128]{3,2,1,0:T(8,128)S(1)}, f32[8,40,128]{2,1,0:T(8,128)S(1)}) custom-call(f32[8000,128]{1,0:T(8,128)S(1)} %bitcast.10, f32[2,8,128]{2,1,0:T(8,128)S(1)} %copy-done.1, s32[1024]{0:T(1024)S(1)} %bitcast.13, s32[1024]{0:T(1024)S(1)} %bitcast.12, s32[1024]{0:T(1024)S(1)} %bitcast.11), custom_call_target="tpu_custom_call" | custom-call | tf_op jit(solution)/shard_map/front/pallas_call | solution.py:266
  102.7 34.6 %analysis.1 = f32[8000,128]{1,0:T(8,128)} custom-call(s32[2]{0:T(128)S(1)} %pad_add_fusion.orig_ref, f32[25,8,40,128]{3,2,1,0:T(8,128)S(1)} %get-tuple-element.7.x_ref, f32[8,40,128]{2,1,0:T(8,128)S(1)} %get-tuple-element.8.y_ref, s32[8,128]{1,0:T(8,128)S(1)} %reshape.31.lat_ref, s32[8,128]{1,0:T(8,128)S(1)} %reshape.32.lon_ref, ...), custom_call_target="tpu_custom_call" | custom-call | tf_op jit(solution)/shard_map/analysis/pallas_call | solution.py:459
Async XLA Ops:
  4.9 2.2 %copy-start = (f32[40,25,8,128]{3,2,1,0:T(8,128)S(1)}, f32[40,25,8,128]{3,2,1,0:T(8,128)}, u32[]{:S(2)}) copy-start(f32[40,25,8,128]{3,2,1,0:T(8,128)} %param.7) | copy-start | bytes 12288004
  7.1 0.7 copy-start.1

commit v3 on v1

--- a/solution.py
+++ b/solution.py
@@ -7,14 +7,417 @@
 
 MEMBERS, NVAR, ROWS, COLS = 40, 25, 8, 128
 NLON = 2048
+GROUPS, OBS = 2, 512
 NB, BLOCK = 8, 128
+PER = OBS // BLOCK
 LOC = 32.0
+DIFFUSE = 0.1
+VS = 5
+NVG = NVAR // VS
+MG = MEMBERS // 8
 KC = 32
 NCH = BLOCK // KC
 VG = 5
 F32, BF = jnp.float32, jnp.bfloat16
-STEPS = 2
-DIFFUSE = 0.1
+MESH = pl.DeviceIdType.MESH
+
+
+def hi(x):
+    return x.astype(BF).astype(F32)
+
+
+def split(x):
+    high = x.astype(BF)
+    return high, (x - high.astype(F32)).astype(BF)
+
+
+def dot(a, b, dims=((1,), (0,))):
+    return lax.dot_general(a, b, (dims, ((), ())), preferred_element_type=F32)
+
+
+def peers(nlat, nlon):
+    me_lat = lax.axis_index("lat")
+    me_lon = lax.axis_index("lon")
+
+    def place(dlat, dlon):
+        lat = lax.rem(me_lat + (dlat + nlat), nlat) if dlat else me_lat
+        lon = lax.rem(me_lon + (dlon + nlon), nlon) if dlon else me_lon
+        return lat, lon
+
+    def remote(src, dst, ssem, rsem, dlat, dlon):
+        return pltpu.make_async_remote_copy(
+            src_ref=src,
+            dst_ref=dst,
+            send_sem=ssem,
+            recv_sem=rsem,
+            device_id=place(dlat, dlon),
+            device_id_type=MESH,
+        )
+
+    def signal(barrier, offsets):
+        for o in offsets:
+            pl.semaphore_signal(barrier, inc=1, device_id=place(*o), device_id_type=MESH)
+
+    return me_lat, me_lon, place, remote, signal
+
+
+def forecast_kernel(
+    nlat, nlon,
+    x_ref, wind_ref, lat_ref, lon_ref, var_ref,
+    xf, desc,
+    xt, edge, edge_w, edge_e, corner, wind_n, halo, halo_s, halo1_s, coef, shift, q1_s,
+    s_row, r_row, s_edge, r_edge, s_corner, r_corner, s_wind, r_wind,
+):
+    me_lat, me_lon, place, remote, signal = peers(nlat, nlon)
+    barrier = pltpu.get_barrier_semaphore()
+    near = [(a, b) for a in (-1, 0, 1) for b in (-1, 0, 1) if a or b]
+    signal(barrier, near)
+
+    def column(r, mg, v):
+        return x_ref[pl.ds(mg * (8 * NVAR * ROWS) + v * ROWS + r, 8, stride=NVAR * ROWS), :]
+
+    @pl.loop(0, NVAR)
+    def _(v):
+        for r in (0, 1, ROWS - 2, ROWS - 1):
+            for mg in range(MG):
+                xt[v, r + 2, mg * 8 : (mg + 1) * 8, :] = column(r, mg, v)
+
+    def rows(vg, up):
+        vs = pl.ds(vg * VS, VS)
+        if up:
+            return remote(
+                xt.at[vs, 2:4],
+                xt.at[vs, ROWS + 2 : ROWS + 4],
+                s_row.at[vg, 0], r_row.at[vg, 0], -1, 0,
+            )
+        return remote(
+            xt.at[vs, ROWS : ROWS + 2], xt.at[vs, 0:2], s_row.at[vg, 1], r_row.at[vg, 1], 1, 0
+        )
+
+    winds = [
+        remote(wind_ref, wind_n.at[i], s_wind.at[i], r_wind.at[i], dlat, dlon)
+        for i, (dlat, dlon) in enumerate([(1, 0), (-1, 0), (0, 1), (0, -1)])
+    ]
+    edges = [
+        remote(edge, edge_w, s_edge.at[0], r_edge.at[0], 0, 1),
+        remote(edge, edge_e, s_edge.at[1], r_edge.at[1], 0, -1),
+    ]
+    corners = [
+        remote(edge.at[ROWS - 1], corner.at[0], s_corner.at[0], r_corner.at[0], 1, 1),
+        remote(edge.at[ROWS - 1], corner.at[1], s_corner.at[1], r_corner.at[1], 1, -1),
+        remote(edge.at[0], corner.at[2], s_corner.at[2], r_corner.at[2], -1, 1),
+        remote(edge.at[0], corner.at[3], s_corner.at[3], r_corner.at[3], -1, -1),
+    ]
+    pl.semaphore_wait(barrier, len(near))
+    for w in winds:
+        w.start()
+    for vg in range(NVG):
+        rows(vg, True).start()
+        rows(vg, False).start()
+
+    lane = lax.broadcasted_iota(jnp.int32, (8, COLS), 1)
+    edge[...] = jnp.zeros_like(edge)
+
+    @pl.loop(0, NVAR)
+    def _(v):
+        mine = ((lane - 4 * v + 2) & (COLS - 1)) < 4
+        for r in range(ROWS):
+            for mg in range(MG):
+                ms = slice(mg * 8, (mg + 1) * 8)
+                if 2 <= r < ROWS - 2:
+                    t = column(r, mg, v)
+                    xt[v, r + 2, ms, :] = t
+                else:
+                    t = xt[v, r + 2, ms, :]
+                edge[r, ms, :] = jnp.where(mine, pltpu.roll(t, 4 * v, 1), edge[r, ms, :])
+
+    for e in edges + corners:
+        e.start()
+
+    row = lat_ref[...] - me_lat * ROWS
+    col = lon_ref[...] - me_lon * COLS
+    owned = (row >= 0) & (row < ROWS) & (col >= 0) & (col < COLS)
+    desc[...] = jnp.where(owned, (var_ref[...] * ROWS + row) * COLS + col, -1)
+
+    src = lax.rem(lax.broadcasted_iota(jnp.int32, (2 * COLS, 2 * COLS), 0), COLS)
+    dst = lax.broadcasted_iota(jnp.int32, (2 * COLS, 2 * COLS), 1)
+    east_of = (dst < COLS) & (src == dst + 1)
+    west_of = (dst >= COLS) & (src == dst - COLS - 1)
+    shift[...] = jnp.where(east_of | west_of, 1.0, 0.0).astype(BF)
+
+    for w in winds:
+        w.wait_recv()
+    has_lo = (me_lat > 0).astype(F32)
+    has_hi = (me_lat < nlat - 1).astype(F32)
+
+    def row_wind(r):
+        if r < 0:
+            return wind_n[0, 0, ROWS - 1 : ROWS, :], wind_n[0, 1, ROWS - 1 : ROWS, :]
+        if r == ROWS:
+            return wind_n[1, 0, 0:1, :], wind_n[1, 1, 0:1, :]
+        return wind_ref[0, r : r + 1, :], wind_ref[1, r : r + 1, :]
+
+    def four(u, v, r):
+        nxt, prv = DIFFUSE - 0.5 * v, DIFFUSE + 0.5 * v
+        if r == 0:
+            prv = prv * has_lo
+        if r == ROWS - 1:
+            nxt = nxt * has_hi
+        return DIFFUSE - 0.5 * u, DIFFUSE + 0.5 * u, nxt, prv
+
+    for r in range(-1, ROWS + 1):
+        u, v = row_wind(r)
+        for i, c in enumerate(four(u, v, r)):
+            coef[i, r + 1] = jnp.broadcast_to(c, (8, COLS))
+
+    for e in edges + corners:
+        e.wait_recv()
+    lane4 = lax.rem(lax.broadcasted_iota(jnp.int32, (MEMBERS, COLS), 1), 4)
+    from_west = lane4 >= 2
+    halo[0] = jnp.where(from_west, corner[0], corner[1])
+    halo[ROWS + 1] = jnp.where(from_west, corner[2], corner[3])
+    for r in range(ROWS):
+        halo[r + 1] = jnp.where(from_west, edge_w[r], edge_e[r])
+    for r in range(ROWS + 2):
+        high, low = split(halo[r])
+        halo_s[r] = jnp.concatenate([high, low], axis=1)
+    for r in range(ROWS):
+        u, v = [
+            jnp.where(
+                from_west,
+                jnp.broadcast_to(wind_n[2, i, r : r + 1, COLS - 1 : COLS], (MEMBERS, COLS)),
+                jnp.broadcast_to(wind_n[3, i, r : r + 1, 0:1], (MEMBERS, COLS)),
+            )
+            for i in range(2)
+        ]
+        ce, cw, cn, cs = four(u, v, r)
+        own, got = edge[r], halo[r + 1]
+        east = pltpu.roll(jnp.where(lane4 == 0, own, got), COLS - 1, 1)
+        west = pltpu.roll(jnp.where(lane4 == 3, own, got), 1, 1)
+        after = (
+            (1.0 - 4.0 * DIFFUSE) * got
+            + ce * east
+            + cw * west
+            + cn * halo[r + 2]
+            + cs * halo[r]
+        )
+        high, low = split(after)
+        halo1_s[r] = jnp.concatenate([high, low], axis=1)
+
+    def step(q, nxt, prv, side, place_side, first, count):
+        shape = (count, MG, 8, COLS)
+        high, low = split(q)
+        both = dot(jnp.concatenate([high, low], axis=1), shift[...]) + dot(
+            side.reshape(count * MEMBERS, 2 * COLS), place_side
+        )
+        c = [coef[i, first : first + count].reshape(count, 1, 8, COLS) for i in range(4)]
+        new = (
+            (1.0 - 4.0 * DIFFUSE) * q.reshape(shape)
+            + c[0] * both[:, :COLS].reshape(shape)
+            + c[1] * both[:, COLS:].reshape(shape)
+            + c[2] * nxt.reshape(shape)
+            + c[3] * prv.reshape(shape)
+        )
+        return new.reshape(count * MEMBERS, COLS)
+
+    def place_side(v):
+        at_end = (dst == COLS - 1) & (src == 4 * v)
+        at_start = (dst == COLS) & (src == ((4 * v - 1) & (COLS - 1)))
+        return jnp.where(at_end | at_start, 1.0, 0.0).astype(BF)
+
+    def block(ref, v, first, count):
+        return ref[v, first : first + count].reshape(count * MEMBERS, COLS)
+
+    @pl.loop(0, NVG)
+    def _(vg):
+        rows(vg, True).wait_recv()
+        rows(vg, False).wait_recv()
+        n1, n2 = ROWS + 2, ROWS
+        for vi in range(VS):
+            v = vg * VS + vi
+            q1_s[vi] = step(
+                block(xt, v, 1, n1), block(xt, v, 2, n1), block(xt, v, 0, n1),
+                halo_s[...], place_side(v), 0, n1,
+            ).reshape(n1, MEMBERS, COLS)
+        for vi in range(VS):
+            v = vg * VS + vi
+            xf[v] = step(
+                block(q1_s, vi, 1, n2), block(q1_s, vi, 2, n2), block(q1_s, vi, 0, n2),
+                halo1_s[...], place_side(v), 1, n2,
+            ).reshape(n2, MEMBERS, COLS)
+
+    for c in winds + edges + corners:
+        c.wait_send()
+
+    @pl.loop(0, NVG)
+    def _(vg):
+        rows(vg, True).wait_send()
+        rows(vg, False).wait_send()
+
+
+def forecast(x, wind, lat, lon, var, nlat, nlon):
+    vm = pl.BlockSpec(memory_space=pltpu.VMEM)
+    dma = pltpu.SemaphoreType.DMA
+    return pl.pallas_call(
+        lambda *refs: forecast_kernel(nlat, nlon, *refs),
+        out_shape=(
+            jax.ShapeDtypeStruct((NVAR, ROWS, MEMBERS, COLS), F32),
+            jax.ShapeDtypeStruct((GROUPS, OBS), jnp.int32),
+        ),
+        in_specs=[vm] * 5,
+        out_specs=(vm, vm),
+        scratch_shapes=[
+            pltpu.VMEM((NVAR, ROWS + 4, MEMBERS, COLS), F32),
+            pltpu.VMEM((ROWS, MEMBERS, COLS), F32),
+            pltpu.VMEM((ROWS, MEMBERS, COLS), F32),
+            pltpu.VMEM((ROWS, MEMBERS, COLS), F32),
+            pltpu.VMEM((4, MEMBERS, COLS), F32),
+            pltpu.VMEM((4, 2, ROWS, COLS), F32),
+            pltpu.VMEM((ROWS + 2, MEMBERS, COLS), F32),
+            pltpu.VMEM((ROWS + 2, MEMBERS, 2 * COLS), BF),
+            pltpu.VMEM((ROWS, MEMBERS, 2 * COLS), BF),
+            pltpu.VMEM((4, ROWS + 2, 8, COLS), F32),
+            pltpu.VMEM((2 * COLS, 2 * COLS), BF),
+            pltpu.VMEM((VS, ROWS + 2, MEMBERS, COLS), F32),
+            dma((NVG, 2)), dma((NVG, 2)), dma((2,)), dma((2,)),
+            dma((4,)), dma((4,)), dma((4,)), dma((4,)),
+        ],
+        compiler_params=pltpu.CompilerParams(
+            collective_id=0, has_side_effects=True, vmem_limit_bytes=40 << 20
+        ),
+        name="forecast",
+    )(x, wind, lat, lon, var)
+
+
+def pick_kernel(desc, xf, part):
+    part[...] = jnp.zeros_like(part)
+    lane = lax.broadcasted_iota(jnp.int32, (MEMBERS, COLS), 1)
+    width = 8
+
+    @pl.loop(0, GROUPS * OBS // width)
+    def _(g):
+        batch, first = g // (OBS // width), lax.rem(g, OBS // width) * width
+        d = [desc[batch, first + j] for j in range(width)]
+        top = d[0]
+        for j in range(1, width):
+            top = jnp.maximum(top, d[j])
+
+        @pl.when(top >= 0)
+        def _():
+            for j in range(width):
+
+                @pl.when(d[j] >= 0)
+                def _(j=j):
+                    k = lax.rem(g, BLOCK // width) * width + j
+                    b = g // (BLOCK // width)
+                    col = d[j] & (COLS - 1)
+                    t = xf[lax.shift_right_logical(d[j], 7)]
+                    part[b] = jnp.where(
+                        lane == k, pltpu.roll(t, (k - col) & (COLS - 1), 1), part[b]
+                    )
+
+
+def pick(desc, xf):
+    vm = pl.BlockSpec(memory_space=pltpu.VMEM)
+    return pl.pallas_call(
+        pick_kernel,
+        out_shape=jax.ShapeDtypeStruct((NB, MEMBERS, BLOCK), F32),
+        in_specs=[pl.BlockSpec(memory_space=pltpu.SMEM), vm],
+        out_specs=vm,
+        compiler_params=pltpu.CompilerParams(vmem_limit_bytes=16 << 20),
+        name="pick",
+    )(desc, xf)
+
+
+def total_kernel(nlat, nlon, part, out, part_b, line, got_a, got_b, send, recv_a, recv_b, recv_c):
+    me_lat = lax.axis_index("lat")
+    me_lon = lax.axis_index("lon")
+
+    def lat_peer(o):
+        return lax.rem(me_lat + o, nlat)
+
+    def lon_peer(o):
+        return lax.rem(me_lon + o, nlon)
+
+    barrier = pltpu.get_barrier_semaphore()
+    for o in range(1, nlat):
+        pl.semaphore_signal(barrier, inc=1, device_id=(lat_peer(o), me_lon), device_id_type=MESH)
+    for o in range(1, nlon):
+        pl.semaphore_signal(barrier, inc=1, device_id=(me_lat, lon_peer(o)), device_id_type=MESH)
+    pl.semaphore_wait(barrier, nlat + nlon - 2)
+
+    first = []
+    for o in range(1, nlat):
+        copy = pltpu.make_async_remote_copy(
+            src_ref=part.at[lat_peer(o)],
+            dst_ref=got_a.at[o - 1],
+            send_sem=send.at[o - 1],
+            recv_sem=recv_a.at[o - 1],
+            device_id=(lat_peer(o), me_lon),
+            device_id_type=MESH,
+        )
+        copy.start()
+        first.append(copy)
+    total = part[me_lat]
+    for copy, o in zip(first, range(1, nlat)):
+        copy.wait_recv()
+        total = total + got_a[o - 1]
+    line[...] = total
+    second = []
+    for o in range(1, nlon):
+        copy = pltpu.make_async_remote_copy(
+            src_ref=line,
+            dst_ref=got_b.at[o - 1],
+            send_sem=send.at[nlat + o - 2],
+            recv_sem=recv_b.at[o - 1],
+            device_id=(me_lat, lon_peer(o)),
+            device_id_type=MESH,
+        )
+        copy.start()
+        second.append(copy)
+    for copy, o in zip(second, range(1, nlon)):
+        copy.wait_recv()
+        total = total + got_b[o - 1]
+    part_b[...] = total
+    third = []
+    for o in range(1, nlat):
+        copy = pltpu.make_async_remote_copy(
+            src_ref=part_b,
+            dst_ref=out.at[me_lat],
+            send_sem=send.at[nlat + nlon + o - 3],
+            recv_sem=recv_c.at[o - 1],
+            device_id=(lat_peer(o), me_lon),
+            device_id_type=MESH,
+        )
+        copy.start()
+        third.append(copy)
+    out[me_lat] = total
+    for copy in third:
+        copy.wait_recv()
+    for copy in first + second + third:
+        copy.wait_send()
+
+
+def total_over_devices(part, nlat, nlon):
+    vm = pl.BlockSpec(memory_space=pltpu.VMEM)
+    return pl.pallas_call(
+        lambda *refs: total_kernel(nlat, nlon, *refs),
+        out_shape=jax.ShapeDtypeStruct(part.shape, F32),
+        in_specs=[vm],
+        out_specs=vm,
+        scratch_shapes=[
+            pltpu.VMEM((MEMBERS, BLOCK), F32),
+            pltpu.VMEM((MEMBERS, BLOCK), F32),
+            pltpu.VMEM((nlat - 1, MEMBERS, BLOCK), F32),
+            pltpu.VMEM((nlon - 1, MEMBERS, BLOCK), F32),
+            pltpu.SemaphoreType.DMA((2 * nlat + nlon - 3,)),
+            pltpu.SemaphoreType.DMA((nlat - 1,)),
+            pltpu.SemaphoreType.DMA((nlon - 1,)),
+            pltpu.SemaphoreType.DMA((nlat - 1,)),
+        ],
+        compiler_params=pltpu.CompilerParams(collective_id=1, has_side_effects=True),
+        name="total_over_devices",
+    )(part)
 
 
 def taper_sq(d2):
@@ -28,23 +431,22 @@
     return jnp.where(z <= 1.0, inner, jnp.where(z < 2.0, outer, 0.0))
 
 
-def hi(x):
-    return x.astype(BF).astype(F32)
-
-
-def dot(a, b, dims=((1,), (0,))):
-    return lax.dot_general(a, b, (dims, ((), ())), preferred_element_type=F32)
-
-
 def analysis_kernel(
-    orig_ref, x_ref, y_ref, lat_ref, lon_ref, val_ref, err_ref,
+    x_ref, y_ref, lat_ref, lon_ref, val_ref, err_ref,
     out_ref,
     ys, a_all, s_all, a_pk, b_pk, t_pk, xv, rhs, q3, nch,
 ):
-    lat0 = orig_ref[0]
-    lon0 = orig_ref[1]
-    lat = lat_ref[...].astype(F32)
-    lon = lon_ref[...].astype(F32)
+    lat0 = lax.axis_index("lat") * ROWS
+    lon0 = lax.axis_index("lon") * COLS
+
+    def by_block(ref):
+        rows = [ref[b // PER : b // PER + 1, (b % PER) * BLOCK : (b % PER + 1) * BLOCK] for b in range(NB)]
+        return jnp.concatenate(rows, axis=0)
+
+    lat = by_block(lat_ref).astype(F32)
+    lon = by_block(lon_ref).astype(F32)
+    values = by_block(val_ref)
+    variances = by_block(err_ref)
     lat_t = lat.T
     lon_t = lon.T
     lat0f = lat0.astype(F32)
@@ -73,10 +475,10 @@
         average = jnp.sum(prior, axis=0, keepdims=True) * (1.0 / MEMBERS)
         anomaly = prior - average
         spread = jnp.sum(anomaly * anomaly, axis=0, keepdims=True) / (MEMBERS - 1)
-        errors = err_ref[b : b + 1, :]
+        errors = variances[b : b + 1, :]
         total = spread + errors
         weights = anomaly * (1.0 / ((MEMBERS - 1) * total))
-        shifts = (val_ref[b : b + 1, :] - average) - anomaly * (
+        shifts = (values[b : b + 1, :] - average) - anomaly * (
             1.0 / (1.0 + jnp.sqrt(errors / total))
         )
         wh = hi(weights)
@@ -141,9 +543,7 @@
     def _(g):
         for i in range(VG):
             for r in range(ROWS):
-                xv[i, :, r * COLS : (r + 1) * COLS] = x_ref[
-                    pl.ds((g * VG + i) * ROWS + r, MEMBERS, stride=NVAR * ROWS), :
-                ]
+                xv[i, :, r * COLS : (r + 1) * COLS] = x_ref[g * VG + i, r]
 
         @pl.loop(0, NB)
         def _(b):
@@ -174,12 +574,12 @@
                 ] = xv[i, :, r * COLS : (r + 1) * COLS]
 
 
-def analysis(origin, x, y, lat, lon, val, err):
+def analysis(x, y, lat, lon, val, err):
     vm = pl.BlockSpec(memory_space=pltpu.VMEM)
     return pl.pallas_call(
         analysis_kernel,
         out_shape=jax.ShapeDtypeStruct((MEMBERS * NVAR * ROWS, COLS), F32),
-        in_specs=[pl.BlockSpec(memory_space=pltpu.SMEM)] + [vm] * 6,
+        in_specs=[vm] * 6,
         out_specs=vm,
         scratch_shapes=[
             pltpu.VMEM((MEMBERS, NB * BLOCK), F32),
@@ -195,92 +595,22 @@
         ],
         compiler_params=pltpu.CompilerParams(vmem_limit_bytes=40 << 20),
         name="analysis",
-    )(origin, x, y, lat, lon, val, err)
-
-
-def with_halo(block, sides, width):
-    for axis, dim in sides:
-        count = lax.axis_size(axis)
-        forward = [(i, i + 1) for i in range(count - 1)]
-        forward.append((count - 1, 0))
-        backward = [(target, source) for source, target in forward]
-        low = lax.ppermute(
-            lax.slice_in_dim(block, block.shape[dim] - width, None, axis=dim), axis, forward
-        )
-        high = lax.ppermute(lax.slice_in_dim(block, 0, width, axis=dim), axis, backward)
-        block = jnp.concatenate([low, block, high], axis=dim)
-    return block
-
-
-def advance(padded, east_wind, north_wind):
-    centre = padded[..., 1:-1, 1:-1]
-    above_v = padded[..., 2:, 1:-1]
-    below_v = padded[..., :-2, 1:-1]
-    right_v = padded[..., 1:-1, 2:]
-    left_v = padded[..., 1:-1, :-2]
-    return (
-        centre
-        - 0.5 * east_wind * (right_v - left_v)
-        - 0.5 * north_wind * (above_v - below_v)
-        + DIFFUSE * (right_v + left_v + above_v + below_v - 4.0 * centre)
-    )
-
-
-def zero_outside_block(padded, margin):
-    overall_line_count = padded.shape[-2]
-    band_rows = overall_line_count - 2 * margin
-    global_row = (
-        lax.axis_index("lat") * band_rows - margin + lax.iota(jnp.int32, overall_line_count)
-    )
-    inside = (global_row >= 0) & (global_row < band_rows * lax.axis_size("lat"))
-    return jnp.where(inside[:, None], padded, 0.0)
-
-
-def read_priors(sample_realizations, sel_lat, sel_lon, sel_var, band_rows, band_cols):
-    members, variables, cells = sample_realizations.shape
-    local_lat = sel_lat - lax.axis_index("lat") * band_rows
-    local_lon = sel_lon - lax.axis_index("lon") * band_cols
-    owned = (local_lat >= 0) & (local_lat < band_rows) & (local_lon >= 0) & (local_lon < band_cols)
-    position = (
-        sel_var * cells
-        + jnp.clip(local_lat, 0, band_rows - 1) * band_cols
-        + jnp.clip(local_lon, 0, band_cols - 1)
-    )
-    picked = jnp.take(sample_realizations.reshape(members, variables * cells), position, axis=1)
-    return jnp.where(owned[None, :], picked, 0.0)
-
-
-def body(prognostic_samples, wind, obs_lat, obs_lon, obs_var, obs_value, obs_error):
-    members, variables, band_rows, band_cols = prognostic_samples.shape
-    state_now = prognostic_samples
-    for section in range(STEPS):
-        padded = with_halo(state_now, (("lat", 2), ("lon", 3)), 1)
-        state_now = advance(zero_outside_block(padded, 1), wind[0], wind[1])
-    sample_realizations = state_now.reshape(members, variables, band_rows * band_cols)
-    own_part = read_priors(
-        sample_realizations,
-        obs_lat.reshape(-1),
-        obs_lon.reshape(-1),
-        obs_var.reshape(-1),
-        band_rows,
-        band_cols,
-    )
-    prior = lax.psum(own_part, ("lat", "lon"))
-    y = jnp.moveaxis(prior.reshape(members, NB, BLOCK), 1, 0)
-    origin = jnp.stack([lax.axis_index("lat") * band_rows, lax.axis_index("lon") * band_cols])
-    out = analysis(
-        origin.astype(jnp.int32),
-        state_now.reshape(members * variables * band_rows, band_cols),
-        y,
-        obs_lat.reshape(NB, BLOCK),
-        obs_lon.reshape(NB, BLOCK),
-        obs_value.reshape(NB, BLOCK),
-        obs_error.reshape(NB, BLOCK),
-    )
-    return out.reshape(members, variables, band_rows, band_cols)
+    )(x, y, lat, lon, val, err)
 
 
 def solution(mesh):
+    nlat, nlon = mesh.shape["lat"], mesh.shape["lon"]
+
+    def body(prognostic_samples, wind, obs_lat, obs_lon, obs_var, obs_value, obs_error):
+        xf, desc = forecast(
+            prognostic_samples.reshape(MEMBERS * NVAR * ROWS, COLS),
+            wind, obs_lat, obs_lon, obs_var, nlat, nlon,
+        )
+        part = pick(desc, xf.reshape(NVAR * ROWS, MEMBERS, COLS))
+        y = total_over_devices(part, nlat, nlon)
+        out = analysis(xf, y, obs_lat, obs_lon, obs_value, obs_error)
+        return out.reshape(prognostic_samples.shape)
+
     in_specs = (P(None, None, "lat", "lon"), P(None, "lat", "lon"), P(), P(), P(), P(), P())
     out_specs = P(None, None, "lat", "lon")
     return jax.shard_map(body, mesh=mesh, in_specs=in_specs, out_specs=out_specs, check_vma=False)

time: 359 us -> 102 us (0.28)
  waiting for transfers between devices: 147 us -> 0 us
  local copies, waits for them, and re-layouts: 94.4 us -> 10.6 us
  Pallas kernels: 35.1 us -> 90.9 us
  other arithmetic: 52.4 us -> 0 us
  starting transfers between devices: 16.5 us -> 0 us
  between operations: 13.6 us -> 0.09 us
    psum x1 -> x0, waiting for transfers between devices: 138 us -> none  [body(): prior = lax.psum(own_part, ('lat', 'lon'))]
    pallas_call x0 -> x3, Pallas kernels: none -> 56.9 us  [the longest x1 28.5 us: forecast(): pl.pallas_call(lambda *refs: forecast_kernel(nlat, nlon, *refs), out_shap...]
    select_n x4 -> x0, other arithmetic: 23.4 us -> none  [the longest x2 23 us: zero_outside_block(): return jnp.where(inside[:, None], padded, 0.0)]
    add x3 -> x0, other arithmetic: 20.1 us -> none  [the longest x2 20.1 us: advance(): centre - 0.5 * east_wind * (right_v - left_v)]
    unnamed x27 -> x26, local copies, waits for them, and re-layouts: 28.7 us -> 10.6 us
    ppermute x6 -> x0, local copies, waits for them, and re-layouts: 18 us -> none  [the longest x3 9.46 us: with_halo(): lax.ppermute(lax.slice_in_dim(block, 0, width, axis=dim), axis, backward)]
    ppermute x8 -> x0, starting transfers between devices: 16.5 us -> none  [the longest x4 10.4 us: with_halo(): lax.ppermute(lax.slice_in_dim(block, 0, width, axis=dim), axis, backward)]
    concatenate x1 -> x0, local copies, waits for them, and re-layouts: 15.4 us -> none  [with_halo(): block = jnp.concatenate([low, block, high], axis=dim)]
  transfers between devices with their start and end apart: 9 -> 0, of which waited for: 3 -> 0; matrix products, arithmetic and copies ran while one was open for 12% -> 0% of each run, Pallas kernels for 0% -> 0%
where the time goes in v3:
time: 102 us
  Pallas kernels  90.9 us (89%)
  local copies, waits for them, and re-layouts  10.6 us (10%)
    pallas_call x1, Pallas kernels, analysis(): pl.pallas_call(analysis_kernel, out_shape=jax.ShapeDtypeStruct((MEMBERS *...  34 us
    pallas_call x1, Pallas kernels, forecast(): pl.pallas_call(lambda *refs: forecast_kernel(nlat, nlon, *refs), out_shap...  28.5 us
    pallas_call x1, Pallas kernels, total_over_devices(): pl.pallas_call(lambda *refs: total_kernel(nlat, nlon, *refs), out_shape=j...  22.3 us
    unnamed x26, local copies, waits for them, and re-layouts  10.6 us
    pallas_call x1, Pallas kernels, pick(): pl.pallas_call(pick_kernel, out_shape=jax.ShapeDtypeStruct((NB, MEMBERS,...  6.09 us

profile of v3, /device:TPU:1, one launch (start us, length us, event | category | flops | bytes accessed | tf_op | source)
XLA Modules:
  0.0 101.6 jit_solution(11734735545923374020)
XLA Ops:
  0.0 0.0 copy-start.2
  0.0 2.2 %copy-done.2 = f32[40,25,8,128]{3,2,1,0:T(8,128)S(1)} copy-done((f32[40,25,8,128]{3,2,1,0:T(8,128)S(1)}, f32[40,25,8,128]{3,2,1,0:T(8,128)}, u32[]{:S(2)}) %copy-start.2) | copy-done | bytes 4096024
  2.2 0.0 copy-start.5
  2.2 0.7 copy-done.5
  2.8 0.0 copy-start.7
  2.9 0.7 copy-done.7
  3.5 0.0 copy-start.9
  3.5 0.7 copy-done.9
  4.2 0.0 copy-start.10
  4.2 0.7 copy-done.10
  4.9 0.0 copy-start.6
  4.9 0.0 copy-start.8
  4.9 0.0 copy-start.11
  4.9 0.0 copy-start.12
  4.9 28.5 %forecast.1 = (f32[25,8,40,128]{3,2,1,0:T(8,128)S(1)}, s32[2,512]{1,0:T(2,128)S(1)}) custom-call(f32[8000,128]{1,0:T(8,128)S(1)} %bitcast.4, f32[2,8,128]{2,1,0:T(8,128)S(1)} %copy-done.9, s32[2,512]{1,0:T(2,128)S(1)} %copy-done.5, s32[2,512]{1,0:T(2,128)S(1)} %copy-done.7, s32[2,512]{1,0:T(2,128)S(1)} %copy-done.10), custom_call_target="tpu_custom_call" | custom-call | tf_op jit(solution)/shard_map/forecast/pallas_call | solution.py:261
  33.4 6.1 %pick.1.refs_0_ = f32[8,40,128]{2,1,0:T(8,128)S(1)} custom-call(s32[2,512]{1,0:T(2,128)S(1)} %get-tuple-element.8.desc, f32[200,40,128]{2,1,0:T(8,128)S(1)} %bitcast.3), custom_call_target="tpu_custom_call" | custom-call | tf_op jit(solution)/shard_map/pick/pallas_call | solution.py:322
  39.5 0.0 copy-start
  39.5 2.0 %copy-done = f32[25,8,40,128]{3,2,1,0:T(8,128)} copy-done((f32[25,8,40,128]{3,2,1,0:T(8,128)}, f32[25,8,40,128]{3,2,1,0:T(8,128)S(1)}, u32[]{:S(2)}) %copy-start) | copy-done | bytes 4096024
  41.5 0.0 copy-start.3
  41.5 0.7 copy-done.3
  42.1 22.3 %total_over_devices.1.y_ref = f32[8,40,128]{2,1,0:T(8,128)} custom-call(f32[8,40,128]{2,1,0:T(8,128)} %copy-done.3), custom_call_target="tpu_custom_call" | custom-call | tf_op jit(solution)/shard_map/total_over_devices/pallas_call | solution.py:403
  64.5 0.0 copy-done.6
  64.5 0.0 copy-done.8
  64.5 0.0 copy-done.11
  64.5 0.0 copy-done.12
  64.5 0.0 copy-start.1
  64.5 2.2 %copy-done.1 = f32[25,8,40,128]{3,2,1,0:T(8,128)S(1)} copy-done((f32[25,8,40,128]{3,2,1,0:T(8,128)S(1)}, f32[25,8,40,128]{3,2,1,0:T(8,128)}, u32[]{:S(2)}) %copy-start.1) | copy-done | bytes 4096024
  66.7 0.0 copy-start.4
  66.7 0.9 copy-done.4
  67.6 34.0 %analysis.1 = f32[8000,128]{1,0:T(8,128)} custom-call(f32[25,8,40,128]{3,2,1,0:T(8,128)S(1)} %copy-done.1, f32[8,40,128]{2,1,0:T(8,128)S(1)} %copy-done.4, s32[2,512]{1,0:T(2,128)S(1)} %copy-done.6, s32[2,512]{1,0:T(2,128)S(1)} %copy-done.8, f32[2,512]{1,0:T(2,128)S(1)} %copy-done.11, f32[2,512]{1,0:T(2,128)S(1)} %copy-done.12), custom_call_target="tpu_custom_call" | custom-call | tf_op jit(solution)/shard_map/analysis/pallas_call | solution.py:579
Async XLA Ops:
  0.0 2.2 %copy-start.2 = (f32[40,25,8,128]{3,2,1,0:T(8,128)S(1)}, f32[40,25,8,128]{3,2,1,0:T(8,128)}, u32[]{:S(2)}) copy-start(f32[40,25,8,128]{3,2,1,0:T(8,128)} %param.7) | copy-start | bytes 12288004
  2.2 0.7 copy-start.5
  2.8 0.7 copy-start.7
  3.5 0.7 copy-start.9
  4.2 0.7 copy-start.10
  4.9 59.6 %copy-start.6 = (s32[2,512]{1,0:T(2,128)S(1)}, s32[2,512]{1,0:T(2,128)}, u32[]{:S(2)}) copy-start(s32[2,512]{1,0:T(2,128)} %lat_ref.1) | copy-start | bytes 12292
  4.9 59.6 %copy-start.8 = (s32[2,512]{1,0:T(2,128)S(1)}, s32[2,512]{1,0:T(2,128)}, u32[]{:S(2)}) copy-start(s32[2,512]{1,0:T(2,128)} %lon_ref.1) | copy-start | bytes 12292
  4.9 59.6 %copy-start.11 = (f32[2,512]{1,0:T(2,128)S(1)}, f32[2,512]{1,0:T(2,128)}, u32[]{:S(2)}) copy-start(f32[2,512]{1,0:T(2,128)} %val_ref.1) | copy-start | bytes 12292
  4.9 59.6 %copy-start.12 = (f32[2,512]{1,0:T(2,128)S(1)}, f32[2,512]{1,0:T(2,128)}, u32[]{:S(2)}) copy-start(f32[2,512]{1,0:T(2,128)} %err_ref.1) | copy-start | bytes 12292
  39.5 2.0 %copy-start = (f32[25,8,40,128]{3,2,1,0:T(8,128)}, f32[25,8,40,128]{3,2,1,0:T(8,128)S(1)}, u32[]{:S(2)}) copy-start(f32[25,8,40,128]{3,2,1,0:T(8,128)S(1)} %get-tuple-element.7.x_ref) | copy-start | bytes 12288004
  41.5 0.7 copy-start.3
  64.5 2.2 %copy-start.1 = (f32[25,8,40,128]{3,2,1,0:T(8,128)S(1)}, f32[25,8,40,128]{3,2,1,0:T(8,128)}, u32[]{:S(2)}) copy-start(f32[25,8,40,128]{3,2,1,0:T(8,128)} %copy-done) | copy-start | bytes 12288004
  66.7 0.9 copy-start.4

commit v4 on v3

--- a/solution.py
+++ b/solution.py
@@ -63,24 +63,36 @@
 
 def forecast_kernel(
     nlat, nlon,
-    x_ref, wind_ref, lat_ref, lon_ref, var_ref,
-    xf, desc,
-    xt, edge, edge_w, edge_e, corner, wind_n, halo, halo_s, halo1_s, coef, shift, q1_s,
+    x_hbm, wind_hbm, lat_hbm, lon_hbm, var_hbm,
+    xf, out,
+    xb, wind_ref, lat_ref, lon_ref, var_ref, desc, desc_s, xft, yo, part, line, block_sum, got_a, got_b,
+    xt, edge, edge_w, edge_e, corner, wind_n, halo, halo_s, halo1_s, coef, shift, unit, q1_s,
     s_row, r_row, s_edge, r_edge, s_corner, r_corner, s_wind, r_wind,
+    send, recv_a, recv_b, recv_c, l_x, l_small,
 ):
+    def fetch(vg):
+        vs = pl.ds(vg * VS, VS)
+        return pltpu.make_async_copy(x_hbm.at[:, vs], xb.at[:, vs], l_x.at[vg])
+
+    small = [
+        pltpu.make_async_copy(a, b, l_small.at[i])
+        for i, (a, b) in enumerate(
+            [(wind_hbm, wind_ref), (lat_hbm, lat_ref), (lon_hbm, lon_ref), (var_hbm, var_ref)]
+        )
+    ]
+    for vg in range(NVG):
+        fetch(vg).start()
+    for c in small:
+        c.start()
+    x_ref = xb.reshape(MEMBERS * NVAR * ROWS, COLS)
     me_lat, me_lon, place, remote, signal = peers(nlat, nlon)
     barrier = pltpu.get_barrier_semaphore()
-    near = [(a, b) for a in (-1, 0, 1) for b in (-1, 0, 1) if a or b]
+    near = [(o, 0) for o in range(1, nlat)] + [(0, o) for o in range(1, nlon)]
+    near += [(-1, -1), (-1, 1), (1, -1), (1, 1)]
     signal(barrier, near)
 
     def column(r, mg, v):
         return x_ref[pl.ds(mg * (8 * NVAR * ROWS) + v * ROWS + r, 8, stride=NVAR * ROWS), :]
-
-    @pl.loop(0, NVAR)
-    def _(v):
-        for r in (0, 1, ROWS - 2, ROWS - 1):
-            for mg in range(MG):
-                xt[v, r + 2, mg * 8 : (mg + 1) * 8, :] = column(r, mg, v)
 
     def rows(vg, up):
         vs = pl.ds(vg * VS, VS)
@@ -108,10 +120,21 @@
         remote(edge.at[0], corner.at[2], s_corner.at[2], r_corner.at[2], -1, 1),
         remote(edge.at[0], corner.at[3], s_corner.at[3], r_corner.at[3], -1, -1),
     ]
-    pl.semaphore_wait(barrier, len(near))
-    for w in winds:
-        w.start()
     for vg in range(NVG):
+        fetch(vg).wait()
+
+        @pl.loop(vg * VS, (vg + 1) * VS)
+        def _(v):
+            for r in (0, 1, ROWS - 2, ROWS - 1):
+                for mg in range(MG):
+                    xt[v, r + 2, mg * 8 : (mg + 1) * 8, :] = column(r, mg, v)
+
+        if vg == 0:
+            for c in small:
+                c.wait()
+            pl.semaphore_wait(barrier, len(near))
+            for w in winds:
+                w.start()
         rows(vg, True).start()
         rows(vg, False).start()
 
@@ -134,16 +157,20 @@
     for e in edges + corners:
         e.start()
 
-    row = lat_ref[...] - me_lat * ROWS
-    col = lon_ref[...] - me_lon * COLS
-    owned = (row >= 0) & (row < ROWS) & (col >= 0) & (col < COLS)
-    desc[...] = jnp.where(owned, (var_ref[...] * ROWS + row) * COLS + col, -1)
+    lat_all, lon_all = lat_ref[...], lon_ref[...]
+    owned = (lat_all // ROWS == me_lat) & (lon_all // COLS == me_lon)
+    desc[...] = (var_ref[...] * ROWS + (lat_all & (ROWS - 1))) * COLS + (lon_all & (COLS - 1))
+    to_scalar = pltpu.make_async_copy(desc, desc_s, l_small.at[4])
+    to_scalar.start()
 
     src = lax.rem(lax.broadcasted_iota(jnp.int32, (2 * COLS, 2 * COLS), 0), COLS)
     dst = lax.broadcasted_iota(jnp.int32, (2 * COLS, 2 * COLS), 1)
     east_of = (dst < COLS) & (src == dst + 1)
     west_of = (dst >= COLS) & (src == dst - COLS - 1)
     shift[...] = jnp.where(east_of | west_of, 1.0, 0.0).astype(BF)
+    col_of = lax.rem(lax.broadcasted_iota(jnp.int32, (COLS, 2 * COLS), 1), COLS)
+    row_of = lax.broadcasted_iota(jnp.int32, (COLS, 2 * COLS), 0)
+    unit[...] = jnp.where(col_of == row_of, 1.0, 0.0).astype(BF)
 
     for w in winds:
         w.wait_recv()
@@ -241,12 +268,64 @@
             ).reshape(n1, MEMBERS, COLS)
         for vi in range(VS):
             v = vg * VS + vi
-            xf[v] = step(
+            new = step(
                 block(q1_s, vi, 1, n2), block(q1_s, vi, 2, n2), block(q1_s, vi, 0, n2),
                 halo1_s[...], place_side(v), 1, n2,
-            ).reshape(n2, MEMBERS, COLS)
-
-    for c in winds + edges + corners:
+            )
+            xf[v] = new.reshape(n2, MEMBERS, COLS)
+            high, low = split(new)
+            both = jnp.concatenate([high, low], axis=1)
+            for r in range(ROWS):
+                xft[pl.ds((v * ROWS + r) * COLS, COLS), 0:MEMBERS] = dot(
+                    unit[...], both[r * MEMBERS : (r + 1) * MEMBERS, :], ((1,), (1,))
+                )
+
+    to_scalar.wait()
+    for b in range(NB):
+
+        @pl.loop(0, BLOCK // 8)
+        def _(g):
+            for j in range(8):
+                k = g * 8 + j
+                at = desc_s[b // PER, (b % PER) * BLOCK + k]
+                yo[b, pl.ds(k, 1), :] = xft[pl.ds(at, 1), :]
+
+    for b in range(NB):
+        mine = owned[b // PER : b // PER + 1, (b % PER) * BLOCK : (b % PER + 1) * BLOCK]
+        part[b] = jnp.where(mine, yo[b].T[0:MEMBERS, :], 0.0)
+
+    first = [
+        remote(part.at[place(o, 0)[0]], got_a.at[o - 1], send.at[o - 1], recv_a.at[o - 1], o, 0)
+        for o in range(1, nlat)
+    ]
+    for c in first:
+        c.start()
+    total = part[me_lat]
+    for i, c in enumerate(first):
+        c.wait_recv()
+        total = total + got_a[i]
+    line[...] = total
+    second = [
+        remote(line, got_b.at[o - 1], send.at[nlat + o - 2], recv_b.at[o - 1], 0, o)
+        for o in range(1, nlon)
+    ]
+    for c in second:
+        c.start()
+    for i, c in enumerate(second):
+        c.wait_recv()
+        total = total + got_b[i]
+    block_sum[...] = total
+    third = [
+        remote(block_sum, out.at[me_lat], send.at[nlat + nlon + o - 3], recv_c.at[o - 1], o, 0)
+        for o in range(1, nlat)
+    ]
+    for c in third:
+        c.start()
+    out[me_lat] = total
+    for c in third:
+        c.wait_recv()
+
+    for c in winds + edges + corners + first + second + third:
         c.wait_send()
 
     @pl.loop(0, NVG)
@@ -262,11 +341,25 @@
         lambda *refs: forecast_kernel(nlat, nlon, *refs),
         out_shape=(
             jax.ShapeDtypeStruct((NVAR, ROWS, MEMBERS, COLS), F32),
-            jax.ShapeDtypeStruct((GROUPS, OBS), jnp.int32),
+            jax.ShapeDtypeStruct((NB, MEMBERS, BLOCK), F32),
         ),
-        in_specs=[vm] * 5,
+        in_specs=[pl.BlockSpec(memory_space=pltpu.HBM)] * 5,
         out_specs=(vm, vm),
         scratch_shapes=[
+            pltpu.VMEM((MEMBERS, NVAR, ROWS, COLS), F32),
+            pltpu.VMEM((2, ROWS, COLS), F32),
+            pltpu.VMEM((GROUPS, OBS), jnp.int32),
+            pltpu.VMEM((GROUPS, OBS), jnp.int32),
+            pltpu.VMEM((GROUPS, OBS), jnp.int32),
+            pltpu.VMEM((GROUPS, OBS), jnp.int32),
+            pltpu.SMEM((GROUPS, OBS), jnp.int32),
+            pltpu.VMEM((NVAR * ROWS * COLS, COLS), F32),
+            pltpu.VMEM((NB, BLOCK, COLS), F32),
+            pltpu.VMEM((NB, MEMBERS, BLOCK), F32),
+            pltpu.VMEM((MEMBERS, BLOCK), F32),
+            pltpu.VMEM((MEMBERS, BLOCK), F32),
+            pltpu.VMEM((nlat - 1, MEMBERS, BLOCK), F32),
+            pltpu.VMEM((nlon - 1, MEMBERS, BLOCK), F32),
             pltpu.VMEM((NVAR, ROWS + 4, MEMBERS, COLS), F32),
             pltpu.VMEM((ROWS, MEMBERS, COLS), F32),
             pltpu.VMEM((ROWS, MEMBERS, COLS), F32),
@@ -278,146 +371,18 @@
             pltpu.VMEM((ROWS, MEMBERS, 2 * COLS), BF),
             pltpu.VMEM((4, ROWS + 2, 8, COLS), F32),
             pltpu.VMEM((2 * COLS, 2 * COLS), BF),
+            pltpu.VMEM((COLS, 2 * COLS), BF),
             pltpu.VMEM((VS, ROWS + 2, MEMBERS, COLS), F32),
             dma((NVG, 2)), dma((NVG, 2)), dma((2,)), dma((2,)),
             dma((4,)), dma((4,)), dma((4,)), dma((4,)),
+            dma((2 * nlat + nlon - 3,)), dma((nlat - 1,)), dma((nlon - 1,)), dma((nlat - 1,)),
+            dma((NVG,)), dma((5,)),
         ],
         compiler_params=pltpu.CompilerParams(
-            collective_id=0, has_side_effects=True, vmem_limit_bytes=40 << 20
+            collective_id=0, has_side_effects=True, vmem_limit_bytes=34 << 20
         ),
         name="forecast",
     )(x, wind, lat, lon, var)
-
-
-def pick_kernel(desc, xf, part):
-    part[...] = jnp.zeros_like(part)
-    lane = lax.broadcasted_iota(jnp.int32, (MEMBERS, COLS), 1)
-    width = 8
-
-    @pl.loop(0, GROUPS * OBS // width)
-    def _(g):
-        batch, first = g // (OBS // width), lax.rem(g, OBS // width) * width
-        d = [desc[batch, first + j] for j in range(width)]
-        top = d[0]
-        for j in range(1, width):
-            top = jnp.maximum(top, d[j])
-
-        @pl.when(top >= 0)
-        def _():
-            for j in range(width):
-
-                @pl.when(d[j] >= 0)
-                def _(j=j):
-                    k = lax.rem(g, BLOCK // width) * width + j
-                    b = g // (BLOCK // width)
-                    col = d[j] & (COLS - 1)
-                    t = xf[lax.shift_right_logical(d[j], 7)]
-                    part[b] = jnp.where(
-                        lane == k, pltpu.roll(t, (k - col) & (COLS - 1), 1), part[b]
-                    )
-
-
-def pick(desc, xf):
-    vm = pl.BlockSpec(memory_space=pltpu.VMEM)
-    return pl.pallas_call(
-        pick_kernel,
-        out_shape=jax.ShapeDtypeStruct((NB, MEMBERS, BLOCK), F32),
-        in_specs=[pl.BlockSpec(memory_space=pltpu.SMEM), vm],
-        out_specs=vm,
-        compiler_params=pltpu.CompilerParams(vmem_limit_bytes=16 << 20),
-        name="pick",
-    )(desc, xf)
-
-
-def total_kernel(nlat, nlon, part, out, part_b, line, got_a, got_b, send, recv_a, recv_b, recv_c):
-    me_lat = lax.axis_index("lat")
-    me_lon = lax.axis_index("lon")
-
-    def lat_peer(o):
-        return lax.rem(me_lat + o, nlat)
-
-    def lon_peer(o):
-        return lax.rem(me_lon + o, nlon)
-
-    barrier = pltpu.get_barrier_semaphore()
-    for o in range(1, nlat):
-        pl.semaphore_signal(barrier, inc=1, device_id=(lat_peer(o), me_lon), device_id_type=MESH)
-    for o in range(1, nlon):
-        pl.semaphore_signal(barrier, inc=1, device_id=(me_lat, lon_peer(o)), device_id_type=MESH)
-    pl.semaphore_wait(barrier, nlat + nlon - 2)
-
-    first = []
-    for o in range(1, nlat):
-        copy = pltpu.make_async_remote_copy(
-            src_ref=part.at[lat_peer(o)],
-            dst_ref=got_a.at[o - 1],
-            send_sem=send.at[o - 1],
-            recv_sem=recv_a.at[o - 1],
-            device_id=(lat_peer(o), me_lon),
-            device_id_type=MESH,
-        )
-        copy.start()
-        first.append(copy)
-    total = part[me_lat]
-    for copy, o in zip(first, range(1, nlat)):
-        copy.wait_recv()
-        total = total + got_a[o - 1]
-    line[...] = total
-    second = []
-    for o in range(1, nlon):
-        copy = pltpu.make_async_remote_copy(
-            src_ref=line,
-            dst_ref=got_b.at[o - 1],
-            send_sem=send.at[nlat + o - 2],
-            recv_sem=recv_b.at[o - 1],
-            device_id=(me_lat, lon_peer(o)),
-            device_id_type=MESH,
-        )
-        copy.start()
-        second.append(copy)
-    for copy, o in zip(second, range(1, nlon)):
-        copy.wait_recv()
-        total = total + got_b[o - 1]
-    part_b[...] = total
-    third = []
-    for o in range(1, nlat):
-        copy = pltpu.make_async_remote_copy(
-            src_ref=part_b,
-            dst_ref=out.at[me_lat],
-            send_sem=send.at[nlat + nlon + o - 3],
-            recv_sem=recv_c.at[o - 1],
-            device_id=(lat_peer(o), me_lon),
-            device_id_type=MESH,
-        )
-        copy.start()
-        third.append(copy)
-    out[me_lat] = total
-    for copy in third:
-        copy.wait_recv()
-    for copy in first + second + third:
-        copy.wait_send()
-
-
-def total_over_devices(part, nlat, nlon):
-    vm = pl.BlockSpec(memory_space=pltpu.VMEM)
-    return pl.pallas_call(
-        lambda *refs: total_kernel(nlat, nlon, *refs),
-        out_shape=jax.ShapeDtypeStruct(part.shape, F32),
-        in_specs=[vm],
-        out_specs=vm,
-        scratch_shapes=[
-            pltpu.VMEM((MEMBERS, BLOCK), F32),
-            pltpu.VMEM((MEMBERS, BLOCK), F32),
-            pltpu.VMEM((nlat - 1, MEMBERS, BLOCK), F32),
-            pltpu.VMEM((nlon - 1, MEMBERS, BLOCK), F32),
-            pltpu.SemaphoreType.DMA((2 * nlat + nlon - 3,)),
-            pltpu.SemaphoreType.DMA((nlat - 1,)),
-            pltpu.SemaphoreType.DMA((nlon - 1,)),
-            pltpu.SemaphoreType.DMA((nlat - 1,)),
-        ],
-        compiler_params=pltpu.CompilerParams(collective_id=1, has_side_effects=True),
-        name="total_over_devices",
-    )(part)
 
 
 def taper_sq(d2):
@@ -593,7 +558,7 @@
             pltpu.VMEM((VG, 3 * KC, ROWS * COLS), BF),
             pltpu.SMEM((NB,), jnp.int32),
         ],
-        compiler_params=pltpu.CompilerParams(vmem_limit_bytes=40 << 20),
+        compiler_params=pltpu.CompilerParams(vmem_limit_bytes=16 << 20),
         name="analysis",
     )(x, y, lat, lon, val, err)
 
@@ -602,12 +567,9 @@
     nlat, nlon = mesh.shape["lat"], mesh.shape["lon"]
 
     def body(prognostic_samples, wind, obs_lat, obs_lon, obs_var, obs_value, obs_error):
-        xf, desc = forecast(
-            prognostic_samples.reshape(MEMBERS * NVAR * ROWS, COLS),
-            wind, obs_lat, obs_lon, obs_var, nlat, nlon,
-        )
-        part = pick(desc, xf.reshape(NVAR * ROWS, MEMBERS, COLS))
-        y = total_over_devices(part, nlat, nlon)
+        xf, y = forecast(
+            prognostic_samples, wind, obs_lat, obs_lon, obs_var, nlat, nlon
+        )
         out = analysis(xf, y, obs_lat, obs_lon, obs_value, obs_error)
         return out.reshape(prognostic_samples.shape)
 

time: 102 us -> 96.2 us (0.943)
  local copies, waits for them, and re-layouts: 10.6 us -> 4.92 us
    pallas_call x1, Pallas kernels: 28.5 us -> 56.9 us  [forecast(): pl.pallas_call(lambda *refs: forecast_kernel(nlat, nlon, *refs), out_shap...]
    pallas_call x2 -> x0, Pallas kernels: 28.4 us -> none  [the longest x1 22.3 us: total_over_devices(): pl.pallas_call(lambda *refs: total_kernel(nlat, nlon, *refs), out_shape=j...]
    unnamed x26 -> x14, local copies, waits for them, and re-layouts: 10.6 us -> 4.92 us
where the time goes in v4:
time: 96.2 us; the launch traced here: 95.9 us
  Pallas kernels  90.9 us (94%)
  local copies, waits for them, and re-layouts  4.92 us (5%)
    pallas_call x1, Pallas kernels, forecast(): pl.pallas_call(lambda *refs: forecast_kernel(nlat, nlon, *refs), out_shap...  56.9 us
    pallas_call x1, Pallas kernels, analysis(): pl.pallas_call(analysis_kernel, out_shape=jax.ShapeDtypeStruct((MEMBERS *...  34.1 us
    unnamed x14, local copies, waits for them, and re-layouts  4.92 us

profile of v4, /device:TPU:1, one launch (start us, length us, event | category | flops | bytes accessed | tf_op | source)
XLA Modules:
  0.0 95.9 jit_solution(1104949834892354980)
XLA Ops:
  0.0 0.0 copy-start
  0.0 2.2 %copy-done = f32[40,25,8,128]{3,2,1,0:T(8,128)S(1)} copy-done((f32[40,25,8,128]{3,2,1,0:T(8,128)S(1)}, f32[40,25,8,128]{3,2,1,0:T(8,128)}, u32[]{:S(2)}) %copy-start) | copy-done | bytes 4096024
  2.2 0.0 copy-start.1
  2.2 0.7 copy-done.1
  2.8 0.0 copy-start.2
  2.9 0.7 copy-done.2
  3.5 0.0 copy-start.3
  3.5 0.7 copy-done.3
  4.2 0.0 copy-start.4
  4.2 0.7 copy-done.4
  4.9 0.0 copy-start.5
  4.9 0.0 copy-start.6
  4.9 56.9 %forecast.1 = (f32[25,8,40,128]{3,2,1,0:T(8,128)S(1)}, f32[8,40,128]{2,1,0:T(8,128)S(1)}) custom-call(f32[40,25,8,128]{3,2,1,0:T(8,128)S(1)} %copy-done, f32[2,8,128]{2,1,0:T(8,128)S(1)} %copy-done.3, s32[2,512]{1,0:T(2,128)S(1)} %copy-done.1, s32[2,512]{1,0:T(2,128)S(1)} %copy-done.2, s32[2,512]{1,0:T(2,128)S(1)} %copy-done.4), custom_call_target="tpu_custom_call" | custom-call | tf_op jit(solution)/shard_map/forecast/pallas_call | solution.py:340
  61.8 0.0 copy-done.5
  61.8 0.0 copy-done.6
  61.8 34.1 %analysis.1 = f32[8000,128]{1,0:T(8,128)} custom-call(f32[25,8,40,128]{3,2,1,0:T(8,128)S(1)} %get-tuple-element.7.x_ref, f32[8,40,128]{2,1,0:T(8,128)S(1)} %get-tuple-element.8.y_ref, s32[2,512]{1,0:T(2,128)S(1)} %copy-done.1, s32[2,512]{1,0:T(2,128)S(1)} %copy-done.2, f32[2,512]{1,0:T(2,128)S(1)} %copy-done.5, f32[2,512]{1,0:T(2,128)S(1)} %copy-done.6), custom_call_target="tpu_custom_call" | custom-call | tf_op jit(solution)/shard_map/analysis/pallas_call | solution.py:544
Async XLA Ops:
  0.0 2.2 %copy-start = (f32[40,25,8,128]{3,2,1,0:T(8,128)S(1)}, f32[40,25,8,128]{3,2,1,0:T(8,128)}, u32[]{:S(2)}) copy-start(f32[40,25,8,128]{3,2,1,0:T(8,128)} %refs_0_.1) | copy-start | bytes 12288004
  2.2 0.7 copy-start.1
  2.8 0.7 copy-start.2
  3.5 0.7 copy-start.3
  4.2 0.7 copy-start.4
  4.9 56.9 %copy-start.5 = (f32[2,512]{1,0:T(2,128)S(1)}, f32[2,512]{1,0:T(2,128)}, u32[]{:S(2)}) copy-start(f32[2,512]{1,0:T(2,128)} %val_ref.1) | copy-start | bytes 12292
  4.9 56.9 %copy-start.6 = (f32[2,512]{1,0:T(2,128)S(1)}, f32[2,512]{1,0:T(2,128)}, u32[]{:S(2)}) copy-start(f32[2,512]{1,0:T(2,128)} %err_ref.1) | copy-start | bytes 12292

commit v5 on v4

--- a/solution.py
+++ b/solution.py
@@ -15,6 +15,7 @@
 VS = 5
 NVG = NVAR // VS
 MG = MEMBERS // 8
+SIDE = (ROWS + 2) // 3
 KC = 32
 NCH = BLOCK // KC
 VG = 5
@@ -106,6 +107,14 @@
             xt.at[vs, ROWS : ROWS + 2], xt.at[vs, 0:2], s_row.at[vg, 1], r_row.at[vg, 1], 1, 0
         )
 
+    def send_rows(vg):
+        rows(vg, True).start()
+        rows(vg, False).start()
+
+    def sent_rows(vg):
+        rows(vg, True).wait_send()
+        rows(vg, False).wait_send()
+
     winds = [
         remote(wind_ref, wind_n.at[i], s_wind.at[i], r_wind.at[i], dlat, dlon)
         for i, (dlat, dlon) in enumerate([(1, 0), (-1, 0), (0, 1), (0, -1)])
@@ -135,8 +144,8 @@
             pl.semaphore_wait(barrier, len(near))
             for w in winds:
                 w.start()
-        rows(vg, True).start()
-        rows(vg, False).start()
+        if vg < 2:
+            send_rows(vg)
 
     lane = lax.broadcasted_iota(jnp.int32, (8, COLS), 1)
     edge[...] = jnp.zeros_like(edge)
@@ -156,10 +165,15 @@
 
     for e in edges + corners:
         e.start()
+    sent_rows(0)
+    send_rows(2)
 
     lat_all, lon_all = lat_ref[...], lon_ref[...]
     owned = (lat_all // ROWS == me_lat) & (lon_all // COLS == me_lon)
-    desc[...] = (var_ref[...] * ROWS + (lat_all & (ROWS - 1))) * COLS + (lon_all & (COLS - 1))
+    row_all = lat_all & (ROWS - 1)
+    group = (row_all >= 3).astype(jnp.int32) + (row_all >= 6).astype(jnp.int32)
+    part_of = row_all - 3 * group
+    desc[...] = (var_ref[...] * SIDE + group) * COLS + (lon_all & (COLS - 1))
     to_scalar = pltpu.make_async_copy(desc, desc_s, l_small.at[4])
     to_scalar.start()
 
@@ -196,6 +210,9 @@
         u, v = row_wind(r)
         for i, c in enumerate(four(u, v, r)):
             coef[i, r + 1] = jnp.broadcast_to(c, (8, COLS))
+
+    sent_rows(1)
+    send_rows(3)
 
     for e in edges + corners:
         e.wait_recv()
@@ -259,6 +276,12 @@
     def _(vg):
         rows(vg, True).wait_recv()
         rows(vg, False).wait_recv()
+
+        @pl.when(vg == 0)
+        def _():
+            sent_rows(2)
+            send_rows(4)
+
         n1, n2 = ROWS + 2, ROWS
         for vi in range(VS):
             v = vg * VS + vi
@@ -275,9 +298,10 @@
             xf[v] = new.reshape(n2, MEMBERS, COLS)
             high, low = split(new)
             both = jnp.concatenate([high, low], axis=1)
-            for r in range(ROWS):
-                xft[pl.ds((v * ROWS + r) * COLS, COLS), 0:MEMBERS] = dot(
-                    unit[...], both[r * MEMBERS : (r + 1) * MEMBERS, :], ((1,), (1,))
+            for i in range(SIDE):
+                n = min(3, ROWS - 3 * i) * MEMBERS
+                xft[pl.ds((v * SIDE + i) * COLS, COLS), 0:n] = dot(
+                    unit[...], both[i * 3 * MEMBERS : i * 3 * MEMBERS + n, :], ((1,), (1,))
                 )
 
     to_scalar.wait()
@@ -291,8 +315,13 @@
                 yo[b, pl.ds(k, 1), :] = xft[pl.ds(at, 1), :]
 
     for b in range(NB):
-        mine = owned[b // PER : b // PER + 1, (b % PER) * BLOCK : (b % PER + 1) * BLOCK]
-        part[b] = jnp.where(mine, yo[b].T[0:MEMBERS, :], 0.0)
+        cut = (slice(b // PER, b // PER + 1), slice((b % PER) * BLOCK, (b % PER + 1) * BLOCK))
+        turned = yo[b].T
+        at = jnp.broadcast_to(jnp.where(owned[cut], part_of[cut], -1), (MEMBERS, BLOCK))
+        mine = jnp.zeros((MEMBERS, BLOCK), F32)
+        for i in range(3):
+            mine = jnp.where(at == i, turned[i * MEMBERS : (i + 1) * MEMBERS, :], mine)
+        part[b] = mine
 
     first = [
         remote(part.at[place(o, 0)[0]], got_a.at[o - 1], send.at[o - 1], recv_a.at[o - 1], o, 0)
@@ -328,10 +357,8 @@
     for c in winds + edges + corners + first + second + third:
         c.wait_send()
 
-    @pl.loop(0, NVG)
-    def _(vg):
-        rows(vg, True).wait_send()
-        rows(vg, False).wait_send()
+    sent_rows(3)
+    sent_rows(4)
 
 
 def forecast(x, wind, lat, lon, var, nlat, nlon):
@@ -353,7 +380,7 @@
             pltpu.VMEM((GROUPS, OBS), jnp.int32),
             pltpu.VMEM((GROUPS, OBS), jnp.int32),
             pltpu.SMEM((GROUPS, OBS), jnp.int32),
-            pltpu.VMEM((NVAR * ROWS * COLS, COLS), F32),
+            pltpu.VMEM((NVAR * SIDE * COLS, COLS), F32),
             pltpu.VMEM((NB, BLOCK, COLS), F32),
             pltpu.VMEM((NB, MEMBERS, BLOCK), F32),
             pltpu.VMEM((MEMBERS, BLOCK), F32),
@@ -567,9 +594,11 @@
     nlat, nlon = mesh.shape["lat"], mesh.shape["lon"]
 
     def body(prognostic_samples, wind, obs_lat, obs_lon, obs_var, obs_value, obs_error):
-        xf, y = forecast(
-            prognostic_samples, wind, obs_lat, obs_lon, obs_var, nlat, nlon
-        )
+        args = [
+            pltpu.with_memory_space_constraint(a, pltpu.HBM)
+            for a in (prognostic_samples, wind, obs_lat, obs_lon, obs_var)
+        ]
+        xf, y = forecast(*args, nlat, nlon)
         out = analysis(xf, y, obs_lat, obs_lon, obs_value, obs_error)
         return out.reshape(prognostic_samples.shape)
 

time: 96.2 us -> 83.7 us (0.87)
  Pallas kernels: 90.9 us -> 83.5 us
  local copies, waits for them, and re-layouts: 4.92 us -> 0.02 us
    pallas_call x1, Pallas kernels: 56.9 us -> 49.5 us  [forecast(): pl.pallas_call(lambda *refs: forecast_kernel(nlat, nlon, *refs), out_shap...]
    unnamed x14 -> x8, local copies, waits for them, and re-layouts: 4.92 us -> 0.02 us
where the time goes in v5:
time: 83.7 us; the launch traced here: 83.6 us
  Pallas kernels  83.5 us (100%)
    pallas_call x1, Pallas kernels, forecast(): pl.pallas_call(lambda *refs: forecast_kernel(nlat, nlon, *refs), out_shap...  49.5 us
    pallas_call x1, Pallas kernels, analysis(): pl.pallas_call(analysis_kernel, out_shape=jax.ShapeDtypeStruct((MEMBERS *...  34 us

profile of v5, /device:TPU:1, one launch (start us, length us, event | category | flops | bytes accessed | tf_op | source)
XLA Modules:
  0.0 83.6 jit_solution(2987663739244993171)
XLA Ops:
  0.0 0.0 copy-start.1
  0.0 0.0 copy-start
  0.0 0.0 copy-start.3
  0.0 0.0 copy-start.2
  0.0 49.5 %forecast.1 = (f32[25,8,40,128]{3,2,1,0:T(8,128)S(1)}, f32[8,40,128]{2,1,0:T(8,128)S(1)}) custom-call(f32[40,25,8,128]{3,2,1,0:T(8,128)} %refs_0_.1, f32[2,8,128]{2,1,0:T(8,128)} %refs_1_.1, s32[2,512]{1,0:T(2,128)} %lat_ref.1, s32[2,512]{1,0:T(2,128)} %lon_ref.1, s32[2,512]{1,0:T(2,128)} %refs_4_.1), custom_call_target="tpu_custom_call" | custom-call | tf_op jit(solution)/shard_map/forecast/pallas_call | solution.py:367
  49.5 0.0 copy-done.1
  49.5 0.0 copy-done
  49.5 0.0 copy-done.3
  49.6 0.0 copy-done.2
  49.6 34.0 %analysis.1 = f32[8000,128]{1,0:T(8,128)} custom-call(f32[25,8,40,128]{3,2,1,0:T(8,128)S(1)} %get-tuple-element.7.x_ref, f32[8,40,128]{2,1,0:T(8,128)S(1)} %get-tuple-element.8.y_ref, s32[2,512]{1,0:T(2,128)S(1)} %copy-done, s32[2,512]{1,0:T(2,128)S(1)} %copy-done.1, f32[2,512]{1,0:T(2,128)S(1)} %copy-done.2, f32[2,512]{1,0:T(2,128)S(1)} %copy-done.3), custom_call_target="tpu_custom_call" | custom-call | tf_op jit(solution)/shard_map/analysis/pallas_call | solution.py:571
Async XLA Ops:
  0.0 49.5 %copy-start.1 = (s32[2,512]{1,0:T(2,128)S(1)}, s32[2,512]{1,0:T(2,128)}, u32[]{:S(2)}) copy-start(s32[2,512]{1,0:T(2,128)} %lon_ref.1) | copy-start | bytes 12292
  0.0 49.5 %copy-start = (s32[2,512]{1,0:T(2,128)S(1)}, s32[2,512]{1,0:T(2,128)}, u32[]{:S(2)}) copy-start(s32[2,512]{1,0:T(2,128)} %lat_ref.1) | copy-start | bytes 12292
  0.0 49.5 %copy-start.3 = (f32[2,512]{1,0:T(2,128)S(1)}, f32[2,512]{1,0:T(2,128)}, u32[]{:S(2)}) copy-start(f32[2,512]{1,0:T(2,128)} %err_ref.1) | copy-start | bytes 12292
  0.0 49.6 %copy-start.2 = (f32[2,512]{1,0:T(2,128)S(1)}, f32[2,512]{1,0:T(2,128)}, u32[]{:S(2)}) copy-start(f32[2,512]{1,0:T(2,128)} %val_ref.1) | copy-start | bytes 12292

commit v6 on v5

--- a/solution.py
+++ b/solution.py
@@ -62,10 +62,73 @@
     return me_lat, me_lon, place, remote, signal
 
 
+def taper_sq(d2):
+    z = jnp.sqrt(d2) * (1.0 / LOC)
+    inner = (((-0.25 * z + 0.5) * z + 0.625) * z - 5.0 / 3.0) * z * z + 1.0
+    outer = (
+        ((((z * (1.0 / 12.0) - 0.5) * z + 0.625) * z + 5.0 / 3.0) * z - 5.0) * z
+        + 4.0
+        - (2.0 / 3.0) / jnp.maximum(z, 1.0)
+    )
+    return jnp.where(z <= 1.0, inner, jnp.where(z < 2.0, outer, 0.0))
+
+
+def by_block(ref):
+    parts = []
+    for b in range(NB):
+        first = (b % PER) * BLOCK
+        parts.append(ref[b // PER : b // PER + 1, first : first + BLOCK])
+    return jnp.concatenate(parts, axis=0)
+
+
+def pair_at(b, j):
+    return b * (2 * NB - b - 1) // 2 + j - b - 1
+
+
+def cell_tapers(pick, lat_row, lon_row, lat0f, lon0f, out, slot):
+    col_f = lax.broadcasted_iota(jnp.int32, (KC, COLS), 1).astype(F32) + lon0f
+    latc = jnp.sum(pick * lat_row, axis=1, keepdims=True)
+    lonc = jnp.sum(pick * lon_row, axis=1, keepdims=True)
+    dlon = jnp.abs(lonc - col_f)
+    dlon = jnp.minimum(dlon, NLON - dlon)
+    dlon = dlon * dlon
+    for r in range(ROWS):
+        dlat = latc - (lat0f + float(r))
+        out[slot, :, r * COLS : (r + 1) * COLS] = taper_sq(dlon + dlat * dlat)
+
+
+def reach_tables(lat, lon, lat0f, lon0f, rank_ref, t0_ref):
+    dy = jnp.maximum(jnp.maximum(lat0f - lat, lat - (lat0f + (ROWS - 1))), 0.0)
+    off = lon - lon0f
+    off = jnp.where(off < 0, off + NLON, off)
+    dx = jnp.maximum(jnp.minimum(off - (COLS - 1), NLON - off), 0.0)
+    reach = dx * dx + dy * dy < 4.0 * LOC * LOC
+    before = (
+        lax.broadcasted_iota(jnp.int32, (BLOCK, BLOCK), 0)
+        < lax.broadcasted_iota(jnp.int32, (BLOCK, BLOCK), 1)
+    ).astype(F32)
+    rank = jnp.where(reach, dot(reach.astype(F32).astype(BF), before.astype(BF)), -1.0)
+    rank_ref[...] = rank
+    row_id = lax.broadcasted_iota(jnp.int32, (KC, BLOCK), 0).astype(F32)
+    for b in range(NB):
+        pick = (row_id == rank[b : b + 1, :]).astype(F32)
+        cell_tapers(pick, lat[b : b + 1, :], lon[b : b + 1, :], lat0f, lon0f, t0_ref, b)
+
+
+def pair_tables(lat, lon, pair_ref):
+    lat_t, lon_t = lat.T, lon.T
+    for b in range(NB):
+        for j in range(b + 1, NB):
+            dlat = lat_t[:, b : b + 1] - lat[j : j + 1, :]
+            dlon = jnp.abs(lon_t[:, b : b + 1] - lon[j : j + 1, :])
+            dlon = jnp.minimum(dlon, NLON - dlon)
+            pair_ref[pair_at(b, j)] = taper_sq(dlat * dlat + dlon * dlon)
+
+
 def forecast_kernel(
     nlat, nlon,
     x_hbm, wind_hbm, lat_hbm, lon_hbm, var_hbm,
-    xf, out,
+    xf, out, rank_ref, t0_ref, pair_ref,
     xb, wind_ref, lat_ref, lon_ref, var_ref, desc, desc_s, xft, yo, part, line, block_sum, got_a, got_b,
     xt, edge, edge_w, edge_e, corner, wind_n, halo, halo_s, halo1_s, coef, shift, unit, q1_s,
     s_row, r_row, s_edge, r_edge, s_corner, r_corner, s_wind, r_wind,
@@ -329,6 +392,9 @@
     ]
     for c in first:
         c.start()
+    lat_f, lon_f = by_block(lat_ref).astype(F32), by_block(lon_ref).astype(F32)
+    lat0f, lon0f = (me_lat * ROWS).astype(F32), (me_lon * COLS).astype(F32)
+    reach_tables(lat_f, lon_f, lat0f, lon0f, rank_ref, t0_ref)
     total = part[me_lat]
     for i, c in enumerate(first):
         c.wait_recv()
@@ -340,6 +406,7 @@
     ]
     for c in second:
         c.start()
+    pair_tables(lat_f, lon_f, pair_ref)
     for i, c in enumerate(second):
         c.wait_recv()
         total = total + got_b[i]
@@ -369,9 +436,12 @@
         out_shape=(
             jax.ShapeDtypeStruct((NVAR, ROWS, MEMBERS, COLS), F32),
             jax.ShapeDtypeStruct((NB, MEMBERS, BLOCK), F32),
+            jax.ShapeDtypeStruct((NB, BLOCK), F32),
+            jax.ShapeDtypeStruct((NB, KC, ROWS * COLS), F32),
+            jax.ShapeDtypeStruct((NB * (NB - 1) // 2, BLOCK, BLOCK), F32),
         ),
         in_specs=[pl.BlockSpec(memory_space=pltpu.HBM)] * 5,
-        out_specs=(vm, vm),
+        out_specs=(vm,) * 5,
         scratch_shapes=[
             pltpu.VMEM((MEMBERS, NVAR, ROWS, COLS), F32),
             pltpu.VMEM((2, ROWS, COLS), F32),
@@ -406,62 +476,59 @@
             dma((NVG,)), dma((5,)),
         ],
         compiler_params=pltpu.CompilerParams(
-            collective_id=0, has_side_effects=True, vmem_limit_bytes=34 << 20
+            collective_id=0, has_side_effects=True, vmem_limit_bytes=30 << 20
         ),
         name="forecast",
     )(x, wind, lat, lon, var)
 
 
-def taper_sq(d2):
-    z = jnp.sqrt(d2) * (1.0 / LOC)
-    inner = (((-0.25 * z + 0.5) * z + 0.625) * z - 5.0 / 3.0) * z * z + 1.0
-    outer = (
-        ((((z * (1.0 / 12.0) - 0.5) * z + 0.625) * z + 5.0 / 3.0) * z - 5.0) * z
-        + 4.0
-        - (2.0 / 3.0) / jnp.maximum(z, 1.0)
-    )
-    return jnp.where(z <= 1.0, inner, jnp.where(z < 2.0, outer, 0.0))
-
-
 def analysis_kernel(
-    x_ref, y_ref, lat_ref, lon_ref, val_ref, err_ref,
-    out_ref,
-    ys, a_all, s_all, a_pk, b_pk, t_pk, xv, rhs, q3, nch,
+    x_ref, y_ref, rank_ref, t0_ref, pair_ref, lat_hbm, lon_hbm, val_hbm, err_hbm,
+    out_hbm,
+    lat_ref, lon_ref, val_ref, err_ref, ob,
+    ys, a_all, s_all, a_pk, b_pk, l_pk, a_more, b_more, t_more, xv, rhs, p2, q3, nch,
+    l_small, l_out,
 ):
-    lat0 = lax.axis_index("lat") * ROWS
-    lon0 = lax.axis_index("lon") * COLS
-
-    def by_block(ref):
-        rows = [ref[b // PER : b // PER + 1, (b % PER) * BLOCK : (b % PER + 1) * BLOCK] for b in range(NB)]
-        return jnp.concatenate(rows, axis=0)
-
-    lat = by_block(lat_ref).astype(F32)
-    lon = by_block(lon_ref).astype(F32)
-    values = by_block(val_ref)
-    variances = by_block(err_ref)
-    lat_t = lat.T
-    lon_t = lon.T
-    lat0f = lat0.astype(F32)
-    lon0f = lon0.astype(F32)
-    dy = jnp.maximum(jnp.maximum(lat0f - lat, lat - (lat0f + (ROWS - 1))), 0.0)
-    off = lon - lon0f
-    off = jnp.where(off < 0, off + NLON, off)
-    dx = jnp.maximum(jnp.minimum(off - (COLS - 1), NLON - off), 0.0)
-    reach = dx * dx + dy * dy < 4.0 * LOC * LOC
-    reach_b = reach.astype(F32)
-    before = (
-        lax.broadcasted_iota(jnp.int32, (BLOCK, BLOCK), 0)
-        < lax.broadcasted_iota(jnp.int32, (BLOCK, BLOCK), 1)
-    ).astype(F32)
-    rank = dot(reach_b.astype(BF), before.astype(BF))
-    rank = jnp.where(reach, rank, -1.0)
-    for b in range(NB):
-        n = jnp.sum(reach_b[b : b + 1, :])
-        nch[b] = ((n + (KC - 1)) * (1.0 / KC)).astype(jnp.int32)
-
-    for b in range(NB):
+    small = [
+        pltpu.make_async_copy(a, b, l_small.at[i])
+        for i, (a, b) in enumerate(
+            [(lat_hbm, lat_ref), (lon_hbm, lon_ref), (val_hbm, val_ref), (err_hbm, err_ref)]
+        )
+    ]
+    for c in small:
+        c.start()
+    out_rows = ob.reshape(MEMBERS * NVAR * ROWS, COLS)
+
+    def store(g):
+        vs = pl.ds(g * VG, VG)
+        return pltpu.make_async_copy(ob.at[:, vs], out_hbm.at[:, vs], l_out.at[g])
+
+    rank = rank_ref[...]
+    for b in range(NB):
+        top = jnp.max(rank[b : b + 1, :])
+        nch[b] = ((top + KC) * (1.0 / KC)).astype(jnp.int32)
         ys[:, b * BLOCK : (b + 1) * BLOCK] = y_ref[b]
+    for c in small:
+        c.wait()
+    lat, lon = by_block(lat_ref).astype(F32), by_block(lon_ref).astype(F32)
+    values, variances = by_block(val_ref), by_block(err_ref)
+    row_id = lax.broadcasted_iota(jnp.int32, (KC, BLOCK), 0).astype(F32)
+    lane96 = lax.broadcasted_iota(jnp.int32, (KC, 3 * KC), 1)
     zero8 = jnp.zeros((8, BLOCK), F32)
+
+    def packed(pick, b):
+        zero = jnp.zeros_like(pick)
+        pick3 = jnp.concatenate(
+            [
+                jnp.concatenate([pick, zero], axis=1),
+                jnp.concatenate([zero, pick], axis=1),
+                jnp.concatenate([pick, zero], axis=1),
+            ],
+            axis=0,
+        )
+        return dot(pick, a_all[b]).astype(BF), dot(s_all[b], pick3, ((1,), (1,))).astype(BF)
+
+    stacked = None
     for b in range(NB):
         prior = ys[:, b * BLOCK : (b + 1) * BLOCK]
         average = jnp.sum(prior, axis=0, keepdims=True) * (1.0 / MEMBERS)
@@ -475,61 +542,57 @@
         )
         wh = hi(weights)
         a = jnp.concatenate([wh, weights - wh, wh, zero8], axis=0).T.astype(BF)
-        sh = shifts.astype(BF)
-        sl = (shifts - sh.astype(F32)).astype(BF)
-        s2 = jnp.concatenate([sh, sl], axis=1)
+        sh, sl = split(shifts)
         a_all[b] = a
-        s_all[b] = s2
-        if b + 1 < NB:
-            first = (b + 1) * BLOCK
-            s3 = jnp.concatenate([sh, sl, sh], axis=1)
-            latk = lat_t[:, b : b + 1]
-            lonk = lon_t[:, b : b + 1]
-            for j in range(b + 1, NB):
-                yl = ys[:, j * BLOCK : (j + 1) * BLOCK]
-                yh = hi(yl)
-                y3 = jnp.concatenate([yh, yh, yl - yh, zero8], axis=0).astype(BF)
-                p = dot(a, y3)
-                dlat = latk - lat[j : j + 1, :]
-                dlon = jnp.abs(lonk - lon[j : j + 1, :])
-                dlon = jnp.minimum(dlon, NLON - dlon)
-                q = p * taper_sq(dlat * dlat + dlon * dlon)
-                qh = q.astype(BF)
-                ql = (q - qh.astype(F32)).astype(BF)
-                ys[:, j * BLOCK : (j + 1) * BLOCK] = yl + dot(
-                    s3, jnp.concatenate([qh, qh, ql], axis=0)
-                )
-
-    row_id = lax.broadcasted_iota(jnp.int32, (KC, BLOCK), 0)
-    col_f = lax.broadcasted_iota(jnp.int32, (KC, COLS), 1).astype(F32) + lon0f
-    for b in range(NB):
-
-        @pl.loop(0, nch[b])
+        s_all[b] = jnp.concatenate([sh, sl], axis=1)
+        s3 = jnp.concatenate([sh, sl, sh], axis=1)
+        for j in range(b + 1, NB):
+            yl = ys[:, j * BLOCK : (j + 1) * BLOCK]
+            yh = hi(yl)
+            y3 = jnp.concatenate([yh, yh, yl - yh, zero8], axis=0).astype(BF)
+            qh, ql = split(dot(a, y3) * pair_ref[pair_at(b, j)])
+            ys[:, j * BLOCK : (j + 1) * BLOCK] = yl + dot(
+                s3, jnp.concatenate([qh, qh, ql], axis=0)
+            )
+        pick = (row_id == rank[b : b + 1, :]).astype(BF)
+        a_pk[b], b_pk[b] = packed(pick, b)
+        if b % 2 == 0:
+            sh32 = sh.astype(F32)
+            s_rows = jnp.concatenate([sh32, sh32, sl.astype(F32), zero8], axis=0).astype(BF)
+            stacked = dot(s_rows, jnp.concatenate([pick] * 3, axis=0), ((1,), (1,))).astype(BF)
+        else:
+            c = dot(a_pk[b], stacked)
+            ch = hi(c)
+            c3 = jnp.where((lane96 >= KC) & (lane96 < 2 * KC), c - ch, ch)
+            l_pk[b // 2] = jnp.concatenate([c3, b_pk[b - 1].astype(F32)], axis=0).astype(BF)
+
+    lat0f = (lax.axis_index("lat") * ROWS).astype(F32)
+    lon0f = (lax.axis_index("lon") * COLS).astype(F32)
+    for b in range(NB):
+
+        @pl.loop(1, nch[b])
         def _(c):
-            slot = b * NCH + c
-            pick = ((row_id + c * KC).astype(F32) == rank[b : b + 1, :]).astype(F32)
-            pick_b = pick.astype(BF)
-            a_pk[slot] = dot(pick_b, a_all[b]).astype(BF)
-            zero = jnp.zeros_like(pick_b)
-            pick3 = jnp.concatenate(
-                [
-                    jnp.concatenate([pick_b, zero], axis=1),
-                    jnp.concatenate([zero, pick_b], axis=1),
-                    jnp.concatenate([pick_b, zero], axis=1),
-                ],
-                axis=0,
-            )
-            b_pk[slot] = dot(s_all[b], pick3, ((1,), (1,))).astype(BF)
-            latc = jnp.sum(pick * lat[b : b + 1, :], axis=1, keepdims=True)
-            lonc = jnp.sum(pick * lon[b : b + 1, :], axis=1, keepdims=True)
-            dlon = jnp.abs(lonc - col_f)
-            dlon = jnp.minimum(dlon, NLON - dlon)
-            dlon = dlon * dlon
-            for r in range(ROWS):
-                dlat = latc - (lat0f + float(r))
-                t_pk[slot, :, r * COLS : (r + 1) * COLS] = taper_sq(dlon + dlat * dlat)
-
-    zero256 = jnp.zeros((8, 256), F32)
+            slot = b * (NCH - 1) + c - 1
+            pick = (row_id + (c * KC).astype(F32) == rank[b : b + 1, :]).astype(F32)
+            a_more[slot], b_more[slot] = packed(pick.astype(BF), b)
+            cell_tapers(pick, lat[b : b + 1, :], lon[b : b + 1, :], lat0f, lon0f, t_more, slot)
+
+    zero_cols = jnp.zeros((8, ROWS * COLS), F32)
+
+    def stack_x(i):
+        x = xv[i]
+        xh = hi(x)
+        rhs[i] = jnp.concatenate([xh, xh, x - xh, zero_cols], axis=0).astype(BF)
+
+    def put_q(i, q):
+        qh, ql = split(q)
+        q3[i] = jnp.concatenate([qh, qh, ql], axis=0)
+
+    def add_chunk(a, s3, t):
+        for i in range(VG):
+            put_q(i, dot(a, rhs[i]) * t[...])
+        for i in range(VG):
+            xv[i] += dot(s3, q3[i])
 
     @pl.loop(0, NVAR // VG)
     def _(g):
@@ -537,70 +600,98 @@
             for r in range(ROWS):
                 xv[i, :, r * COLS : (r + 1) * COLS] = x_ref[g * VG + i, r]
 
-        @pl.loop(0, NB)
-        def _(b):
-            for i in range(VG):
-                for h in range(4):
-                    x = xv[i, :, h * 256 : (h + 1) * 256]
-                    xh = hi(x)
-                    rhs[i, :, h * 256 : (h + 1) * 256] = jnp.concatenate(
-                        [xh, xh, x - xh, zero256], axis=0
-                    ).astype(BF)
-
-            @pl.loop(0, nch[b])
-            def _(c):
-                slot = b * NCH + c
-                a = a_pk[slot]
-                s3 = b_pk[slot]
+        @pl.loop(0, NB // 2)
+        def _(pair):
+            b = 2 * pair
+            few = jnp.maximum(nch[b], nch[b + 1]) <= 1
+
+            @pl.when(few)
+            def _():
+                a2 = a_pk[pl.ds(b, 2)].reshape(2 * KC, 128)
                 for i in range(VG):
-                    q = dot(a, rhs[i]) * t_pk[slot]
-                    qh = q.astype(BF)
-                    q3[i] = jnp.concatenate([qh, qh, (q - qh.astype(F32)).astype(BF)], axis=0)
+                    stack_x(i)
                 for i in range(VG):
-                    xv[i] += dot(s3, q3[i])
+                    p = dot(a2, rhs[i])
+                    p2[i] = p[KC:]
+                    put_q(i, p[:KC] * t0_ref[b])
+                for i in range(VG):
+                    r = dot(l_pk[pair], q3[i])
+                    xv[i] += r[KC:]
+                    put_q(i, (p2[i] + r[:KC]) * t0_ref[b + 1])
+                for i in range(VG):
+                    xv[i] += dot(b_pk[b + 1], q3[i])
+
+            @pl.when(jnp.logical_not(few))
+            def _():
+                @pl.loop(b, b + 2)
+                def _(bb):
+                    for i in range(VG):
+                        stack_x(i)
+                    add_chunk(a_pk[bb], b_pk[bb], t0_ref.at[bb])
+
+                    @pl.loop(1, nch[bb])
+                    def _(c):
+                        slot = bb * (NCH - 1) + c - 1
+                        add_chunk(a_more[slot], b_more[slot], t_more.at[slot])
 
         for i in range(VG):
             for r in range(ROWS):
-                out_ref[
+                out_rows[
                     pl.ds((g * VG + i) * ROWS + r, MEMBERS, stride=NVAR * ROWS), :
                 ] = xv[i, :, r * COLS : (r + 1) * COLS]
-
-
-def analysis(x, y, lat, lon, val, err):
+        store(g).start()
+
+    for g in range(NVAR // VG):
+        store(g).wait()
+
+
+def analysis(x, y, rank, t0, pairs, lat, lon, val, err):
     vm = pl.BlockSpec(memory_space=pltpu.VMEM)
+    hbm = pl.BlockSpec(memory_space=pltpu.HBM)
+    more = NB * (NCH - 1)
+    dma = pltpu.SemaphoreType.DMA
     return pl.pallas_call(
         analysis_kernel,
-        out_shape=jax.ShapeDtypeStruct((MEMBERS * NVAR * ROWS, COLS), F32),
-        in_specs=[vm] * 6,
-        out_specs=vm,
+        out_shape=jax.ShapeDtypeStruct((MEMBERS, NVAR, ROWS, COLS), F32),
+        in_specs=[vm] * 5 + [hbm] * 4,
+        out_specs=hbm,
         scratch_shapes=[
+            pltpu.VMEM((GROUPS, OBS), jnp.int32),
+            pltpu.VMEM((GROUPS, OBS), jnp.int32),
+            pltpu.VMEM((GROUPS, OBS), F32),
+            pltpu.VMEM((GROUPS, OBS), F32),
+            pltpu.VMEM((MEMBERS, NVAR, ROWS, COLS), F32),
             pltpu.VMEM((MEMBERS, NB * BLOCK), F32),
             pltpu.VMEM((NB, BLOCK, 128), BF),
             pltpu.VMEM((NB, MEMBERS, 256), BF),
-            pltpu.VMEM((NB * NCH, KC, 128), BF),
-            pltpu.VMEM((NB * NCH, MEMBERS, 3 * KC), BF),
-            pltpu.VMEM((NB * NCH, KC, ROWS * COLS), F32),
+            pltpu.VMEM((NB, KC, 128), BF),
+            pltpu.VMEM((NB, MEMBERS, 3 * KC), BF),
+            pltpu.VMEM((NB // 2, KC + MEMBERS, 3 * KC), BF),
+            pltpu.VMEM((more, KC, 128), BF),
+            pltpu.VMEM((more, MEMBERS, 3 * KC), BF),
+            pltpu.VMEM((more, KC, ROWS * COLS), F32),
             pltpu.VMEM((VG, MEMBERS, ROWS * COLS), F32),
             pltpu.VMEM((VG, 128, ROWS * COLS), BF),
+            pltpu.VMEM((VG, KC, ROWS * COLS), F32),
             pltpu.VMEM((VG, 3 * KC, ROWS * COLS), BF),
             pltpu.SMEM((NB,), jnp.int32),
+            dma((4,)), dma((NVAR // VG,)),
         ],
-        compiler_params=pltpu.CompilerParams(vmem_limit_bytes=16 << 20),
+        compiler_params=pltpu.CompilerParams(vmem_limit_bytes=22 << 20),
         name="analysis",
-    )(x, y, lat, lon, val, err)
+    )(x, y, rank, t0, pairs, lat, lon, val, err)
 
 
 def solution(mesh):
     nlat, nlon = mesh.shape["lat"], mesh.shape["lon"]
 
     def body(prognostic_samples, wind, obs_lat, obs_lon, obs_var, obs_value, obs_error):
-        args = [
+        hbm = [
             pltpu.with_memory_space_constraint(a, pltpu.HBM)
-            for a in (prognostic_samples, wind, obs_lat, obs_lon, obs_var)
+            for a in (prognostic_samples, wind, obs_lat, obs_lon, obs_var, obs_value, obs_error)
         ]
-        xf, y = forecast(*args, nlat, nlon)
-        out = analysis(xf, y, obs_lat, obs_lon, obs_value, obs_error)
-        return out.reshape(prognostic_samples.shape)
+        xf, y, rank, t0, pairs = forecast(*hbm[:5], nlat, nlon)
+        return analysis(xf, y, rank, t0, pairs, hbm[2], hbm[3], hbm[5], hbm[6])
 
     in_specs = (P(None, None, "lat", "lon"), P(None, "lat", "lon"), P(), P(), P(), P(), P())
     out_specs = P(None, None, "lat", "lon")

time: 83.7 us -> 72.4 us (0.86)
  Pallas kernels: 83.5 us -> 72.2 us
    pallas_call x1, Pallas kernels: 34 us -> 22.8 us  [analysis(): pl.pallas_call(analysis_kernel, out_shape=jax.ShapeDtypeStruct((MEMBERS,...]
where the time goes in v6:
time: 72.4 us; the launch traced here: 72.2 us
  Pallas kernels  72.2 us (100%)
    pallas_call x1, Pallas kernels, forecast(): pl.pallas_call(lambda *refs: forecast_kernel(nlat, nlon, *refs), out_shap...  49.4 us
    pallas_call x1, Pallas kernels, analysis(): pl.pallas_call(analysis_kernel, out_shape=jax.ShapeDtypeStruct((MEMBERS,...  22.8 us

profile of v6, /device:TPU:1, one launch (start us, length us, event | category | flops | bytes accessed | tf_op | source)
XLA Modules:
  0.0 72.2 jit_solution(4759270859420112220)
XLA Ops:
  0.0 49.4 %forecast.1 = (f32[25,8,40,128]{3,2,1,0:T(8,128)S(1)}, f32[8,40,128]{2,1,0:T(8,128)S(1)}, f32[8,128]{1,0:T(8,128)S(1)}, f32[8,32,1024]{2,1,0:T(8,128)S(1)}, f32[28,128,128]{2,1,0:T(8,128)S(1)}) custom-call(f32[40,25,8,128]{3,2,1,0:T(8,128)} %refs_0_.1, f32[2,8,128]{2,1,0:T(8,128)} %refs_1_.1, s32[2,512]{1,0:T(2,128)} %lat_hbm.1, s32[2,512]{1,0:T(2,128)} %lon_hbm.1, ...), custom_call_target="tpu_custom_call" | custom-call | tf_op jit(solution)/shard_map/forecast/pallas_call | solution.py:434
  49.4 22.8 %analysis.1 = f32[40,25,8,128]{3,2,1,0:T(8,128)} custom-call(f32[25,8,40,128]{3,2,1,0:T(8,128)S(1)} %get-tuple-element.10.x_ref, f32[8,40,128]{2,1,0:T(8,128)S(1)} %get-tuple-element.11.y_ref, f32[8,128]{1,0:T(8,128)S(1)} %get-tuple-element.12.rank_ref, f32[8,32,1024]{2,1,0:T(8,128)S(1)} %get-tuple-element.13.t0_ref, ...), custom_call_target="tpu_custom_call" | custom-call | tf_op jit(solution)/shard_map/analysis/pallas_call | solution.py:653

commit v7 on v6

--- a/solution.py
+++ b/solution.py
@@ -16,6 +16,7 @@
 NVG = NVAR // VS
 MG = MEMBERS // 8
 SIDE = (ROWS + 2) // 3
+PIECE = 24
 KC = 32
 NCH = BLOCK // KC
 VG = 5
@@ -130,9 +131,9 @@
     x_hbm, wind_hbm, lat_hbm, lon_hbm, var_hbm,
     xf, out, rank_ref, t0_ref, pair_ref,
     xb, wind_ref, lat_ref, lon_ref, var_ref, desc, desc_s, xft, yo, part, line, block_sum, got_a, got_b,
-    xt, edge, edge_w, edge_e, corner, wind_n, halo, halo_s, halo1_s, coef, shift, unit, q1_s,
+    xt, edge, edge_w, edge_e, corner, wind_n, halo, halo_s, halo1_s, coef, shift, unit, q1_s, to_edge, at8,
     s_row, r_row, s_edge, r_edge, s_corner, r_corner, s_wind, r_wind,
-    send, recv_a, recv_b, recv_c, l_x, l_small,
+    send, send_a, recv_a, recv_b, recv_c, l_x, l_small,
 ):
     def fetch(vg):
         vs = pl.ds(vg * VS, VS)
@@ -192,6 +193,18 @@
         remote(edge.at[0], corner.at[2], s_corner.at[2], r_corner.at[2], -1, 1),
         remote(edge.at[0], corner.at[3], s_corner.at[3], r_corner.at[3], -1, -1),
     ]
+    edge_src = lax.rem(lax.broadcasted_iota(jnp.int32, (2 * COLS, COLS), 0), COLS)
+    edge_dst = lax.broadcasted_iota(jnp.int32, (2 * COLS, COLS), 1)
+    outer = (edge_src < 2) | (edge_src >= COLS - 2)
+    moved = jnp.where(outer, (edge_dst - edge_src) & (COLS - 1), -1)
+
+    @pl.loop(0, NVG)
+    def _(vg):
+        for vi in range(VS):
+            to_edge[vg, vi * 2 * COLS : (vi + 1) * 2 * COLS, :] = jnp.where(
+                moved == 4 * (vg * VS + vi), 1.0, 0.0
+            ).astype(BF)
+
     for vg in range(NVG):
         fetch(vg).wait()
 
@@ -210,21 +223,20 @@
         if vg < 2:
             send_rows(vg)
 
-    lane = lax.broadcasted_iota(jnp.int32, (8, COLS), 1)
     edge[...] = jnp.zeros_like(edge)
 
-    @pl.loop(0, NVAR)
-    def _(v):
-        mine = ((lane - 4 * v + 2) & (COLS - 1)) < 4
-        for r in range(ROWS):
-            for mg in range(MG):
-                ms = slice(mg * 8, (mg + 1) * 8)
-                if 2 <= r < ROWS - 2:
-                    t = column(r, mg, v)
-                    xt[v, r + 2, ms, :] = t
-                else:
-                    t = xt[v, r + 2, ms, :]
-                edge[r, ms, :] = jnp.where(mine, pltpu.roll(t, 4 * v, 1), edge[r, ms, :])
+    @pl.loop(0, NVG)
+    def _(vg):
+        pieces = []
+        for vi in range(VS):
+            v = vg * VS + vi
+            for r in range(2, ROWS - 2):
+                for mg in range(MG):
+                    xt[v, r + 2, mg * 8 : (mg + 1) * 8, :] = column(r, mg, v)
+        for vi in range(VS):
+            pieces += split(xt[vg * VS + vi, 2 : ROWS + 2].reshape(ROWS * MEMBERS, COLS))
+        packed = dot(jnp.concatenate(pieces, axis=1), to_edge[vg])
+        edge[...] += packed.reshape(ROWS, MEMBERS, COLS)
 
     for e in edges + corners:
         e.start()
@@ -239,6 +251,10 @@
     desc[...] = (var_ref[...] * SIDE + group) * COLS + (lon_all & (COLS - 1))
     to_scalar = pltpu.make_async_copy(desc, desc_s, l_small.at[4])
     to_scalar.start()
+    at_all = jnp.where(owned, part_of, -1)
+    for b in range(NB):
+        cut = (b % PER) * BLOCK
+        at8[b : b + 1, :] = at_all[b // PER : b // PER + 1, cut : cut + BLOCK]
 
     src = lax.rem(lax.broadcasted_iota(jnp.int32, (2 * COLS, 2 * COLS), 0), COLS)
     dst = lax.broadcasted_iota(jnp.int32, (2 * COLS, 2 * COLS), 1)
@@ -285,9 +301,12 @@
     halo[ROWS + 1] = jnp.where(from_west, corner[2], corner[3])
     for r in range(ROWS):
         halo[r + 1] = jnp.where(from_west, edge_w[r], edge_e[r])
+
+    def beside(t):
+        return jnp.where(lane4 == 0, t, pltpu.roll(t, 2, 1))
+
     for r in range(ROWS + 2):
-        high, low = split(halo[r])
-        halo_s[r] = jnp.concatenate([high, low], axis=1)
+        halo_s[r] = beside(halo[r])
     for r in range(ROWS):
         u, v = [
             jnp.where(
@@ -308,29 +327,25 @@
             + cn * halo[r + 2]
             + cs * halo[r]
         )
-        high, low = split(after)
-        halo1_s[r] = jnp.concatenate([high, low], axis=1)
-
-    def step(q, nxt, prv, side, place_side, first, count):
+        halo1_s[r] = beside(after)
+
+    def step(q, nxt, prv, side, back, first, count):
         shape = (count, MG, 8, COLS)
         high, low = split(q)
-        both = dot(jnp.concatenate([high, low], axis=1), shift[...]) + dot(
-            side.reshape(count * MEMBERS, 2 * COLS), place_side
-        )
+        both = dot(jnp.concatenate([high, low], axis=1), shift[...])
+        lane = lax.broadcasted_iota(jnp.int32, (count * MEMBERS, COLS), 1)
+        beyond = pltpu.roll(side.reshape(count * MEMBERS, COLS), back, 1)
+        east = jnp.where(lane == COLS - 1, beyond, both[:, :COLS])
+        west = jnp.where(lane == 0, beyond, both[:, COLS:])
         c = [coef[i, first : first + count].reshape(count, 1, 8, COLS) for i in range(4)]
         new = (
             (1.0 - 4.0 * DIFFUSE) * q.reshape(shape)
-            + c[0] * both[:, :COLS].reshape(shape)
-            + c[1] * both[:, COLS:].reshape(shape)
+            + c[0] * east.reshape(shape)
+            + c[1] * west.reshape(shape)
             + c[2] * nxt.reshape(shape)
             + c[3] * prv.reshape(shape)
         )
         return new.reshape(count * MEMBERS, COLS)
-
-    def place_side(v):
-        at_end = (dst == COLS - 1) & (src == 4 * v)
-        at_start = (dst == COLS) & (src == ((4 * v - 1) & (COLS - 1)))
-        return jnp.where(at_end | at_start, 1.0, 0.0).astype(BF)
 
     def block(ref, v, first, count):
         return ref[v, first : first + count].reshape(count * MEMBERS, COLS)
@@ -350,13 +365,13 @@
             v = vg * VS + vi
             q1_s[vi] = step(
                 block(xt, v, 1, n1), block(xt, v, 2, n1), block(xt, v, 0, n1),
-                halo_s[...], place_side(v), 0, n1,
+                halo_s[...], (COLS - 1 - 4 * v) & (COLS - 1), 0, n1,
             ).reshape(n1, MEMBERS, COLS)
         for vi in range(VS):
             v = vg * VS + vi
             new = step(
                 block(q1_s, vi, 1, n2), block(q1_s, vi, 2, n2), block(q1_s, vi, 0, n2),
-                halo1_s[...], place_side(v), 1, n2,
+                halo1_s[...], (COLS - 1 - 4 * v) & (COLS - 1), 1, n2,
             )
             xf[v] = new.reshape(n2, MEMBERS, COLS)
             high, low = split(new)
@@ -368,56 +383,81 @@
                 )
 
     to_scalar.wait()
-    for b in range(NB):
+    half, odd = me_lon // 2, lax.rem(me_lon, 2)
+
+    def piece(i, h, b):
+        return pltpu.make_async_remote_copy(
+            src_ref=part.at[2 * b + h],
+            dst_ref=got_a.at[i, odd],
+            send_sem=send_a.at[i, h],
+            recv_sem=recv_a.at[i, odd],
+            device_id=(me_lat, 2 * b + h),
+            device_id_type=MESH,
+        )
+
+    def arrival(i, p):
+        return pltpu.make_async_remote_copy(
+            src_ref=part.at[0],
+            dst_ref=got_a.at[i, p],
+            send_sem=send_a.at[i, 0],
+            recv_sem=recv_a.at[i, p],
+            device_id=(me_lat, lax.rem(me_lon + 1, nlon)),
+            device_id_type=MESH,
+        )
+
+    first = []
+    for i in list(range(1, NB)) + [0]:
+        b = lax.rem(half + i, NB)
 
         @pl.loop(0, BLOCK // 8)
         def _(g):
             for j in range(8):
                 k = g * 8 + j
-                at = desc_s[b // PER, (b % PER) * BLOCK + k]
-                yo[b, pl.ds(k, 1), :] = xft[pl.ds(at, 1), :]
-
-    for b in range(NB):
-        cut = (slice(b // PER, b // PER + 1), slice((b % PER) * BLOCK, (b % PER + 1) * BLOCK))
-        turned = yo[b].T
-        at = jnp.broadcast_to(jnp.where(owned[cut], part_of[cut], -1), (MEMBERS, BLOCK))
+                at = desc_s[b // PER, lax.rem(b, PER) * BLOCK + k]
+                yo[i, pl.ds(k, 1), :] = xft[pl.ds(at, 1), :]
+
+        turned = yo[i].T
+        at = jnp.broadcast_to(at8[pl.ds(b, 1), :], (MEMBERS, BLOCK))
         mine = jnp.zeros((MEMBERS, BLOCK), F32)
-        for i in range(3):
-            mine = jnp.where(at == i, turned[i * MEMBERS : (i + 1) * MEMBERS, :], mine)
-        part[b] = mine
-
-    first = [
-        remote(part.at[place(o, 0)[0]], got_a.at[o - 1], send.at[o - 1], recv_a.at[o - 1], o, 0)
-        for o in range(1, nlat)
-    ]
-    for c in first:
-        c.start()
+        for n in range(3):
+            mine = jnp.where(at == n, turned[n * MEMBERS : (n + 1) * MEMBERS, :], mine)
+        part[2 * b] = mine[0:PIECE]
+        part[2 * b + 1] = jnp.concatenate(
+            [mine[PIECE:], jnp.zeros((2 * PIECE - MEMBERS, BLOCK), F32)], axis=0
+        )
+        for h in (0, 1) if i else (1 - odd,):
+            c = piece(i, h, b)
+            c.start()
+            first.append(c)
     lat_f, lon_f = by_block(lat_ref).astype(F32), by_block(lon_ref).astype(F32)
     lat0f, lon0f = (me_lat * ROWS).astype(F32), (me_lon * COLS).astype(F32)
     reach_tables(lat_f, lon_f, lat0f, lon0f, rank_ref, t0_ref)
-    total = part[me_lat]
-    for i, c in enumerate(first):
-        c.wait_recv()
-        total = total + got_a[i]
+    total = part[me_lon]
+    for i in range(1, NB):
+        for p in (0, 1):
+            arrival(i, p).wait_recv()
+            total = total + got_a[i, p]
+    arrival(0, 1 - odd).wait_recv()
+    total = total + got_a[0, 1 - odd]
     line[...] = total
     second = [
-        remote(line, got_b.at[o - 1], send.at[nlat + o - 2], recv_b.at[o - 1], 0, o)
-        for o in range(1, nlon)
+        remote(line, got_b.at[o - 1], send.at[o - 1], recv_b.at[o - 1], o, 0)
+        for o in range(1, nlat)
     ]
     for c in second:
         c.start()
-    pair_tables(lat_f, lon_f, pair_ref)
     for i, c in enumerate(second):
         c.wait_recv()
         total = total + got_b[i]
     block_sum[...] = total
     third = [
-        remote(block_sum, out.at[me_lat], send.at[nlat + nlon + o - 3], recv_c.at[o - 1], o, 0)
-        for o in range(1, nlat)
+        remote(block_sum, out.at[me_lon], send.at[nlat + o - 2], recv_c.at[o - 1], 0, o)
+        for o in range(1, nlon)
     ]
     for c in third:
         c.start()
-    out[me_lat] = total
+    out[me_lon] = total
+    pair_tables(lat_f, lon_f, pair_ref)
     for c in third:
         c.wait_recv()
 
@@ -435,7 +475,7 @@
         lambda *refs: forecast_kernel(nlat, nlon, *refs),
         out_shape=(
             jax.ShapeDtypeStruct((NVAR, ROWS, MEMBERS, COLS), F32),
-            jax.ShapeDtypeStruct((NB, MEMBERS, BLOCK), F32),
+            jax.ShapeDtypeStruct((2 * NB, PIECE, BLOCK), F32),
             jax.ShapeDtypeStruct((NB, BLOCK), F32),
             jax.ShapeDtypeStruct((NB, KC, ROWS * COLS), F32),
             jax.ShapeDtypeStruct((NB * (NB - 1) // 2, BLOCK, BLOCK), F32),
@@ -452,11 +492,11 @@
             pltpu.SMEM((GROUPS, OBS), jnp.int32),
             pltpu.VMEM((NVAR * SIDE * COLS, COLS), F32),
             pltpu.VMEM((NB, BLOCK, COLS), F32),
-            pltpu.VMEM((NB, MEMBERS, BLOCK), F32),
-            pltpu.VMEM((MEMBERS, BLOCK), F32),
-            pltpu.VMEM((MEMBERS, BLOCK), F32),
-            pltpu.VMEM((nlat - 1, MEMBERS, BLOCK), F32),
-            pltpu.VMEM((nlon - 1, MEMBERS, BLOCK), F32),
+            pltpu.VMEM((2 * NB, PIECE, BLOCK), F32),
+            pltpu.VMEM((PIECE, BLOCK), F32),
+            pltpu.VMEM((PIECE, BLOCK), F32),
+            pltpu.VMEM((NB, 2, PIECE, BLOCK), F32),
+            pltpu.VMEM((nlat - 1, PIECE, BLOCK), F32),
             pltpu.VMEM((NVAR, ROWS + 4, MEMBERS, COLS), F32),
             pltpu.VMEM((ROWS, MEMBERS, COLS), F32),
             pltpu.VMEM((ROWS, MEMBERS, COLS), F32),
@@ -464,19 +504,21 @@
             pltpu.VMEM((4, MEMBERS, COLS), F32),
             pltpu.VMEM((4, 2, ROWS, COLS), F32),
             pltpu.VMEM((ROWS + 2, MEMBERS, COLS), F32),
-            pltpu.VMEM((ROWS + 2, MEMBERS, 2 * COLS), BF),
-            pltpu.VMEM((ROWS, MEMBERS, 2 * COLS), BF),
+            pltpu.VMEM((ROWS + 2, MEMBERS, COLS), F32),
+            pltpu.VMEM((ROWS, MEMBERS, COLS), F32),
             pltpu.VMEM((4, ROWS + 2, 8, COLS), F32),
             pltpu.VMEM((2 * COLS, 2 * COLS), BF),
             pltpu.VMEM((COLS, 2 * COLS), BF),
             pltpu.VMEM((VS, ROWS + 2, MEMBERS, COLS), F32),
+            pltpu.VMEM((NVG, VS * 2 * COLS, COLS), BF),
+            pltpu.VMEM((NB, BLOCK), jnp.int32),
             dma((NVG, 2)), dma((NVG, 2)), dma((2,)), dma((2,)),
             dma((4,)), dma((4,)), dma((4,)), dma((4,)),
-            dma((2 * nlat + nlon - 3,)), dma((nlat - 1,)), dma((nlon - 1,)), dma((nlat - 1,)),
+            dma((nlat + nlon - 2,)), dma((NB, 2)), dma((NB, 2)), dma((nlat - 1,)), dma((nlon - 1,)),
             dma((NVG,)), dma((5,)),
         ],
         compiler_params=pltpu.CompilerParams(
-            collective_id=0, has_side_effects=True, vmem_limit_bytes=30 << 20
+            collective_id=0, has_side_effects=True, vmem_limit_bytes=34 << 20
         ),
         name="forecast",
     )(x, wind, lat, lon, var)
@@ -507,7 +549,8 @@
     for b in range(NB):
         top = jnp.max(rank[b : b + 1, :])
         nch[b] = ((top + KC) * (1.0 / KC)).astype(jnp.int32)
-        ys[:, b * BLOCK : (b + 1) * BLOCK] = y_ref[b]
+        ys[0:PIECE, b * BLOCK : (b + 1) * BLOCK] = y_ref[2 * b]
+        ys[PIECE:, b * BLOCK : (b + 1) * BLOCK] = y_ref[2 * b + 1][0 : MEMBERS - PIECE]
     for c in small:
         c.wait()
     lat, lon = by_block(lat_ref).astype(F32), by_block(lon_ref).astype(F32)
@@ -684,6 +727,7 @@
 
 def solution(mesh):
     nlat, nlon = mesh.shape["lat"], mesh.shape["lon"]
+    assert nlon == 2 * NB
 
     def body(prognostic_samples, wind, obs_lat, obs_lon, obs_var, obs_value, obs_error):
         hbm = [

time: 72.4 us -> 69.2 us (0.956)
  Pallas kernels: 72.2 us -> 69 us
    pallas_call x1, Pallas kernels: 49.4 us -> 46.2 us  [forecast(): pl.pallas_call(lambda *refs: forecast_kernel(nlat, nlon, *refs), out_shap...]
where the time goes in v7:
time: 69.2 us; the launch traced here: 69 us
  Pallas kernels  69 us (100%)
    pallas_call x1, Pallas kernels, forecast(): pl.pallas_call(lambda *refs: forecast_kernel(nlat, nlon, *refs), out_shap...  46.2 us
    pallas_call x1, Pallas kernels, analysis(): pl.pallas_call(analysis_kernel, out_shape=jax.ShapeDtypeStruct((MEMBERS,...  22.8 us

profile of v7, /device:TPU:1, one launch (start us, length us, event | category | flops | bytes accessed | tf_op | source)
XLA Modules:
  0.0 69.0 jit_solution(17314689287723307210)
XLA Ops:
  0.0 46.2 %forecast.1 = (f32[25,8,40,128]{3,2,1,0:T(8,128)S(1)}, f32[16,24,128]{2,1,0:T(8,128)S(1)}, f32[8,128]{1,0:T(8,128)S(1)}, f32[8,32,1024]{2,1,0:T(8,128)S(1)}, f32[28,128,128]{2,1,0:T(8,128)S(1)}) custom-call(f32[40,25,8,128]{3,2,1,0:T(8,128)} %refs_0_.1, f32[2,8,128]{2,1,0:T(8,128)} %refs_1_.1, s32[2,512]{1,0:T(2,128)} %lat_hbm.1, s32[2,512]{1,0:T(2,128)} %lon_hbm.1, ...), custom_call_target="tpu_custom_call" | custom-call | tf_op jit(solution)/shard_map/forecast/pallas_call | solution.py:474
  46.2 22.8 %analysis.1 = f32[40,25,8,128]{3,2,1,0:T(8,128)} custom-call(f32[25,8,40,128]{3,2,1,0:T(8,128)S(1)} %get-tuple-element.10.x_ref, f32[16,24,128]{2,1,0:T(8,128)S(1)} %get-tuple-element.11.y_ref, f32[8,128]{1,0:T(8,128)S(1)} %get-tuple-element.12.rank_ref, f32[8,32,1024]{2,1,0:T(8,128)S(1)} %get-tuple-element.13.t0_ref, ...), custom_call_target="tpu_custom_call" | custom-call | tf_op jit(solution)/shard_map/analysis/pallas_call | solution.py:696

commit v8 on v7

--- a/solution.py
+++ b/solution.py
@@ -128,9 +128,9 @@
 
 def forecast_kernel(
     nlat, nlon,
-    x_hbm, wind_hbm, lat_hbm, lon_hbm, var_hbm,
-    xf, out, rank_ref, t0_ref, pair_ref,
-    xb, wind_ref, lat_ref, lon_ref, var_ref, desc, desc_s, xft, yo, part, line, block_sum, got_a, got_b,
+    x_hbm, wind_hbm, lat_hbm, lon_hbm, var_hbm, val_hbm, err_hbm,
+    xf, out, rank_ref, t0_ref, pair_ref, obs_ref,
+    xb, wind_ref, lat_ref, lon_ref, var_ref, val_ref, err_ref, desc, desc_s, xft, yo, part, line, block_sum, got_a, got_b,
     xt, edge, edge_w, edge_e, corner, wind_n, halo, halo_s, halo1_s, coef, shift, unit, q1_s, to_edge, at8,
     s_row, r_row, s_edge, r_edge, s_corner, r_corner, s_wind, r_wind,
     send, send_a, recv_a, recv_b, recv_c, l_x, l_small,
@@ -142,7 +142,10 @@
     small = [
         pltpu.make_async_copy(a, b, l_small.at[i])
         for i, (a, b) in enumerate(
-            [(wind_hbm, wind_ref), (lat_hbm, lat_ref), (lon_hbm, lon_ref), (var_hbm, var_ref)]
+            [
+                (wind_hbm, wind_ref), (lat_hbm, lat_ref), (lon_hbm, lon_ref),
+                (var_hbm, var_ref), (val_hbm, val_ref), (err_hbm, err_ref),
+            ]
         )
     ]
     for vg in range(NVG):
@@ -193,18 +196,6 @@
         remote(edge.at[0], corner.at[2], s_corner.at[2], r_corner.at[2], -1, 1),
         remote(edge.at[0], corner.at[3], s_corner.at[3], r_corner.at[3], -1, -1),
     ]
-    edge_src = lax.rem(lax.broadcasted_iota(jnp.int32, (2 * COLS, COLS), 0), COLS)
-    edge_dst = lax.broadcasted_iota(jnp.int32, (2 * COLS, COLS), 1)
-    outer = (edge_src < 2) | (edge_src >= COLS - 2)
-    moved = jnp.where(outer, (edge_dst - edge_src) & (COLS - 1), -1)
-
-    @pl.loop(0, NVG)
-    def _(vg):
-        for vi in range(VS):
-            to_edge[vg, vi * 2 * COLS : (vi + 1) * 2 * COLS, :] = jnp.where(
-                moved == 4 * (vg * VS + vi), 1.0, 0.0
-            ).astype(BF)
-
     for vg in range(NVG):
         fetch(vg).wait()
 
@@ -222,6 +213,18 @@
                 w.start()
         if vg < 2:
             send_rows(vg)
+
+    edge_src = lax.rem(lax.broadcasted_iota(jnp.int32, (2 * COLS, COLS), 0), COLS)
+    edge_dst = lax.broadcasted_iota(jnp.int32, (2 * COLS, COLS), 1)
+    outer = (edge_src < 2) | (edge_src >= COLS - 2)
+    moved = jnp.where(outer, (edge_dst - edge_src) & (COLS - 1), -1)
+
+    @pl.loop(0, NVG)
+    def _(vg):
+        for vi in range(VS):
+            to_edge[vg, vi * 2 * COLS : (vi + 1) * 2 * COLS, :] = jnp.where(
+                moved == 4 * (vg * VS + vi), 1.0, 0.0
+            ).astype(BF)
 
     edge[...] = jnp.zeros_like(edge)
 
@@ -249,7 +252,7 @@
     group = (row_all >= 3).astype(jnp.int32) + (row_all >= 6).astype(jnp.int32)
     part_of = row_all - 3 * group
     desc[...] = (var_ref[...] * SIDE + group) * COLS + (lon_all & (COLS - 1))
-    to_scalar = pltpu.make_async_copy(desc, desc_s, l_small.at[4])
+    to_scalar = pltpu.make_async_copy(desc, desc_s, l_small.at[6])
     to_scalar.start()
     at_all = jnp.where(owned, part_of, -1)
     for b in range(NB):
@@ -431,6 +434,8 @@
             first.append(c)
     lat_f, lon_f = by_block(lat_ref).astype(F32), by_block(lon_ref).astype(F32)
     lat0f, lon0f = (me_lat * ROWS).astype(F32), (me_lon * COLS).astype(F32)
+    for i, t in enumerate([lat_f, lon_f, by_block(val_ref), by_block(err_ref)]):
+        obs_ref[i] = t
     reach_tables(lat_f, lon_f, lat0f, lon0f, rank_ref, t0_ref)
     total = part[me_lon]
     for i in range(1, NB):
@@ -468,7 +473,7 @@
     sent_rows(4)
 
 
-def forecast(x, wind, lat, lon, var, nlat, nlon):
+def forecast(x, wind, lat, lon, var, val, err, nlat, nlon):
     vm = pl.BlockSpec(memory_space=pltpu.VMEM)
     dma = pltpu.SemaphoreType.DMA
     return pl.pallas_call(
@@ -479,15 +484,18 @@
             jax.ShapeDtypeStruct((NB, BLOCK), F32),
             jax.ShapeDtypeStruct((NB, KC, ROWS * COLS), F32),
             jax.ShapeDtypeStruct((NB * (NB - 1) // 2, BLOCK, BLOCK), F32),
+            jax.ShapeDtypeStruct((4, NB, BLOCK), F32),
         ),
-        in_specs=[pl.BlockSpec(memory_space=pltpu.HBM)] * 5,
-        out_specs=(vm,) * 5,
+        in_specs=[pl.BlockSpec(memory_space=pltpu.HBM)] * 7,
+        out_specs=(vm,) * 6,
         scratch_shapes=[
             pltpu.VMEM((MEMBERS, NVAR, ROWS, COLS), F32),
             pltpu.VMEM((2, ROWS, COLS), F32),
             pltpu.VMEM((GROUPS, OBS), jnp.int32),
             pltpu.VMEM((GROUPS, OBS), jnp.int32),
             pltpu.VMEM((GROUPS, OBS), jnp.int32),
+            pltpu.VMEM((GROUPS, OBS), F32),
+            pltpu.VMEM((GROUPS, OBS), F32),
             pltpu.VMEM((GROUPS, OBS), jnp.int32),
             pltpu.SMEM((GROUPS, OBS), jnp.int32),
             pltpu.VMEM((NVAR * SIDE * COLS, COLS), F32),
@@ -515,30 +523,22 @@
             dma((NVG, 2)), dma((NVG, 2)), dma((2,)), dma((2,)),
             dma((4,)), dma((4,)), dma((4,)), dma((4,)),
             dma((nlat + nlon - 2,)), dma((NB, 2)), dma((NB, 2)), dma((nlat - 1,)), dma((nlon - 1,)),
-            dma((NVG,)), dma((5,)),
+            dma((NVG,)), dma((7,)),
         ],
         compiler_params=pltpu.CompilerParams(
             collective_id=0, has_side_effects=True, vmem_limit_bytes=34 << 20
         ),
         name="forecast",
-    )(x, wind, lat, lon, var)
+    )(x, wind, lat, lon, var, val, err)
 
 
 def analysis_kernel(
-    x_ref, y_ref, rank_ref, t0_ref, pair_ref, lat_hbm, lon_hbm, val_hbm, err_hbm,
+    x_ref, y_ref, rank_ref, t0_ref, pair_ref, obs_ref,
     out_hbm,
-    lat_ref, lon_ref, val_ref, err_ref, ob,
+    ob,
     ys, a_all, s_all, a_pk, b_pk, l_pk, a_more, b_more, t_more, xv, rhs, p2, q3, nch,
-    l_small, l_out,
+    l_out,
 ):
-    small = [
-        pltpu.make_async_copy(a, b, l_small.at[i])
-        for i, (a, b) in enumerate(
-            [(lat_hbm, lat_ref), (lon_hbm, lon_ref), (val_hbm, val_ref), (err_hbm, err_ref)]
-        )
-    ]
-    for c in small:
-        c.start()
     out_rows = ob.reshape(MEMBERS * NVAR * ROWS, COLS)
 
     def store(g):
@@ -551,10 +551,7 @@
         nch[b] = ((top + KC) * (1.0 / KC)).astype(jnp.int32)
         ys[0:PIECE, b * BLOCK : (b + 1) * BLOCK] = y_ref[2 * b]
         ys[PIECE:, b * BLOCK : (b + 1) * BLOCK] = y_ref[2 * b + 1][0 : MEMBERS - PIECE]
-    for c in small:
-        c.wait()
-    lat, lon = by_block(lat_ref).astype(F32), by_block(lon_ref).astype(F32)
-    values, variances = by_block(val_ref), by_block(err_ref)
+    lat, lon, values, variances = [obs_ref[i] for i in range(4)]
     row_id = lax.broadcasted_iota(jnp.int32, (KC, BLOCK), 0).astype(F32)
     lane96 = lax.broadcasted_iota(jnp.int32, (KC, 3 * KC), 1)
     zero8 = jnp.zeros((8, BLOCK), F32)
@@ -688,7 +685,7 @@
         store(g).wait()
 
 
-def analysis(x, y, rank, t0, pairs, lat, lon, val, err):
+def analysis(x, y, rank, t0, pairs, obs):
     vm = pl.BlockSpec(memory_space=pltpu.VMEM)
     hbm = pl.BlockSpec(memory_space=pltpu.HBM)
     more = NB * (NCH - 1)
@@ -696,13 +693,9 @@
     return pl.pallas_call(
         analysis_kernel,
         out_shape=jax.ShapeDtypeStruct((MEMBERS, NVAR, ROWS, COLS), F32),
-        in_specs=[vm] * 5 + [hbm] * 4,
+        in_specs=[vm] * 6,
         out_specs=hbm,
         scratch_shapes=[
-            pltpu.VMEM((GROUPS, OBS), jnp.int32),
-            pltpu.VMEM((GROUPS, OBS), jnp.int32),
-            pltpu.VMEM((GROUPS, OBS), F32),
-            pltpu.VMEM((GROUPS, OBS), F32),
             pltpu.VMEM((MEMBERS, NVAR, ROWS, COLS), F32),
             pltpu.VMEM((MEMBERS, NB * BLOCK), F32),
             pltpu.VMEM((NB, BLOCK, 128), BF),
@@ -718,11 +711,11 @@
             pltpu.VMEM((VG, KC, ROWS * COLS), F32),
             pltpu.VMEM((VG, 3 * KC, ROWS * COLS), BF),
             pltpu.SMEM((NB,), jnp.int32),
-            dma((4,)), dma((NVAR // VG,)),
+            dma((NVAR // VG,)),
         ],
         compiler_params=pltpu.CompilerParams(vmem_limit_bytes=22 << 20),
         name="analysis",
-    )(x, y, rank, t0, pairs, lat, lon, val, err)
+    )(x, y, rank, t0, pairs, obs)
 
 
 def solution(mesh):
@@ -734,8 +727,7 @@
             pltpu.with_memory_space_constraint(a, pltpu.HBM)
             for a in (prognostic_samples, wind, obs_lat, obs_lon, obs_var, obs_value, obs_error)
         ]
-        xf, y, rank, t0, pairs = forecast(*hbm[:5], nlat, nlon)
-        return analysis(xf, y, rank, t0, pairs, hbm[2], hbm[3], hbm[5], hbm[6])
+        return analysis(*forecast(*hbm, nlat, nlon))
 
     in_specs = (P(None, None, "lat", "lon"), P(None, "lat", "lon"), P(), P(), P(), P(), P())
     out_specs = P(None, None, "lat", "lon")

time: 69.2 us -> 68.7 us (level)
    pallas_call x1, Pallas kernels: 22.8 us -> 22.1 us  [analysis(): pl.pallas_call(analysis_kernel, out_shape=jax.ShapeDtypeStruct((MEMBERS,...]
where the time goes in v8:
time: 68.7 us; the launch traced here: 68.5 us
  Pallas kernels  68.5 us (100%)
    pallas_call x1, Pallas kernels, forecast(): pl.pallas_call(lambda *refs: forecast_kernel(nlat, nlon, *refs), out_shap...  46.4 us
    pallas_call x1, Pallas kernels, analysis(): pl.pallas_call(analysis_kernel, out_shape=jax.ShapeDtypeStruct((MEMBERS,...  22.1 us

profile of v8, /device:TPU:1, one launch (start us, length us, event | category | flops | bytes accessed | tf_op | source)
XLA Modules:
  0.0 68.5 jit_solution(6688230315357407438)
XLA Ops:
  0.0 46.4 %forecast.1 = (f32[25,8,40,128]{3,2,1,0:T(8,128)S(1)}, f32[16,24,128]{2,1,0:T(8,128)S(1)}, f32[8,128]{1,0:T(8,128)S(1)}, f32[8,32,1024]{2,1,0:T(8,128)S(1)}, f32...) custom-call(f32[40,25,8,128]{3,2,1,0:T(8,128)} %refs_0_.1, f32[2,8,128]{2,1,0:T(8,128)} %refs_1_.1, s32[2,512]{1,0:T(2,128)} %refs_2_.1, ...), custom_call_target="tpu_custom_call" | custom-call | tf_op jit(solution)/shard_map/forecast/pallas_call | solution.py:479
  46.4 22.1 %analysis.1 = f32[40,25,8,128]{3,2,1,0:T(8,128)} custom-call(f32[25,8,40,128]{3,2,1,0:T(8,128)S(1)} %get-tuple-element.11.x_ref, f32[16,24,128]{2,1,0:T(8,128)S(1)} %get-tuple-element.12.y_ref, f32[8,128]{1,0:T(8,128)S(1)} %get-tuple-element.13.rank_ref, f32[8,32,1024]{2,1,0:T(8,128)S(1)} %get-tuple-element.14.t0_ref, ...), custom_call_target="tpu_custom_call" | custom-call | tf_op jit(solution)/shard_map/analysis/pallas_call | solution.py:693

commit v9 on v8

--- a/solution.py
+++ b/solution.py
@@ -372,13 +372,13 @@
             ).reshape(n1, MEMBERS, COLS)
         for vi in range(VS):
             v = vg * VS + vi
-            new = step(
+            xf[v] = step(
                 block(q1_s, vi, 1, n2), block(q1_s, vi, 2, n2), block(q1_s, vi, 0, n2),
                 halo1_s[...], (COLS - 1 - 4 * v) & (COLS - 1), 1, n2,
-            )
-            xf[v] = new.reshape(n2, MEMBERS, COLS)
-            high, low = split(new)
-            both = jnp.concatenate([high, low], axis=1)
+            ).reshape(n2, MEMBERS, COLS)
+        for vi in range(VS):
+            v = vg * VS + vi
+            both = jnp.concatenate(split(block(xf, v, 0, n2)), axis=1)
             for i in range(SIDE):
                 n = min(3, ROWS - 3 * i) * MEMBERS
                 xft[pl.ds((v * SIDE + i) * COLS, COLS), 0:n] = dot(

time: 68.7 us -> 68 us (0.990)
  Pallas kernels: 68.5 us -> 67.8 us
    pallas_call x1, Pallas kernels: 46.4 us -> 45.7 us  [forecast(): pl.pallas_call(lambda *refs: forecast_kernel(nlat, nlon, *refs), out_shap...]
where the time goes in v9:
time: 68 us; the launch traced here: 67.8 us
  Pallas kernels  67.8 us (100%)
    pallas_call x1, Pallas kernels, forecast(): pl.pallas_call(lambda *refs: forecast_kernel(nlat, nlon, *refs), out_shap...  45.7 us
    pallas_call x1, Pallas kernels, analysis(): pl.pallas_call(analysis_kernel, out_shape=jax.ShapeDtypeStruct((MEMBERS,...  22.1 us

profile of v9, /device:TPU:1, one launch (start us, length us, event | category | flops | bytes accessed | tf_op | source)
XLA Modules:
  0.0 67.8 jit_solution(6694839963116742753)
XLA Ops:
  0.0 45.7 %forecast.1 = (f32[25,8,40,128]{3,2,1,0:T(8,128)S(1)}, f32[16,24,128]{2,1,0:T(8,128)S(1)}, f32[8,128]{1,0:T(8,128)S(1)}, f32[8,32,1024]{2,1,0:T(8,128)S(1)}, f32...) custom-call(f32[40,25,8,128]{3,2,1,0:T(8,128)} %refs_0_.1, f32[2,8,128]{2,1,0:T(8,128)} %refs_1_.1, s32[2,512]{1,0:T(2,128)} %refs_2_.1, ...), custom_call_target="tpu_custom_call" | custom-call | tf_op jit(solution)/shard_map/forecast/pallas_call | solution.py:479
  45.8 22.1 %analysis.1 = f32[40,25,8,128]{3,2,1,0:T(8,128)} custom-call(f32[25,8,40,128]{3,2,1,0:T(8,128)S(1)} %get-tuple-element.11.x_ref, f32[16,24,128]{2,1,0:T(8,128)S(1)} %get-tuple-element.12.y_ref, f32[8,128]{1,0:T(8,128)S(1)} %get-tuple-element.13.rank_ref, f32[8,32,1024]{2,1,0:T(8,128)S(1)} %get-tuple-element.14.t0_ref, ...), custom_call_target="tpu_custom_call" | custom-call | tf_op jit(solution)/shard_map/analysis/pallas_call | solution.py:693

commit v10 on v9

--- a/solution.py
+++ b/solution.py
@@ -131,7 +131,7 @@
     x_hbm, wind_hbm, lat_hbm, lon_hbm, var_hbm, val_hbm, err_hbm,
     xf, out, rank_ref, t0_ref, pair_ref, obs_ref,
     xb, wind_ref, lat_ref, lon_ref, var_ref, val_ref, err_ref, desc, desc_s, xft, yo, part, line, block_sum, got_a, got_b,
-    xt, edge, edge_w, edge_e, corner, wind_n, halo, halo_s, halo1_s, coef, shift, unit, q1_s, to_edge, at8,
+    xt, edge, edge_w, edge_e, corner, wind_n, halo, halo_s, halo1_s, coef, shift, unit, q1_s, both_s, to_edge, at8,
     s_row, r_row, s_edge, r_edge, s_corner, r_corner, s_wind, r_wind,
     send, send_a, recv_a, recv_b, recv_c, l_x, l_small,
 ):
@@ -332,10 +332,12 @@
         )
         halo1_s[r] = beside(after)
 
-    def step(q, nxt, prv, side, back, first, count):
+    def shifted(vi, q, count):
+        both_s[vi, 0 : count * MEMBERS] = dot(jnp.concatenate(split(q), axis=1), shift[...])
+
+    def step(vi, q, nxt, prv, side, back, first, count):
         shape = (count, MG, 8, COLS)
-        high, low = split(q)
-        both = dot(jnp.concatenate([high, low], axis=1), shift[...])
+        both = both_s[vi, 0 : count * MEMBERS]
         lane = lax.broadcasted_iota(jnp.int32, (count * MEMBERS, COLS), 1)
         beyond = pltpu.roll(side.reshape(count * MEMBERS, COLS), back, 1)
         east = jnp.where(lane == COLS - 1, beyond, both[:, :COLS])
@@ -365,15 +367,19 @@
 
         n1, n2 = ROWS + 2, ROWS
         for vi in range(VS):
+            shifted(vi, block(xt, vg * VS + vi, 1, n1), n1)
+        for vi in range(VS):
             v = vg * VS + vi
             q1_s[vi] = step(
-                block(xt, v, 1, n1), block(xt, v, 2, n1), block(xt, v, 0, n1),
+                vi, block(xt, v, 1, n1), block(xt, v, 2, n1), block(xt, v, 0, n1),
                 halo_s[...], (COLS - 1 - 4 * v) & (COLS - 1), 0, n1,
             ).reshape(n1, MEMBERS, COLS)
         for vi in range(VS):
+            shifted(vi, block(q1_s, vi, 1, n2), n2)
+        for vi in range(VS):
             v = vg * VS + vi
             xf[v] = step(
-                block(q1_s, vi, 1, n2), block(q1_s, vi, 2, n2), block(q1_s, vi, 0, n2),
+                vi, block(q1_s, vi, 1, n2), block(q1_s, vi, 2, n2), block(q1_s, vi, 0, n2),
                 halo1_s[...], (COLS - 1 - 4 * v) & (COLS - 1), 1, n2,
             ).reshape(n2, MEMBERS, COLS)
         for vi in range(VS):
@@ -518,6 +524,7 @@
             pltpu.VMEM((2 * COLS, 2 * COLS), BF),
             pltpu.VMEM((COLS, 2 * COLS), BF),
             pltpu.VMEM((VS, ROWS + 2, MEMBERS, COLS), F32),
+            pltpu.VMEM((VS, (ROWS + 2) * MEMBERS, 2 * COLS), F32),
             pltpu.VMEM((NVG, VS * 2 * COLS, COLS), BF),
             pltpu.VMEM((NB, BLOCK), jnp.int32),
             dma((NVG, 2)), dma((NVG, 2)), dma((2,)), dma((2,)),

time: 68 us -> 67.9 us (level)
  no operation moved by 1% of the time
where the time goes in v10:
time: 67.9 us; the launch traced here: 67.7 us
  Pallas kernels  67.7 us (100%)
    pallas_call x1, Pallas kernels, forecast(): pl.pallas_call(lambda *refs: forecast_kernel(nlat, nlon, *refs), out_shap...  45.6 us
    pallas_call x1, Pallas kernels, analysis(): pl.pallas_call(analysis_kernel, out_shape=jax.ShapeDtypeStruct((MEMBERS,...  22.1 us

profile of v10, /device:TPU:1, one launch (start us, length us, event | category | flops | bytes accessed | tf_op | source)
XLA Modules:
  0.0 67.7 jit_solution(8359514781304680924)
XLA Ops:
  0.0 45.6 %forecast.1 = (f32[25,8,40,128]{3,2,1,0:T(8,128)S(1)}, f32[16,24,128]{2,1,0:T(8,128)S(1)}, f32[8,128]{1,0:T(8,128)S(1)}, f32[8,32,1024]{2,1,0:T(8,128)S(1)}, f32...) custom-call(f32[40,25,8,128]{3,2,1,0:T(8,128)} %refs_0_.1, f32[2,8,128]{2,1,0:T(8,128)} %refs_1_.1, s32[2,512]{1,0:T(2,128)} %refs_2_.1, ...), custom_call_target="tpu_custom_call" | custom-call | tf_op jit(solution)/shard_map/forecast/pallas_call | solution.py:485
  45.7 22.1 %analysis.1 = f32[40,25,8,128]{3,2,1,0:T(8,128)} custom-call(f32[25,8,40,128]{3,2,1,0:T(8,128)S(1)} %get-tuple-element.11.x_ref, f32[16,24,128]{2,1,0:T(8,128)S(1)} %get-tuple-element.12.y_ref, f32[8,128]{1,0:T(8,128)S(1)} %get-tuple-element.13.rank_ref, f32[8,32,1024]{2,1,0:T(8,128)S(1)} %get-tuple-element.14.t0_ref, ...), custom_call_target="tpu_custom_call" | custom-call | tf_op jit(solution)/shard_map/analysis/pallas_call | solution.py:700
